TPU v7x, 128 devices: a whole 4x4x4 slice. The times are simulated.
128 devices in a mesh: dp: 8 (over z, core), tensor: 16 (over y, x).
Axes of the slice: x: 4, y: 4, z: 4, core: 2. Of those that a mesh axis runs over, the one named last changes fastest.
Arguments:
- residues: bfloat16 [4096, 1024], P('dp'), may hold values from -40 to 40
- block_protein: int32 [32], P('dp'), may hold values from 0 to 31, as said below
- protein_length: int32 [32], replicated, may hold values from 0 to 256, as said below
- decoder_group: int32 [32], replicated, may hold values from 0 to 7, as said below
- enc_gain: float32 [1024], replicated, may hold values from 0.1 to 1.9
- enc_query: bfloat16 [1024, 16384], P(None, 'tensor'), may hold values from -2 to 2
- enc_key: bfloat16 [1024, 16384], P(None, 'tensor'), may hold values from -2 to 2
- enc_value: bfloat16 [1024, 16384], P(None, 'tensor'), may hold values from -0.1875 to 0.1875
- enc_out: bfloat16 [16384, 1024], P('tensor'), may hold values from -0.1875 to 0.1875
- decoder_states: bfloat16 [3072, 1024], P('dp'), may hold values from -40 to 40
- query_protein: int32 [3072], P('dp'), may hold values from 0 to 31, as said below
- dec_gain: float32 [1024], replicated, may hold values from 0.1 to 1.9
- final_gain: float32 [1024], replicated, may hold values from 0.1 to 1.9
- cross_query: bfloat16 [1024, 16384], P(None, 'tensor'), may hold values from -2 to 2
- cross_key: bfloat16 [1024, 16384], P(None, 'tensor'), may hold values from -2 to 2
- cross_value: bfloat16 [1024, 16384], P(None, 'tensor'), may hold values from -0.1875 to 0.1875
- cross_out: bfloat16 [16384, 1024], P('tensor'), may hold values from -0.1875 to 0.1875
Outputs:
- encoded: bfloat16 [4096, 1024], P('dp', 'tensor')
- decoded: bfloat16 [3072, 1024], P(('dp', 'tensor'))
Inputs may be any that keep to these rules, and one draw needn't show every extreme that they name: `block_protein`: block b of dp group d names a protein id from d * 4 to (d + 1) * 4 - 1; the blocks of one protein are consecutive and the ids rise along a group's blocks. `protein_length`: A protein of n blocks has a length from (n - 1) * 128 + 1 to n * 128; an id that no block names has length 0; no protein spans more than 2 blocks. `decoder_group`: at most 2 blocks of one dp group belong to proteins of one decoder group, and in every draw some decoder group gets exactly 2 blocks from every dp group; every decoder group owns a protein of positive length. `query_protein`: query row i names a protein of positive length whose decoder group is i // 384.
All inputs are finite; a program needn't handle non-finite values.
Results may differ from a plain program's by a relative error of at most 0.017.
Values may be sent and summed in bfloat16 or wider, within the bound.
No kernel may reach another device: no remote copies, remote signals or barrier semaphores. Data moves between devices by JAX's collectives and lax.ppermute only.
A program may use at most 128 MiB of HBM per device.

v0:
```python
import jax
import jax.numpy as jnp
from jax import lax
from jax.sharding import PartitionSpec as P

HEAD_DIM = 128
BLOCK = 128


EPSILON = 1e-06
MASKED = -1000000000.0


def split_up(x, dim, size):
    before, after = (x.shape[:dim], x.shape[dim + 1 :])
    return jnp.moveaxis(x.reshape(*before, size, -1, *after), dim, 0)


def sent_and_summed(x, axis, dim):
    blocks = split_up(x, dim, lax.axis_size(axis))
    arrived = lax.all_to_all(blocks, axis, split_axis=0, concat_axis=0, tiled=True)
    return arrived.sum(axis=0)


def summed_on_arrival(x, axis, dim):
    blocks = split_up(x, dim, lax.axis_size(axis))
    arrived = lax.all_to_all(blocks, axis, split_axis=0, concat_axis=0, tiled=True)
    return arrived.astype(jnp.float32).sum(axis=0)


def row_scale(matrix):
    values = matrix.astype(jnp.float32)
    return lax.rsqrt(jnp.mean(values * values, axis=1, keepdims=True) + EPSILON)


def table_lookup(indices, table):
    match = indices[:, None] == jnp.arange(table.shape[0], dtype=jnp.int32)[None, :]
    return jnp.sum(jnp.where(match, table[None, :], 0), axis=1)


def attend(queries, keys, values, allowed):
    count = queries.shape[0]
    heads = queries.shape[1] // HEAD_DIM
    query_heads = queries.reshape(count, heads, HEAD_DIM)
    key_heads = keys.reshape(keys.shape[0], heads, HEAD_DIM)
    value_heads = values.reshape(values.shape[0], heads, HEAD_DIM)
    scores = jnp.einsum(
        "qhd,khd->hqk", query_heads, key_heads, preferred_element_type=jnp.float32
    ) * HEAD_DIM ** (-0.5)
    scores = jnp.where(allowed[None], scores, MASKED)
    top = jnp.max(scores, axis=2, keepdims=True)
    expo = jnp.exp(scores - top)
    total = jnp.sum(expo, axis=2)
    weights = expo.astype(jnp.bfloat16)
    context = jnp.einsum("hqk,khd->qhd", weights, value_heads, preferred_element_type=jnp.float32)
    context = context / jnp.transpose(total)[:, :, None]
    return context.reshape(count, heads * HEAD_DIM).astype(jnp.bfloat16)


def body(
    residues,
    block_protein,
    protein_length,
    decoder_group,
    enc_gain,
    enc_query,
    enc_key,
    enc_value,
    enc_out,
    decoder_states,
    query_protein,
    dec_gain,
    final_gain,
    cross_query,
    cross_key,
    cross_value,
    cross_out,
):
    groups = lax.axis_size("dp")
    tensor_count = lax.axis_size("tensor")
    tensor_index = lax.axis_index("tensor")
    tok_rows = residues.shape[0]
    width = residues.shape[1]
    blocks = block_protein.shape[0]
    slots = blocks // 2
    order = jnp.arange(blocks, dtype=jnp.int32)
    same = block_protein[:, None] == block_protein[None, :]
    offset = jnp.sum(same & (order[None, :] < order[:, None]), axis=1)
    live = jnp.clip(table_lookup(block_protein, protein_length) - offset * BLOCK, 0, BLOCK)
    dest = table_lookup(block_protein, decoder_group)
    position = jnp.arange(BLOCK, dtype=jnp.int32)
    token_protein = jnp.broadcast_to(block_protein[:, None], (blocks, BLOCK)).reshape(tok_rows)
    token_valid = (position[None, :] < live[:, None]).reshape(tok_rows)
    normed = (residues.astype(jnp.float32) * row_scale(residues) * enc_gain[None, :]).astype(
        jnp.bfloat16
    )
    enc_queries = jnp.dot(normed, enc_query, preferred_element_type=jnp.float32).astype(
        jnp.bfloat16
    )
    enc_keys = jnp.dot(normed, enc_key, preferred_element_type=jnp.float32).astype(jnp.bfloat16)
    enc_values = jnp.dot(normed, enc_value, preferred_element_type=jnp.float32).astype(jnp.bfloat16)
    row_block = min(tok_rows, 512)
    block_count = tok_rows // row_block

    def encode_block(item):
        block_queries, block_owner = item
        permit = (block_owner[:, None] == token_protein[None, :]) & token_valid[None, :]
        return attend(block_queries, enc_keys, enc_values, permit)

    context = lax.map(
        encode_block,
        (
            enc_queries.reshape(block_count, row_block, -1),
            token_protein.reshape(block_count, row_block),
        ),
    )
    context = context.reshape(tok_rows, -1)
    partial_value = jnp.dot(context, enc_out, preferred_element_type=jnp.float32)
    slice_width = width // tensor_count
    column_start = tensor_index * slice_width
    same_dest = dest[:, None] == dest[None, :]
    rank = jnp.sum(same_dest & (order[None, :] < order[:, None]), axis=1)
    place = dest * slots + rank
    target = jnp.arange(groups * slots, dtype=jnp.int32)
    chosen = target[:, None] == place[None, :]
    occupied = jnp.any(chosen, axis=1)
    send_ids = jnp.where(
        occupied, jnp.sum(jnp.where(chosen, block_protein[None, :], 0), axis=1), -1
    )
    send_live = jnp.sum(jnp.where(chosen, live[None, :], 0), axis=1)
    send_meta = jnp.stack([send_ids, send_live], axis=-1).reshape(groups, slots, 2)
    shares = sent_and_summed(partial_value, "tensor", 1)
    own_columns = lax.dynamic_slice_in_dim(residues, column_start, slice_width, 1)
    encoded = (own_columns.astype(jnp.float32) + shares).astype(jnp.bfloat16)
    features = encoded.shape[1]
    stacked = encoded.reshape(blocks, BLOCK * features)
    placed = jnp.dot(
        chosen.astype(jnp.bfloat16), stacked, preferred_element_type=jnp.float32
    ).astype(jnp.bfloat16)
    slice_grid = lax.all_to_all(
        placed.reshape(groups, slots, BLOCK, features),
        "dp",
        split_axis=0,
        concat_axis=0,
        tiled=True,
    )
    meta = lax.all_to_all(send_meta, "dp", split_axis=0, concat_axis=0, tiled=True)
    flat = slice_grid.reshape(-1, slice_width)
    inner = cross_key.shape[1]
    values32 = lax.all_gather(flat, "tensor", axis=1, tiled=True).astype(jnp.float32)
    scaled = (values32 * final_gain[None, :]).astype(jnp.bfloat16)
    key_sum = jnp.dot(scaled, cross_key, preferred_element_type=jnp.float32)
    value_sum = jnp.dot(scaled, cross_value, preferred_element_type=jnp.float32)
    squares = jnp.sum(values32 * values32, axis=1, keepdims=True)
    key_sum, value_sum, squares = (key_sum, value_sum, squares)
    key_scale = lax.rsqrt(squares / width + EPSILON)
    grid_shape = (groups, slots, BLOCK, inner)
    key_grid = (key_sum * key_scale).astype(jnp.bfloat16).reshape(grid_shape)
    value_grid = (value_sum * key_scale).astype(jnp.bfloat16).reshape(grid_shape)
    key_ids = meta[:, :, 0]
    key_live = meta[:, :, 1]
    key_valid = position[None, None, :] < key_live[:, :, None]
    query_rows = decoder_states.shape[0]
    dec_normed = (
        decoder_states.astype(jnp.float32) * row_scale(decoder_states) * dec_gain[None, :]
    ).astype(jnp.bfloat16)
    cross_queries = jnp.dot(dec_normed, cross_query, preferred_element_type=jnp.float32).astype(
        jnp.bfloat16
    )
    allowed = (query_protein[:, None, None, None] == key_ids[None, :, :, None]) & key_valid[None]
    slot_total = groups * slots
    inner_width = key_grid.shape[3]
    cross_context = attend(
        cross_queries,
        key_grid.reshape(slot_total * BLOCK, inner_width),
        value_grid.reshape(slot_total * BLOCK, inner_width),
        allowed.reshape(query_rows, slot_total * BLOCK),
    )
    share_rows = query_rows // tensor_count
    mixed = summed_on_arrival(
        jnp.dot(cross_context, cross_out, preferred_element_type=jnp.float32).astype(jnp.bfloat16),
        "tensor",
        0,
    )
    own_rows = lax.dynamic_slice_in_dim(decoder_states, tensor_index * share_rows, share_rows, 0)
    decoded = (own_rows.astype(jnp.float32) + mixed).astype(jnp.bfloat16)
    return (encoded, decoded)


def solution(mesh):
    in_specs = (
        P("dp", None),
        P("dp"),
        P(),
        P(),
        P(),
        P(None, "tensor"),
        P(None, "tensor"),
        P(None, "tensor"),
        P("tensor", None),
        P("dp", None),
        P("dp"),
        P(),
        P(),
        P(None, "tensor"),
        P(None, "tensor"),
        P(None, "tensor"),
        P("tensor", None),
    )
    out_specs = (P("dp", "tensor"), P(("dp", "tensor"), None))
    return jax.shard_map(body, mesh=mesh, in_specs=in_specs, out_specs=out_specs, check_vma=False)
```

profile of v0, /device:TPU:0, one launch (start us, length us, event | category | flops | bytes accessed | tf_op | source)
XLA Modules:
  0.0 220.1 jit_solution(1068523723538875895)
XLA Ops:
  7.2 1.0 convert_reduce_fusion.2
  8.2 0.7 broadcast_bitcast_fusion
  8.9 0.9 select_reduce_fusion.2
  9.8 0.2 convert_reduce_fusion.1
  10.1 1.5 fusion.17
  11.6 4.4 %fusion.31 = bf16[64,8,8,128]{3,2,1,0:T(8,128)(2,1)} fusion(bf16[1024,1024]{1,0:T(8,128)(2,1)} %param.22, bf16[512,1024]{1,0:T(8,128)(2,1)} %param.17, f32[1024]{0:T(1024)} %param.21, f32[512]{0:T(512)S(1)} %add_rsqrt_fusion.2), kind=kOutput, calls=%fused_computation.46 | convolution fusion | flops 1076363264 | bytes 4200448 | tf_op jit(solution)/shard_map/dot_general | solution.py:97
  16.0 2.3 %fusion.32 = bf16[64,8,8,128]{3,2,1,0:T(8,128)(2,1)} fusion(bf16[1024,1024]{1,0:T(8,128)(2,1)S(1)} %copy-done.11, bf16[512,1024]{1,0:T(8,128)(2,1)S(1)} %copy-done.6, f32[1024]{0:T(1024)S(1)} %copy-done.14, f32[512]{0:T(512)S(1)} %add_rsqrt_fusion.2), kind=kOutput, calls=%fused_computation.47 | convolution fusion | flops 1076363264 | bytes 4200448 | tf_op jit(solution)/shard_map/dot_general | solution.py:100
  18.3 2.3 %convolution_convert_fusion.3 = bf16[512,1024]{1,0:T(8,128)(2,1)} fusion(bf16[1024,1024]{1,0:T(8,128)(2,1)S(1)} %copy-done.12, bf16[512,1024]{1,0:T(8,128)(2,1)S(1)} %copy-done.6, f32[1024]{0:T(1024)S(1)} %copy-done.14, f32[512]{0:T(512)S(1)} %add_rsqrt_fusion.2), kind=kOutput, calls=%fused_computation.43 | convolution fusion | flops 1076363264 | bytes 4200448 | tf_op jit(solution)/shard_map/dot_general | solution.py:101
  20.6 2.3 %copy.107 = bf16[512,1024]{0,1:T(8,128)(2,1)} copy(bf16[512,1024]{1,0:T(8,128)(2,1)} %convolution_convert_fusion.3) | data formatting | bytes 2097152 | tf_op jit(solution)/shard_map/while/body/eval_jaxpr/reshape | solution.py:46
  22.9 4.0 %copy.91 = bf16[1024,1024]{0,1:T(8,128)(2,1)} copy(bf16[1024,1024]{1,0:T(8,128)(2,1)} %param.25) | data formatting | bytes 4194304 | tf_op args[8]
  26.9 0.2 compare_and_fusion
  27.1 3.2 %fusion.8 = (f32[8,512]{1,0:T(8,128)S(1)}, f32[8,512,512]{1,2,0:T(8,128)S(1)}) fusion(pred[512,512]{0,1:T(8,128)(4,1)S(1)} %compare_and_fusion, bf16[64,8,8,128]{3,2,1,0:T(8,128)(2,1)} %fusion.32, bf16[64,8,8,128]{3,2,1,0:T(8,128)(2,1)} %fusion.31), kind=kOutput, calls=%fused_computation.16 | convolution fusion | flops 543158272 | bytes 10764288 | tf_op jit(solution)/shard_map/while/body/eval_jaxpr/qhd,khd->hqk/dot_general | solution.py:47
  30.3 1.7 fusion.9
  32.1 2.6 %fusion.20 = bf16[512,8,128]{0,2,1:T(8,128)(2,1)S(1)} fusion(bf16[512,8,128]{0,2,1:T(8,128)(2,1)S(1)} %bitcast.70, f32[8,512,512]{1,2,0:T(8,128)S(1)} %get-tuple-element.33, f32[8,512]{1,0:T(8,128)S(1)} %get-tuple-element.32, pred[512,512]{0,1:T(8,128)(4,1)S(1)} %compare_and_fusion, f32[512,8]{0,1:T(8,128)S(1)} %bitcast.72), kind=kOutput, calls=%fused_computation.31 | convolution fusion | flops 546308096 | bytes 10780672 | tf_op jit(solution)/shard_map/while/body/eval_jaxpr/hqk,khd->qhd/dot_general | solution.py:55
  34.7 2.5 %convolution_bitcast_fusion = f32[16,512,64]{1,2,0:T(8,128)} fusion(bf16[512,1024,1]{0,1,2:T(8,128)(2,1)S(1)} %bitcast.77, bf16[16,64,1024]{2,1,0:T(8,128)(2,1)S(1)} %bitcast.69), kind=kOutput, calls=%fused_computation.34 | convolution fusion | flops 1073741824 | bytes 5242880 | tf_op jit(solution)/shard_map/dot_general | solution.py:118
  37.2 7.2 %all-to-all-start = ((f32[16,512,64]{1,2,0:T(8,128)}), f32[16,512,64]{1,2,0:T(8,128)}, u32[]{:S(2)}, u32[]{:S(2)}) async-start(f32[16,512,64]{1,2,0:T(8,128)} %convolution_bitcast_fusion), calls=%async_computation | async-start | bytes 4194304 | tf_op jit(solution)/shard_map/all_to_all | solution.py:21
  44.5 0.1 constant_dynamic-slice_fusion
  44.6 0.1 copy.111
  44.7 31.5 %all-to-all-done = f32[16,512,64]{1,2,0:T(8,128)} async-done(((f32[16,512,64]{1,2,0:T(8,128)}), f32[16,512,64]{1,2,0:T(8,128)}, u32[]{:S(2)}, u32[]{:S(2)}) %all-to-all-start) | async-done | bytes 2097184 | tf_op jit(solution)/shard_map/all_to_all | solution.py:21
  76.2 1.8 reduce_sum.122
  78.0 0.1 copy.93
  78.2 0.1 reshape.224
  78.3 0.4 convolution_convert_fusion
  78.7 0.5 reshape.225
  79.2 0.2 copy.94
  79.4 12.7 %all_to_all.20 = bf16[8,2,128,64]{2,3,1,0:T(8,128)(2,1)S(1)} all-to-all(bf16[8,2,128,64]{2,3,1,0:T(8,128)(2,1)S(1)} %copy.94), channel_id=1, replica_groups=mesh['dp'=8,'tensor'=16] {'dp'}, dimensions={0} | all-to-all | bytes 524288 | tf_op jit(solution)/shard_map/all_to_all | solution.py:140
  92.1 0.3 copy.95
  92.4 0.9 reshape.226
  93.3 0.1 fusion.45
  93.7 0.6 copy.96
  94.3 3.5 %all-to-all-start.2 = ((s32[8,2,2]{1,2,0:T(2,128)}), s32[8,2,2]{1,2,0:T(2,128)S(1)}, u32[]{:S(2)}, u32[]{:S(2)}) async-start(s32[8,2,2]{1,2,0:T(2,128)} %copy.96), calls=%async_computation.2 | async-start | bytes 16384 | tf_op jit(solution)/shard_map/all_to_all | solution.py:147
  97.8 1.4 fusion.25
  99.2 3.9 %fusion.33 = bf16[48,8,8,128]{3,2,1,0:T(8,128)(2,1)} fusion(bf16[1024,1024]{1,0:T(8,128)(2,1)} %param.30, bf16[384,1024]{1,0:T(8,128)(2,1)} %param.26, f32[1024]{0:T(1024)S(1)} %copy-done.15, f32[384]{0:T(512)S(1)} %add_rsqrt_fusion.1), kind=kOutput, calls=%fused_computation.48 | convolution fusion | flops 807272448 | bytes 3675648 | tf_op jit(solution)/shard_map/dot_general | solution.py:167
  103.3 1.3 bitcast_and_fusion
  104.6 2.2 copy.101
  106.8 33.9 %all-gather.2.cloned.1.call-done = bf16[2048,1024]{0,1:T(8,128)(2,1)} async-done(((bf16[2048,64]{0,1:T(8,128)(2,1)}), bf16[2048,1024]{0,1:T(8,128)(2,1)}) %all-gather.2.cloned.1.call-update) | async-done | bytes 4194320 | tf_op jit(solution)/shard_map/all_gather | solution.py:150
  140.7 3.2 %fusion.7 = f32[2048]{0:T(1024)S(1)} fusion(bf16[2048,1024]{0,1:T(8,128)(2,1)} %all-gather.2.cloned.1.call-done), kind=kLoop, calls=%fused_computation.11 | loop fusion | flops 6289408 | bytes 4202496 | tf_op jit(solution)/shard_map/reduce_sum | solution.py:154
  143.9 0.2 copy-done.2
  144.1 5.6 %multiply_convert_fusion = bf16[2048,1024]{0,1:T(8,128)(2,1)S(1)} fusion(bf16[1024,1024]{1,0:T(8,128)(2,1)S(1)} %copy-done, f32[2048]{0:T(1024)S(1)} %add_rsqrt_fusion, bf16[2048,1024]{0,1:T(8,128)(2,1)S(1)} %copy-done.2, f32[1024]{0:T(1024)S(1)} %copy-done.16), kind=kOutput, calls=%fused_computation.12 | convolution fusion | flops 4305453056 | bytes 10498048 | tf_op jit(solution)/shard_map/dot_general | solution.py:152
  149.8 10.9 %fusion = (f32[8,384]{1,0:T(8,128)S(1)}, f32[8,384,2048]{2,1,0:T(8,128)}) fusion(pred[384,2048]{1,0:T(8,128)(4,1)S(1)} %copy.101, bf16[2048,8,128]{0,2,1:T(8,128)(2,1)S(1)} %bitcast.68, bf16[48,8,8,128]{3,2,1,0:T(8,128)(2,1)S(1)} %copy-done.5), kind=kOutput, calls=%fused_computation.2 | convolution fusion | flops 1629484032 | bytes 30945280 | tf_op jit(solution)/shard_map/qhd,khd->hqk/dot_general | solution.py:47
  160.7 11.7 %fusion.1 = f32[8,384]{1,0:T(8,128)S(1)} fusion(f32[8,384,2048]{2,1,0:T(8,128)} %get-tuple-element.35, f32[8,384]{1,0:T(8,128)S(1)} %get-tuple-element.34, pred[384,2048]{1,0:T(8,128)(4,1)S(1)} %copy.101), kind=kLoop, calls=%fused_computation.3 | loop fusion | flops 25162752 | bytes 25976832 | tf_op jit(solution)/shard_map/reduce_sum | solution.py:53
  172.4 5.6 %multiply_convert_fusion.1 = bf16[2048,1024]{0,1:T(8,128)(2,1)S(1)} fusion(bf16[1024,1024]{1,0:T(8,128)(2,1)S(1)} %copy-done.13, f32[2048]{0:T(1024)S(1)} %add_rsqrt_fusion, bf16[2048,1024]{0,1:T(8,128)(2,1)S(1)} %copy-done.2, f32[1024]{0:T(1024)S(1)} %copy-done.16), kind=kOutput, calls=%fused_computation.13 | convolution fusion | flops 4305453056 | bytes 10498048 | tf_op jit(solution)/shard_map/dot_general | solution.py:153
  178.1 12.2 %fusion.28 = bf16[384,8,128]{0,2,1:T(8,128)(2,1)S(1)} fusion(bf16[2048,8,128]{0,2,1:T(8,128)(2,1)S(1)} %bitcast.76, f32[8,384,2048]{2,1,0:T(8,128)} %get-tuple-element.35, f32[8,384]{1,0:T(8,128)S(1)} %get-tuple-element.34, pred[384,2048]{1,0:T(8,128)(4,1)S(1)} %copy.101, f32[384,8]{0,1:T(8,128)S(1)} %bitcast.75), kind=kOutput, calls=%fused_computation.39 | convolution fusion | flops 1636564992 | bytes 30957568 | tf_op jit(solution)/shard_map/hqk,khd->qhd/dot_general | solution.py:55
  190.3 1.9 convolution_convert_fusion.4
  192.1 5.3 %all-to-all-start.3 = ((bf16[16,24,1024]{2,1,0:T(8,128)(2,1)}), bf16[16,24,1024]{2,1,0:T(8,128)(2,1)S(1)}, u32[]{:S(2)}, u32[]{:S(2)}) async-start(bf16[16,24,1024]{2,1,0:T(8,128)(2,1)} %bitcast.18), calls=%async_computation.3 | async-start | bytes 1572864 | tf_op jit(solution)/shard_map/all_to_all | solution.py:27
  197.4 14.3 %all-to-all-done.3 = bf16[16,24,1024]{2,1,0:T(8,128)(2,1)S(1)} async-done(((bf16[16,24,1024]{2,1,0:T(8,128)(2,1)}), bf16[16,24,1024]{2,1,0:T(8,128)(2,1)S(1)}, u32[]{:S(2)}, u32[]{:S(2)}) %all-to-all-start.3) | async-done | bytes 786464 | tf_op jit(solution)/shard_map/all_to_all | solution.py:27
  211.7 0.1 convert_reduce_fusion
  211.8 1.4 add_convert_fusion.1
  (51 shorter events, 0.7 us)
Async XLA Ops:
  7.2 136.7 %copy-start = (bf16[1024,1024]{1,0:T(8,128)(2,1)S(1)}, bf16[1024,1024]{1,0:T(8,128)(2,1)}, u32[]{:S(2)}) copy-start(bf16[1024,1024]{1,0:T(8,128)(2,1)} %param.31) | copy-start | bytes 6291460
  11.6 4.4 %copy-start.6 = (bf16[512,1024]{1,0:T(8,128)(2,1)S(1)}, bf16[512,1024]{1,0:T(8,128)(2,1)}, u32[]{:S(2)}) copy-start(bf16[512,1024]{1,0:T(8,128)(2,1)} %param.17) | copy-start | bytes 3145732
  11.6 4.4 %copy-start.11 = (bf16[1024,1024]{1,0:T(8,128)(2,1)S(1)}, bf16[1024,1024]{1,0:T(8,128)(2,1)}, u32[]{:S(2)}) copy-start(bf16[1024,1024]{1,0:T(8,128)(2,1)} %param.23) | copy-start | bytes 6291460
  11.6 4.4 %copy-start.14 = (f32[1024]{0:T(1024)S(1)}, f32[1024]{0:T(1024)}, u32[]{:S(2)}) copy-start(f32[1024]{0:T(1024)} %param.21) | copy-start | bytes 12292
  16.0 2.3 %copy-start.12 = (bf16[1024,1024]{1,0:T(8,128)(2,1)S(1)}, bf16[1024,1024]{1,0:T(8,128)(2,1)}, u32[]{:S(2)}) copy-start(bf16[1024,1024]{1,0:T(8,128)(2,1)} %param.24) | copy-start | bytes 6291460
  30.3 1.8 copy-start.7
  32.1 2.6 %copy-start.4 = (bf16[1024,1024]{0,1:T(8,128)(2,1)S(1)}, bf16[1024,1024]{0,1:T(8,128)(2,1)}, u32[]{:S(2)}) copy-start(bf16[1024,1024]{0,1:T(8,128)(2,1)} %copy.91) | copy-start | bytes 6291460
  37.2 39.0 %all-to-all-start = ((f32[16,512,64]{1,2,0:T(8,128)}), f32[16,512,64]{1,2,0:T(8,128)}, u32[]{:S(2)}, u32[]{:S(2)}) async-start(f32[16,512,64]{1,2,0:T(8,128)} %convolution_bitcast_fusion), calls=%async_computation | async-start | bytes 4194304 | tf_op jit(solution)/shard_map/all_to_all | solution.py:21
  44.4 49.0 %copy-start.9 = (s32[4]{0:T(128)S(1)}, s32[4]{0:T(128)}, u32[]{:S(2)}) copy-start(s32[4]{0:T(128)} %param.18) | copy-start | bytes 52
  44.4 54.8 %copy-start.15 = (f32[1024]{0:T(1024)S(1)}, f32[1024]{0:T(1024)}, u32[]{:S(2)}) copy-start(f32[1024]{0:T(1024)} %param.28) | copy-start | bytes 12292
  44.4 96.2 %all-gather.2.cloned.1.call-start = ((), (), s32[]{:S(2)}) async-start(), calls=%async_computation.4 | async-start | bytes 4456448 | tf_op jit(solution)/shard_map/all_gather | solution.py:150
  78.0 25.0 %copy-start.8 = (bf16[512,64]{0,1:T(8,128)(2,1)}, bf16[512,64]{0,1:T(8,128)(2,1)S(1)}, u32[]{:S(2)}) copy-start(bf16[512,64]{0,1:T(8,128)(2,1)S(1)} %add_convert_fusion) | copy-start | bytes 196612
  92.4 10.8 %copy-start.10 = (s32[384]{0:T(512)S(1)}, s32[384]{0:T(512)}, u32[]{:S(2)}) copy-start(s32[384]{0:T(512)} %param.27) | copy-start | bytes 4612
  94.3 8.8 %all-to-all-start.2 = ((s32[8,2,2]{1,2,0:T(2,128)}), s32[8,2,2]{1,2,0:T(2,128)S(1)}, u32[]{:S(2)}, u32[]{:S(2)}) async-start(s32[8,2,2]{1,2,0:T(2,128)} %copy.96), calls=%async_computation.2 | async-start | bytes 16384 | tf_op jit(solution)/shard_map/all_to_all | solution.py:147
  103.1 40.9 %copy-start.16 = (f32[1024]{0:T(1024)S(1)}, f32[1024]{0:T(1024)}, u32[]{:S(2)}) copy-start(f32[1024]{0:T(1024)} %param.29) | copy-start | bytes 12292
  140.7 3.4 %copy-start.2 = (bf16[2048,1024]{0,1:T(8,128)(2,1)S(1)}, bf16[2048,1024]{0,1:T(8,128)(2,1)}, u32[]{:S(2)}) copy-start(bf16[2048,1024]{0,1:T(8,128)(2,1)} %all-gather.2.cloned.1.call-done) | copy-start | bytes 12582916
  144.1 5.6 %copy-start.5 = (bf16[48,8,8,128]{3,2,1,0:T(8,128)(2,1)S(1)}, bf16[48,8,8,128]{3,2,1,0:T(8,128)(2,1)}, u32[]{:S(2)}) copy-start(bf16[48,8,8,128]{3,2,1,0:T(8,128)(2,1)} %fusion.33) | copy-start | bytes 2359300
  160.7 11.7 %copy-start.13 = (bf16[1024,1024]{1,0:T(8,128)(2,1)S(1)}, bf16[1024,1024]{1,0:T(8,128)(2,1)}, u32[]{:S(2)}) copy-start(bf16[1024,1024]{1,0:T(8,128)(2,1)} %param.32) | copy-start | bytes 6291460
  178.0 12.2 %copy-start.3 = (bf16[1024,1024]{1,0:T(8,128)(2,1)S(1)}, bf16[1024,1024]{1,0:T(8,128)(2,1)}, u32[]{:S(2)}) copy-start(bf16[1024,1024]{1,0:T(8,128)(2,1)} %param.33) | copy-start | bytes 6291460
  178.1 35.2 %copy-start.1 = (bf16[1024,1024]{1,0:T(8,128)(2,1)S(1)}, bf16[1024,1024]{1,0:T(8,128)(2,1)}, u32[]{:S(2)}) copy-start(bf16[1024,1024]{1,0:T(8,128)(2,1)} %param.31) | copy-start | bytes 6291460
  192.1 19.6 %all-to-all-start.3 = ((bf16[16,24,1024]{2,1,0:T(8,128)(2,1)}), bf16[16,24,1024]{2,1,0:T(8,128)(2,1)S(1)}, u32[]{:S(2)}, u32[]{:S(2)}) async-start(bf16[16,24,1024]{2,1,0:T(8,128)(2,1)} %bitcast.18), calls=%async_computation.3 | async-start | bytes 1572864 | tf_op jit(solution)/shard_map/all_to_all | solution.py:27
Sparse Core Ops, SparseCore 0:
  93.4 47.2 all-gather.1
where the time goes:
time: 221 us; the launch traced here: 220 us
  waiting for transfers between devices  79.8 us (36%)
  matrix products  57.7 us (26%)
  other arithmetic  27 us (12%)
  starting transfers between devices  16 us (7%)
  between operations  14.4 us (7%)
  blocking collectives  12.7 us (6%)
  local copies, waits for them, and re-layouts  12.6 us (6%)
    all_gather x1, waiting for transfers between devices, body(): lax.all_gather(flat, 'tensor', axis=1, tiled=True).astype(jnp.float32)  33.9 us
    all_to_all x1, waiting for transfers between devices, sent_and_summed(): lax.all_to_all(blocks, axis, split_axis=0, concat_axis=0, tiled=True)  31.5 us
    dot_general x2, matrix products, attend(): jnp.einsum('hqk,khd->qhd', weights, value_heads, preferred_element_type=j...  14.7 us
    all_to_all x1, waiting for transfers between devices, summed_on_arrival(): lax.all_to_all(blocks, axis, split_axis=0, concat_axis=0, tiled=True)  14.3 us
    dot_general x2, matrix products, attend(): jnp.einsum('qhd,khd->hqk', query_heads, key_heads, preferred_element_type...  14.1 us
    reduce_sum x2, other arithmetic, attend(): total = jnp.sum(expo, axis=2)  13.4 us
    all_to_all x1, blocking collectives, body(): lax.all_to_all(placed.reshape(groups, slots, BLOCK, features), 'dp', spli...  12.7 us
    all_to_all x1, starting transfers between devices, sent_and_summed(): lax.all_to_all(blocks, axis, split_axis=0, concat_axis=0, tiled=True)  7.19 us
  transfers between devices with their start and end apart: 4, of which 3 were waited for; matrix products, arithmetic and copies ran while one was open for 5% of the time, Pallas kernels for 0%

commit v1 on v0

v1 whole, which is shorter than its diff:
```python
import jax
import jax.numpy as jnp
import numpy as np
from jax import lax
from jax.experimental import pallas as pl
from jax.experimental.pallas import tpu as pltpu
from jax.sharding import PartitionSpec as P

HEAD_DIM = 128
BLOCK = 128
EPSILON = 1e-06
MASKED = -1000000000.0
SCALE = HEAD_DIM ** (-0.5)
BF16 = jnp.bfloat16
F32 = jnp.float32
VMEM_LIMIT = 56 * 1024 * 1024

VMEM = pl.BlockSpec(memory_space=pltpu.VMEM)
SMEM = pl.BlockSpec(memory_space=pltpu.SMEM)
ANY = pl.BlockSpec(memory_space=pl.ANY)

XA, XB, YA, YB = 1, 3, 4, 12
ORDERS = (((XA, XB, YA, YB), (XB, XA, YB, YA)), ((YA, YB, XA, XB), (YB, YA, XB, XA)))


def rms_scaled(x, gain):
    scale = lax.rsqrt(jnp.mean(x * x, axis=1, keepdims=True) + EPSILON)
    return (x * scale * gain).astype(BF16)


def dot(a, b):
    return jnp.dot(a, b, preferred_element_type=F32)


def dot_t(a, b):
    return lax.dot_general(a, b, (((1,), (1,)), ((), ())), preferred_element_type=F32)


def block_facts(blocks, protein_ref, length_ref):
    ids = [protein_ref[b] for b in range(blocks)]
    live = []
    for b in range(blocks):
        offset = jnp.int32(0)
        for other in range(b):
            offset += jnp.where(ids[other] == ids[b], BLOCK, 0)
        live.append(jnp.clip(length_ref[ids[b]] - offset, 0, BLOCK))
    return ids, live


def encoder_kernel(
    protein_ref,
    length_ref,
    residue_ref,
    gain_ref,
    wq_hbm,
    wk_hbm,
    wv_hbm,
    wo_hbm,
    out_ref,
    wq,
    wk,
    wv,
    wo,
    normed,
    q,
    k,
    v,
    context,
    sems,
):
    copies = [
        pltpu.make_async_copy(src, dst, sems.at[i])
        for i, (src, dst) in enumerate(((wq_hbm, wq), (wk_hbm, wk), (wv_hbm, wv), (wo_hbm, wo)))
    ]
    for copy in copies:
        copy.start()
    rows, width = residue_ref.shape
    blocks = rows // BLOCK
    inner = q.shape[1]
    ids, live = block_facts(blocks, protein_ref, length_ref)
    gain = gain_ref[...]
    for b in range(blocks):
        span = slice(b * BLOCK, (b + 1) * BLOCK)
        normed[span, :] = rms_scaled(residue_ref[span, :].astype(F32), gain)
    for copy, weight, result in zip(copies[:3], (wq, wk, wv), (q, k, v)):
        copy.wait()

        @pl.loop(0, inner // 256)
        def _(n):
            cols = pl.ds(pl.multiple_of(n * 256, 256), 256)
            result[:, cols] = dot(normed[...], weight[:, cols]).astype(BF16)

    lane = lax.broadcasted_iota(jnp.int32, (1, BLOCK), 1)

    @pl.loop(0, inner // HEAD_DIM)
    def _(h):
        cols = pl.ds(pl.multiple_of(h * HEAD_DIM, HEAD_DIM), HEAD_DIM)
        for b in range(blocks):
            low, high = max(0, b - 1), min(blocks, b + 2)
            span = slice(b * BLOCK, (b + 1) * BLOCK)
            keys = slice(low * BLOCK, high * BLOCK)
            scores = dot_t(q[span, cols], k[keys, cols]) * SCALE
            seen = jnp.concatenate(
                [
                    jnp.broadcast_to(lane < jnp.where(ids[o] == ids[b], live[o], 0), (BLOCK, BLOCK))
                    for o in range(low, high)
                ],
                axis=1,
            )
            scores = jnp.where(seen, scores, MASKED)
            top = jnp.max(scores, axis=1, keepdims=True)
            expo = jnp.exp(scores - top)
            total = jnp.sum(expo, axis=1, keepdims=True)
            mixed = dot(expo.astype(BF16), v[keys, cols])
            context[span, cols] = (mixed / total).astype(BF16)

    copies[3].wait()

    @pl.loop(0, width // 256)
    def _(n):
        cols = pl.ds(pl.multiple_of(n * 256, 256), 256)
        out_ref[cols, :] = dot(context[...], wo[:, cols]).T.astype(BF16)


def encoder(protein, length, residues, gain, wq, wk, wv, wo):
    rows, width = residues.shape
    inner = wq.shape[1]
    return pl.pallas_call(
        encoder_kernel,
        out_shape=jax.ShapeDtypeStruct((width, rows), BF16),
        in_specs=[SMEM, SMEM, VMEM, VMEM, ANY, ANY, ANY, ANY],
        out_specs=VMEM,
        scratch_shapes=[pltpu.VMEM((width, inner), BF16)] * 3
        + [pltpu.VMEM((inner, width), BF16), pltpu.VMEM((rows, width), BF16)]
        + [pltpu.VMEM((rows, inner), BF16)] * 4
        + [pltpu.SemaphoreType.DMA((4,))],
        compiler_params=pltpu.CompilerParams(vmem_limit_bytes=VMEM_LIMIT),
        cost_estimate=pl.CostEstimate(
            flops=2 * rows * width * inner * 4, bytes_accessed=8 * width * inner, transcendentals=rows * rows * 8
        ),
        name="encoder",
    )(protein, length, residues, gain, wq, wk, wv, wo)


def query_kernel(
    state_ref, dec_gain_ref, final_gain_ref, id_row_ref, id_col_ref, wq_ref, wk_ref, out_ref, back_ref, id_ref
):
    rows = state_ref.shape[0]
    id_row = id_row_ref[...]
    id_col = id_col_ref[...]
    down = lax.broadcasted_iota(jnp.int32, (rows, rows), 0)
    along = lax.broadcasted_iota(jnp.int32, (rows, rows), 1)
    before = (id_col < id_row) | ((id_col == id_row) & (down < along))
    place_row = jnp.sum(before.astype(F32), axis=0, keepdims=True).astype(jnp.int32)
    before = (id_row < id_col) | ((id_row == id_col) & (along < down))
    place_col = jnp.sum(before.astype(F32), axis=1, keepdims=True).astype(jnp.int32)
    chosen = down == place_row
    back_ref[...] = (along == place_col).astype(F32).astype(BF16)
    id_ref[...] = jnp.sum(jnp.where(chosen, id_row.astype(F32), 0.0), axis=1, keepdims=True)
    normed = rms_scaled(state_ref[...].astype(F32), dec_gain_ref[...])
    normed = dot(chosen.astype(F32).astype(BF16), normed).astype(BF16)
    gain = final_gain_ref[...]
    for pair in range(wq_ref.shape[1] // 256):
        queries = dot(normed, wq_ref[:, pair * 256 : (pair + 1) * 256]).astype(BF16)
        for side in range(2):
            h = pair * 2 + side
            head = queries[:, side * HEAD_DIM : (side + 1) * HEAD_DIM]
            back = dot_t(head, wk_ref[:, h * HEAD_DIM : (h + 1) * HEAD_DIM])
            out_ref[h] = (back * gain).astype(BF16)


def query_side(states, dec_gain, final_gain, ids, wq, wk):
    rows, width = states.shape
    inner = wq.shape[1]
    heads = inner // HEAD_DIM
    return pl.pallas_call(
        query_kernel,
        out_shape=(
            jax.ShapeDtypeStruct((heads, rows, width), BF16),
            jax.ShapeDtypeStruct((rows, rows), BF16),
            jax.ShapeDtypeStruct((rows, 1), F32),
        ),
        in_specs=[VMEM] * 7,
        out_specs=(VMEM,) * 3,
        compiler_params=pltpu.CompilerParams(vmem_limit_bytes=VMEM_LIMIT),
        cost_estimate=pl.CostEstimate(
            flops=4 * rows * width * inner, bytes_accessed=4 * width * inner + 2 * heads * rows * width, transcendentals=0
        ),
        name="query_side",
    )(states, dec_gain, final_gain, ids.reshape(1, rows), ids.reshape(rows, 1), wq, wk)


def placing_kernel(protein_ref, length_ref, group_ref, arrived_ref, own_ref, encoded_ref, placed_ref):
    sources, features, rows = arrived_ref.shape
    blocks = rows // BLOCK
    groups = placed_ref.shape[0]
    slots = placed_ref.shape[2] // BLOCK
    total = own_ref[...].astype(F32)
    sums = arrived_ref[0].astype(F32)
    for s in range(1, sources):
        sums = sums + arrived_ref[s].astype(F32)
    encoded_ref[...] = (total + sums).astype(BF16)
    ids, live = block_facts(blocks, protein_ref, length_ref)
    dest = [group_ref[ids[b]] for b in range(blocks)]
    rank = []
    for b in range(blocks):
        count = jnp.int32(0)
        for other in range(b):
            count += jnp.where(dest[other] == dest[b], 1, 0)
        rank.append(count)
    lane = lax.broadcasted_iota(jnp.int32, (16, BLOCK), 1)
    for d in range(groups):
        for s in range(slots):
            block, name, limit = jnp.int32(0), jnp.int32(-1), jnp.int32(0)
            for b in range(blocks):
                here = (dest[b] == d) & (rank[b] == s)
                block = jnp.where(here, b, block)
                name = jnp.where(here, ids[b], name)
                limit = jnp.where(here, live[b], limit)
            cols = slice(s * BLOCK, (s + 1) * BLOCK)
            start = pl.multiple_of(block * BLOCK, BLOCK)
            placed_ref[d, 0:features, cols] = encoded_ref[:, pl.ds(start, BLOCK)]
            placed_ref[d, features : features + 16, cols] = (
                jnp.where(lane < limit, name, -1).astype(F32).astype(BF16)
            )


def placing(protein, length, group, arrived, own, groups):
    sources, features, rows = arrived.shape
    slots = rows // BLOCK // 2
    return pl.pallas_call(
        placing_kernel,
        out_shape=(
            jax.ShapeDtypeStruct((features, rows), BF16),
            jax.ShapeDtypeStruct((groups, features + 16, slots * BLOCK), BF16),
        ),
        in_specs=[SMEM, SMEM, SMEM, VMEM, VMEM],
        out_specs=(VMEM, VMEM),
        compiler_params=pltpu.CompilerParams(vmem_limit_bytes=VMEM_LIMIT),
        name="placing",
    )(protein, length, group, arrived, own)


ROW_TILE = 32


def cross_kernel(
    start_ref,
    origin_ref,
    query_ref,
    id_ref,
    key_id_ref,
    gain_ref,
    back_ref,
    low_hbm,
    high_hbm,
    wv_hbm,
    wo_hbm,
    out_ref,
    keys,
    key_scale,
    mixed,
    context,
    wv,
    wo,
    key_sem,
    weight_sems,
):
    heads, rows, width = query_ref.shape
    groups, _, span = keys.shape
    chunks, _, part, _ = low_hbm.shape
    weight_copies = [
        pltpu.make_async_copy(wv_hbm, wv, weight_sems.at[0]),
        pltpu.make_async_copy(wo_hbm, wo, weight_sems.at[1]),
    ]
    key_copies = []
    for half, source in enumerate((low_hbm, high_hbm)):
        for j in range(chunks):
            at = pl.multiple_of(origin_ref[half * chunks + j] * (2 * part) + half * part, part)
            key_copies.append(pltpu.make_async_copy(source.at[j], keys.at[:, pl.ds(at, part), :], key_sem))
    for copy in key_copies:
        copy.start()
    for copy in weight_copies:
        copy.start()
    for copy in key_copies:
        copy.wait()

    @pl.loop(0, groups)
    def _(e):
        squares = jnp.zeros((8, span), F32)
        for piece in range(width // 128):
            values = keys[e, piece * 128 : (piece + 1) * 128, :].astype(F32)
            squares = squares + jnp.sum((values * values).reshape(16, 8, span), axis=0)
        total = jnp.sum(squares, axis=0, keepdims=True)
        key_scale[e] = lax.rsqrt(total / width + EPSILON)

    gain = gain_ref[...]
    flat = heads * ROW_TILE

    @pl.loop(0, groups)
    def _(e):
        first = start_ref[e] // ROW_TILE
        last = (start_ref[e + 1] + ROW_TILE - 1) // ROW_TILE

        @pl.when(start_ref[e + 1] > start_ref[e])
        def _():
            @pl.loop(first, last)
            def _(i):
                at = pl.ds(pl.multiple_of(i * ROW_TILE, ROW_TILE), ROW_TILE)
                ids = id_ref[at, :]
                scale = key_scale[e]
                seen = ids == key_id_ref[e]
                mine = (ids >= (e * 4).astype(F32)) & (ids < (e * 4 + 4).astype(F32))
                scores = dot(query_ref[:, at, :].reshape(flat, width), keys[e]) * (scale * SCALE)
                scores = jnp.where(seen[None], scores.reshape(heads, ROW_TILE, span), MASKED)
                top = jnp.max(scores, axis=2, keepdims=True)
                expo = jnp.exp(scores - top)
                total = jnp.sum(expo, axis=2, keepdims=True)
                weights = (expo * scale[None]).astype(BF16).reshape(flat, span)
                spread = dot_t(weights, keys[e]).reshape(heads, ROW_TILE, width)
                spread = (spread * (1.0 / total) * gain[None]).astype(BF16)
                mixed[:, at, :] = jnp.where(mine[None], spread, mixed[:, at, :])

    for copy in weight_copies:
        copy.wait()

    @pl.loop(0, heads)
    def _(h):
        cols = pl.ds(pl.multiple_of(h * HEAD_DIM, HEAD_DIM), HEAD_DIM)
        context[:, cols] = dot(mixed[h], wv[:, cols]).astype(BF16)

    context[...] = dot(back_ref[...], context[...]).astype(BF16)

    @pl.loop(0, width // 256)
    def _(n):
        cols = pl.ds(pl.multiple_of(n * 256, 256), 256)
        out_ref[:, cols] = dot(context[...], wo[:, cols]).astype(BF16)


def cross(starts, origins, queries, ids, key_ids, gain, back, low, high, wv, wo):
    heads, rows, width = queries.shape
    groups, span = key_ids.shape[0], key_ids.shape[2]
    inner = wv.shape[1]
    return pl.pallas_call(
        cross_kernel,
        out_shape=jax.ShapeDtypeStruct((rows, width), BF16),
        in_specs=[SMEM, SMEM] + [VMEM] * 5 + [ANY] * 4,
        out_specs=VMEM,
        scratch_shapes=[
            pltpu.VMEM((groups, width, span), BF16),
            pltpu.VMEM((groups, 1, span), F32),
            pltpu.VMEM((heads, rows, width), BF16),
            pltpu.VMEM((rows, inner), BF16),
            pltpu.VMEM((width, inner), BF16),
            pltpu.VMEM((inner, width), BF16),
            pltpu.SemaphoreType.DMA,
            pltpu.SemaphoreType.DMA((2,)),
        ],
        compiler_params=pltpu.CompilerParams(vmem_limit_bytes=VMEM_LIMIT),
        cost_estimate=pl.CostEstimate(
            flops=8 * rows * width * inner, bytes_accessed=2 * groups * width * span, transcendentals=rows * span * heads
        ),
        name="cross",
    )(starts, origins, queries, ids, key_ids, gain, back, low, high, wv, wo)


def exchange(x, groups, tensor, half, step):
    pairs = [
        (d * tensor + t, d * tensor + (t ^ ORDERS[d % 2][half][step]))
        for d in range(groups)
        for t in range(tensor)
    ]
    return lax.ppermute(x, ("dp", "tensor"), pairs)


def gathered(low, high, groups, tensor):
    halves = [low[None], high[None]]
    for step in range(4):
        got = [exchange(halves[h], groups, tensor, h, step) for h in range(2)]
        halves = [jnp.concatenate([halves[h], got[h]], axis=0) for h in range(2)]
    return halves


def origin_masks():
    table = np.zeros((2, 2, 16), np.int32)
    for core in range(2):
        for half in range(2):
            for j in range(16):
                for step in range(4):
                    if j >> step & 1:
                        table[core, half, j] ^= ORDERS[core][half][step]
    return table.reshape(2, 32)


def body(
    residues,
    block_protein,
    protein_length,
    decoder_group,
    enc_gain,
    enc_query,
    enc_key,
    enc_value,
    enc_out,
    decoder_states,
    query_protein,
    dec_gain,
    final_gain,
    cross_query,
    cross_key,
    cross_value,
    cross_out,
):
    groups = lax.axis_size("dp")
    tensor = lax.axis_size("tensor")
    dp_index = lax.axis_index("dp")
    tensor_index = lax.axis_index("tensor")
    rows, width = residues.shape
    query_rows = decoder_states.shape[0]
    slice_width = width // tensor
    part = slice_width // 2

    partial_sums = encoder(
        block_protein, protein_length, residues, enc_gain.reshape(1, width), enc_query, enc_key, enc_value, enc_out
    )
    arrived = lax.all_to_all(
        partial_sums.reshape(tensor, slice_width, rows), "tensor", split_axis=0, concat_axis=0, tiled=True
    )
    queries, back, sorted_ids = query_side(
        decoder_states, dec_gain.reshape(1, width), final_gain.reshape(1, width), query_protein, cross_query, cross_key
    )
    bounds = 4 * jnp.arange(groups + 1, dtype=jnp.int32)
    starts = jnp.sum((query_protein[None, :] < bounds[:, None]).astype(jnp.int32), axis=1)
    masks = origin_masks()
    origins = tensor_index.astype(jnp.int32) ^ jnp.where(dp_index % 2 == 0, masks[0], masks[1])
    own = lax.dynamic_slice_in_dim(residues, tensor_index * slice_width, slice_width, 1).T
    encoded, placed = placing(block_protein, protein_length, decoder_group, arrived, own, groups)
    received = lax.all_to_all(placed, "dp", split_axis=0, concat_axis=0, tiled=True)
    low, high = gathered(received[:, :part], received[:, part : 2 * part], groups, tensor)
    key_ids = received[:, slice_width : slice_width + 1].astype(F32)
    outcome = cross(
        starts,
        origins,
        queries,
        sorted_ids,
        key_ids,
        final_gain.reshape(1, width),
        back,
        low,
        high,
        cross_value,
        cross_out,
    )
    share = query_rows // tensor
    mixed = lax.all_to_all(
        outcome.reshape(tensor, share, width), "tensor", split_axis=0, concat_axis=0, tiled=True
    )
    mixed = mixed.astype(F32).sum(axis=0)
    own_rows = lax.dynamic_slice_in_dim(decoder_states, tensor_index * share, share, 0)
    decoded = (own_rows.astype(F32) + mixed).astype(BF16)
    return (encoded.T, decoded)


def solution(mesh):
    in_specs = (
        P("dp", None),
        P("dp"),
        P(),
        P(),
        P(),
        P(None, "tensor"),
        P(None, "tensor"),
        P(None, "tensor"),
        P("tensor", None),
        P("dp", None),
        P("dp"),
        P(),
        P(),
        P(None, "tensor"),
        P(None, "tensor"),
        P(None, "tensor"),
        P("tensor", None),
    )
    out_specs = (P("dp", "tensor"), P(("dp", "tensor"), None))
    return jax.shard_map(body, mesh=mesh, in_specs=in_specs, out_specs=out_specs, check_vma=False)
```

time: 221 us -> 152 us (0.69)
  matrix products: 57.7 us -> 0 us
  Pallas kernels: 0 us -> 55.4 us
  waiting for transfers between devices: 79.8 us -> 51.1 us
  other arithmetic: 27 us -> 3.88 us
  between operations: 14.4 us -> 0.89 us
  local copies, waits for them, and re-layouts: 12.6 us -> 5.8 us
  starting transfers between devices: 16 us -> 18.6 us
    dot_general x13 -> x0, matrix products: 57.7 us -> none  [the longest x2 14.7 us: attend(): jnp.einsum('hqk,khd->qhd', weights, value_heads, preferred_element_type=j...]
    pallas_call x0 -> x4, Pallas kernels: none -> 55.4 us  [the longest x1 23.3 us: cross(): pl.pallas_call(cross_kernel, out_shape=jax.ShapeDtypeStruct((rows, width)...]
    all_gather x1 -> x0, waiting for transfers between devices: 33.9 us -> none  [body(): lax.all_gather(flat, 'tensor', axis=1, tiled=True).astype(jnp.float32)]
    ppermute x0 -> x8, waiting for transfers between devices: none -> 23.6 us  [exchange(): return lax.ppermute(x, ('dp', 'tensor'), pairs)]
    reduce_sum x11 -> x2, other arithmetic: 23.6 us -> 0.88 us  [the longest x1 0.76 us: body(): jnp.sum((query_protein[None, :] < bounds[:, None]).astype(jnp.int32), axi...]
    all_to_all x3 -> x2, waiting for transfers between devices: 45.8 us -> 27.5 us  [the longest x1 15.9 us: body(): lax.all_to_all(partial_sums.reshape(tensor, slice_width, rows), 'tensor',...]
    ppermute x0 -> x8, starting transfers between devices: none -> 7.24 us  [exchange(): return lax.ppermute(x, ('dp', 'tensor'), pairs)]
    all_to_all x3 -> x2, starting transfers between devices: 16 us -> 11.4 us  [the longest x1 7.16 us: body(): lax.all_to_all(partial_sums.reshape(tensor, slice_width, rows), 'tensor',...]
  transfers between devices with their start and end apart: 4 -> 10, of which waited for: 3 -> 7; matrix products, arithmetic and copies ran while one was open for 5% -> 4% of each run, Pallas kernels for 0% -> 6%
where the time goes in v1:
time: 152 us; the launch traced here: 149 us
  Pallas kernels  55.4 us (36%)
  waiting for transfers between devices  51.1 us (34%)
  starting transfers between devices  18.6 us (12%)
  blocking collectives  13.6 us (9%)
  local copies, waits for them, and re-layouts  5.8 us (4%)
  other arithmetic  3.88 us (3%)
    ppermute x8, waiting for transfers between devices, exchange(): return lax.ppermute(x, ('dp', 'tensor'), pairs)  23.6 us
    pallas_call x1, Pallas kernels, cross(): pl.pallas_call(cross_kernel, out_shape=jax.ShapeDtypeStruct((rows, width)...  23.3 us
    pallas_call x1, Pallas kernels, encoder(): pl.pallas_call(encoder_kernel, out_shape=jax.ShapeDtypeStruct((width, row...  20.5 us
    all_to_all x1, waiting for transfers between devices, body(): lax.all_to_all(partial_sums.reshape(tensor, slice_width, rows), 'tensor',...  15.9 us
    all_to_all x1, blocking collectives, body(): lax.all_to_all(placed, 'dp', split_axis=0, concat_axis=0, tiled=True)  13.6 us
    all_to_all x1, waiting for transfers between devices, body(): lax.all_to_all(outcome.reshape(tensor, share, width), 'tensor', split_axi...  11.6 us
    pallas_call x1, Pallas kernels, query_side(): pl.pallas_call(query_kernel, out_shape=(jax.ShapeDtypeStruct((heads, rows...  9.32 us
    ppermute x8, starting transfers between devices, exchange(): return lax.ppermute(x, ('dp', 'tensor'), pairs)  7.24 us
  transfers between devices with their start and end apart: 10, of which 7 were waited for; matrix products, arithmetic and copies ran while one was open for 4% of the time, Pallas kernels for 6%

profile of v1, /device:TPU:0, one launch (start us, length us, event | category | flops | bytes accessed | tf_op | source)
XLA Modules:
  0.0 149.4 jit_solution(12824013136654036057)
XLA Ops:
  0.6 20.5 %encoder.1 = bf16[1024,512]{1,0:T(8,128)(2,1)} custom-call(s32[4]{0:T(128)} %protein_ref.3, s32[32]{0:T(128)} %length_ref.3, bf16[512,1024]{1,0:T(8,128)(2,1)} %residue_ref.1, f32[1,1024]{1,0:T(1,128)} %bitcast.21, bf16[1024,1024]{1,0:T(8,128)(2,1)} %wq_hbm.1, bf16[1024,1024]{1,0:T(8,128)(2,1)} %wk_hbm.1, bf16[1024,1024]{1,0:T(8,128)(2,1)} %wv_hbm.2, ...), custom_call_target="tpu_custom_call" | custom-call | flops 4294967296 | bytes 8388608 | tf_op jit(solution)/shard_map/encoder/pallas_call | solution.py:128
  21.1 7.2 %all-to-all-start = ((bf16[16,64,512]{2,1,0:T(8,128)(2,1)}), bf16[16,64,512]{2,1,0:T(8,128)(2,1)S(1)}, u32[]{:S(2)}, u32[]{:S(2)}) async-start(bf16[16,64,512]{2,1,0:T(8,128)(2,1)} %bitcast.16), calls=%async_computation | async-start | bytes 2097152 | tf_op jit(solution)/shard_map/all_to_all | solution.py:426
  28.3 0.0 copy-start.4
  28.3 0.0 copy-start.5
  28.3 1.0 constant_dynamic-slice_fusion
  29.3 0.7 copy.26
  30.1 15.9 %all-to-all-done.arrived_ref = bf16[16,64,512]{2,1,0:T(8,128)(2,1)S(1)} async-done(((bf16[16,64,512]{2,1,0:T(8,128)(2,1)}), bf16[16,64,512]{2,1,0:T(8,128)(2,1)S(1)}, u32[]{:S(2)}, u32[]{:S(2)}) %all-to-all-start) | async-done | bytes 1048608 | tf_op jit(solution)/shard_map/all_to_all | solution.py:426
  46.0 1.0 copy-done
  47.0 2.3 %placing.1 = (bf16[64,512]{1,0:T(8,128)(2,1)}, bf16[8,80,256]{2,1,0:T(8,128)(2,1)}) custom-call(s32[4]{0:T(128)} %protein_ref.3, s32[32]{0:T(128)} %length_ref.3, s32[32]{0:T(128)} %group_ref.1, bf16[16,64,512]{2,1,0:T(8,128)(2,1)} %copy-done, bf16[64,512]{1,0:T(8,128)(2,1)} %bitcast.17), custom_call_target="tpu_custom_call" | custom-call | tf_op jit(solution)/shard_map/placing/pallas_call | solution.py:231
  49.2 13.6 %all_to_all.15 = bf16[8,80,256]{2,1,0:T(8,128)(2,1)S(1)} all-to-all(bf16[8,80,256]{2,1,0:T(8,128)(2,1)} %get-tuple-element.10), channel_id=1, replica_groups=mesh['dp'=8,'tensor'=16] {'dp'}, dimensions={0} | all-to-all | bytes 655360 | tf_op jit(solution)/shard_map/all_to_all | solution.py:438
  62.9 0.1 collective-permute-start.4
  63.0 0.2 collective-permute-start
  63.2 5.9 %collective-permute-done.4 = bf16[1,8,32,256]{3,2,1,0:T(8,128)(2,1)S(1)} collective-permute-done((bf16[1,8,32,256]{3,2,1,0:T(8,128)(2,1)S(1)}, bf16[1,8,32,256]{3,2,1,0:T(8,128)(2,1)S(1)}, u32[]{:S(2)}, u32[]{:S(2)}) %collective-permute-start.4) | collective-permute-done | bytes 131104 | tf_op jit(solution)/shard_map/ppermute | solution.py:373
  69.2 0.1 collective-permute-start.5
  69.3 0.0 collective-permute-done
  69.3 2.0 %collective-permute-start.1 = (bf16[2,8,32,256]{3,2,1,0:T(8,128)(2,1)S(1)}, bf16[2,8,32,256]{3,2,1,0:T(8,128)(2,1)S(1)}, u32[]{:S(2)}, u32[]{:S(2)}) collective-permute-start(bf16[2,8,32,256]{3,2,1,0:T(8,128)(2,1)S(1)} %pad_maximum_fusion.4), channel_id=1, source_target_pairs={{0,3},{1,2},{2,1},{3,0},{4,7},{5,6},{6,5},{7,4},{8,11},{9,10},{10,... | collective-permute-start | bytes 786440 | tf_op jit(solution)/shard_map/ppermute | solution.py:373
  71.3 0.0 copy-done.4
  71.3 0.0 copy-done.5
  71.3 0.6 fusion.origin_ref
  71.9 3.7 %collective-permute-done.5 = bf16[2,8,32,256]{3,2,1,0:T(8,128)(2,1)S(1)} collective-permute-done((bf16[2,8,32,256]{3,2,1,0:T(8,128)(2,1)S(1)}, bf16[2,8,32,256]{3,2,1,0:T(8,128)(2,1)S(1)}, u32[]{:S(2)}, u32[]{:S(2)}) %collective-permute-start.5) | collective-permute-done | bytes 262176 | tf_op jit(solution)/shard_map/ppermute | solution.py:373
  75.6 0.1 pad_maximum_fusion.3
  75.7 0.4 collective-permute-start.6
  76.1 0.9 collective-permute-done.1
  77.0 0.1 pad_maximum_fusion.2
  77.0 0.1 collective-permute-start.2
  77.1 0.0 copy-done.3
  77.1 0.8 convert_reduce_fusion.1.start_ref
  77.9 0.6 broadcast_in_dim.10.id_row_ref
  78.5 0.8 reshape.35.id_col_ref
  79.3 9.3 %query_side.1 = (bf16[8,384,1024]{2,1,0:T(8,128)(2,1)}, bf16[384,384]{1,0:T(8,128)(2,1)}, f32[384,1]{1,0:T(8,128)}) custom-call(bf16[384,1024]{1,0:T(8,128)(2,1)} %state_ref.1, f32[1,1024]{1,0:T(1,128)} %bitcast.22, f32[1,1024]{1,0:T(1,128)} %bitcast.18, s32[1,384]{1,0:T(1,128)} %broadcast_in_dim.10.id_row_ref, s32[384,1]{1,0:T(8,128)} %reshape.35.id_col_ref, ...), custom_call_target="tpu_custom_call" | custom-call | flops 1610612736 | bytes 10485760 | tf_op jit(solution)/shard_map/query_side/pallas_call | solution.py:176
  88.6 0.0 collective-permute-done.6
  88.6 0.1 pad_maximum_fusion.1
  88.7 2.1 %collective-permute-start.7 = (bf16[8,8,32,256]{3,2,1,0:T(8,128)(2,1)S(1)}, bf16[8,8,32,256]{3,2,1,0:T(8,128)(2,1)S(1)}, u32[]{:S(2)}, u32[]{:S(2)}) collective-permute-start(bf16[8,8,32,256]{3,2,1,0:T(8,128)(2,1)S(1)} %pad_maximum_fusion.1), channel_id=1, source_target_pairs={{0,4},{1,5},{2,6},{3,7},{4,0},{5,1},{6,2},{7,3},{8,12},{9,13},{10,... | collective-permute-start | bytes 3145736 | tf_op jit(solution)/shard_map/ppermute | solution.py:373
  90.8 0.0 collective-permute-done.2
  90.8 0.1 pad_maximum_fusion
  90.9 2.3 %collective-permute-start.3 = (bf16[8,8,32,256]{3,2,1,0:T(8,128)(2,1)S(1)}, bf16[8,8,32,256]{3,2,1,0:T(8,128)(2,1)S(1)}, u32[]{:S(2)}, u32[]{:S(2)}) collective-permute-start(bf16[8,8,32,256]{3,2,1,0:T(8,128)(2,1)S(1)} %pad_maximum_fusion), channel_id=1, source_target_pairs={{0,12},{1,13},{2,14},{3,15},{4,8},{5,9},{6,10},{7,11},{8,4},{9,5},... | collective-permute-start | bytes 3145736 | tf_op jit(solution)/shard_map/ppermute | solution.py:373
  93.2 0.6 slice_convert_fusion.key_id_ref
  94.0 9.6 %collective-permute-done.7 = bf16[8,8,32,256]{3,2,1,0:T(8,128)(2,1)S(1)} collective-permute-done((bf16[8,8,32,256]{3,2,1,0:T(8,128)(2,1)S(1)}, bf16[8,8,32,256]{3,2,1,0:T(8,128)(2,1)S(1)}, u32[]{:S(2)}, u32[]{:S(2)}) %collective-permute-start.7) | collective-permute-done | bytes 1048608 | tf_op jit(solution)/shard_map/ppermute | solution.py:373
  103.6 0.1 constant_dynamic-update-slice_fusion.5.high_hbm
  103.7 0.0 copy-start.2
  103.7 3.5 %collective-permute-done.3 = bf16[8,8,32,256]{3,2,1,0:T(8,128)(2,1)S(1)} collective-permute-done((bf16[8,8,32,256]{3,2,1,0:T(8,128)(2,1)S(1)}, bf16[8,8,32,256]{3,2,1,0:T(8,128)(2,1)S(1)}, u32[]{:S(2)}, u32[]{:S(2)}) %collective-permute-start.3) | collective-permute-done | bytes 1048608 | tf_op jit(solution)/shard_map/ppermute | solution.py:373
  107.2 0.1 constant_dynamic-update-slice_fusion.low_hbm
  107.3 1.3 copy-done.1
  108.7 23.3 %cross.1 = bf16[384,1024]{1,0:T(8,128)(2,1)} custom-call(s32[9]{0:T(128)} %convert_reduce_fusion.1.start_ref, s32[32]{0:T(128)} %fusion.origin_ref, bf16[8,384,1024]{2,1,0:T(8,128)(2,1)} %get-tuple-element.8.query_ref, f32[384,1]{1,0:T(8,128)} %get-tuple-element.9.id_ref, f32[8,1,256]{2,1,0:T(1,128)} %slice_convert_fusion.key_id_ref, f32[1,1024]{1,0:T(1,128)} %bitcast.19, ...), custom_call_target="tpu_custom_call" | custom-call | flops 3221225472 | bytes 4194304 | tf_op jit(solution)/shard_map/cross/pallas_call | solution.py:344
  132.0 4.2 %all-to-all-start.2 = ((bf16[16,24,1024]{2,1,0:T(8,128)(2,1)}), bf16[16,24,1024]{2,1,0:T(8,128)(2,1)S(1)}, u32[]{:S(2)}, u32[]{:S(2)}) async-start(bf16[16,24,1024]{2,1,0:T(8,128)(2,1)} %bitcast.15), calls=%async_computation.2 | async-start | bytes 1572864 | tf_op jit(solution)/shard_map/all_to_all | solution.py:455
  136.2 11.6 %all-to-all-done.2 = bf16[16,24,1024]{2,1,0:T(8,128)(2,1)S(1)} async-done(((bf16[16,24,1024]{2,1,0:T(8,128)(2,1)}), bf16[16,24,1024]{2,1,0:T(8,128)(2,1)S(1)}, u32[]{:S(2)}, u32[]{:S(2)}) %all-to-all-start.2) | async-done | bytes 786464 | tf_op jit(solution)/shard_map/all_to_all | solution.py:455
  147.8 0.1 convert_reduce_fusion
  147.9 1.4 add_convert_fusion
  (15 shorter events, 0.2 us)
Async XLA Ops:
  21.1 24.8 %all-to-all-start = ((bf16[16,64,512]{2,1,0:T(8,128)(2,1)}), bf16[16,64,512]{2,1,0:T(8,128)(2,1)S(1)}, u32[]{:S(2)}, u32[]{:S(2)}) async-start(bf16[16,64,512]{2,1,0:T(8,128)(2,1)} %bitcast.16), calls=%async_computation | async-start | bytes 2097152 | tf_op jit(solution)/shard_map/all_to_all | solution.py:426
  28.3 43.0 %copy-start.4 = (s32[32]{0:T(128)S(1)}, s32[32]{0:T(128)}, u32[]{:S(2)}) copy-start(s32[32]{0:T(128)} %constant.40.clone) | copy-start | bytes 388
  28.3 43.0 %copy-start.5 = (s32[32]{0:T(128)S(1)}, s32[32]{0:T(128)}, u32[]{:S(2)}) copy-start(s32[32]{0:T(128)} %constant.39.clone) | copy-start | bytes 388
  46.0 1.0 copy-start
  49.2 27.9 %copy-start.3 = (s32[384]{0:T(512)S(1)}, s32[384]{0:T(512)}, u32[]{:S(2)}) copy-start(s32[384]{0:T(512)} %param.29) | copy-start | bytes 4612
  62.9 6.3 %collective-permute-start.4 = (bf16[1,8,32,256]{3,2,1,0:T(8,128)(2,1)S(1)}, bf16[1,8,32,256]{3,2,1,0:T(8,128)(2,1)S(1)}, u32[]{:S(2)}, u32[]{:S(2)}) collective-permute-start(bf16[1,8,32,256]{3,2,1,0:T(8,128)(2,1)S(1)} %get-tuple-element.12), channel_id=1, source_target_pairs={{0,3},{1,2},{2,1},{3,0},{4,7},{5,6},{6,5},{7,4},{8,11},{9,10},{10,... | collective-permute-start | bytes 393224 | tf_op jit(solution)/shard_map/ppermute | solution.py:373
  63.0 6.3 %collective-permute-start = (bf16[1,8,32,256]{3,2,1,0:T(8,128)(2,1)S(1)}, bf16[1,8,32,256]{3,2,1,0:T(8,128)(2,1)S(1)}, u32[]{:S(2)}, u32[]{:S(2)}) collective-permute-start(bf16[1,8,32,256]{3,2,1,0:T(8,128)(2,1)S(1)} %get-tuple-element.13), channel_id=1, source_target_pairs={{0,1},{1,0},{2,3},{3,2},{4,5},{5,4},{6,7},{7,6},{8,9},{9,8},{10,11... | collective-permute-start | bytes 393224 | tf_op jit(solution)/shard_map/ppermute | solution.py:373
  69.2 6.5 %collective-permute-start.5 = (bf16[2,8,32,256]{3,2,1,0:T(8,128)(2,1)S(1)}, bf16[2,8,32,256]{3,2,1,0:T(8,128)(2,1)S(1)}, u32[]{:S(2)}, u32[]{:S(2)}) collective-permute-start(bf16[2,8,32,256]{3,2,1,0:T(8,128)(2,1)S(1)} %pad_maximum_fusion.5), channel_id=1, source_target_pairs={{0,1},{1,0},{2,3},{3,2},{4,5},{5,4},{6,7},{7,6},{8,9},{9,8},{10,11... | collective-permute-start | bytes 786440 | tf_op jit(solution)/shard_map/ppermute | solution.py:373
  69.3 7.7 %collective-permute-start.1 = (bf16[2,8,32,256]{3,2,1,0:T(8,128)(2,1)S(1)}, bf16[2,8,32,256]{3,2,1,0:T(8,128)(2,1)S(1)}, u32[]{:S(2)}, u32[]{:S(2)}) collective-permute-start(bf16[2,8,32,256]{3,2,1,0:T(8,128)(2,1)S(1)} %pad_maximum_fusion.4), channel_id=1, source_target_pairs={{0,3},{1,2},{2,1},{3,0},{4,7},{5,6},{6,5},{7,4},{8,11},{9,10},{10,... | collective-permute-start | bytes 786440 | tf_op jit(solution)/shard_map/ppermute | solution.py:373
  75.7 12.9 %collective-permute-start.6 = (bf16[4,8,32,256]{3,2,1,0:T(8,128)(2,1)S(1)}, bf16[4,8,32,256]{3,2,1,0:T(8,128)(2,1)S(1)}, u32[]{:S(2)}, u32[]{:S(2)}) collective-permute-start(bf16[4,8,32,256]{3,2,1,0:T(8,128)(2,1)S(1)} %pad_maximum_fusion.3), channel_id=1, source_target_pairs={{0,12},{1,13},{2,14},{3,15},{4,8},{5,9},{6,10},{7,11},{8,4},{9,5},... | collective-permute-start | bytes 1572872 | tf_op jit(solution)/shard_map/ppermute | solution.py:373
  77.0 13.8 %collective-permute-start.2 = (bf16[4,8,32,256]{3,2,1,0:T(8,128)(2,1)S(1)}, bf16[4,8,32,256]{3,2,1,0:T(8,128)(2,1)S(1)}, u32[]{:S(2)}, u32[]{:S(2)}) collective-permute-start(bf16[4,8,32,256]{3,2,1,0:T(8,128)(2,1)S(1)} %pad_maximum_fusion.2), channel_id=1, source_target_pairs={{0,4},{1,5},{2,6},{3,7},{4,0},{5,1},{6,2},{7,3},{8,12},{9,13},{10,... | collective-permute-start | bytes 1572872 | tf_op jit(solution)/shard_map/ppermute | solution.py:373
  88.7 14.9 %collective-permute-start.7 = (bf16[8,8,32,256]{3,2,1,0:T(8,128)(2,1)S(1)}, bf16[8,8,32,256]{3,2,1,0:T(8,128)(2,1)S(1)}, u32[]{:S(2)}, u32[]{:S(2)}) collective-permute-start(bf16[8,8,32,256]{3,2,1,0:T(8,128)(2,1)S(1)} %pad_maximum_fusion.1), channel_id=1, source_target_pairs={{0,4},{1,5},{2,6},{3,7},{4,0},{5,1},{6,2},{7,3},{8,12},{9,13},{10,... | collective-permute-start | bytes 3145736 | tf_op jit(solution)/shard_map/ppermute | solution.py:373
  90.9 16.3 %collective-permute-start.3 = (bf16[8,8,32,256]{3,2,1,0:T(8,128)(2,1)S(1)}, bf16[8,8,32,256]{3,2,1,0:T(8,128)(2,1)S(1)}, u32[]{:S(2)}, u32[]{:S(2)}) collective-permute-start(bf16[8,8,32,256]{3,2,1,0:T(8,128)(2,1)S(1)} %pad_maximum_fusion), channel_id=1, source_target_pairs={{0,12},{1,13},{2,14},{3,15},{4,8},{5,9},{6,10},{7,11},{8,4},{9,5},... | collective-permute-start | bytes 3145736 | tf_op jit(solution)/shard_map/ppermute | solution.py:373
  103.7 3.6 %copy-start.2 = (bf16[16,8,32,256]{3,2,1,0:T(8,128)(2,1)}, bf16[16,8,32,256]{3,2,1,0:T(8,128)(2,1)S(1)}, u32[]{:S(2)}) copy-start(bf16[16,8,32,256]{3,2,1,0:T(8,128)(2,1)S(1)} %constant_dynamic-update-slice_fusion.5.high_hbm) | copy-start | bytes 6291460
  107.3 1.4 copy-start.1
  132.0 15.8 %all-to-all-start.2 = ((bf16[16,24,1024]{2,1,0:T(8,128)(2,1)}), bf16[16,24,1024]{2,1,0:T(8,128)(2,1)S(1)}, u32[]{:S(2)}, u32[]{:S(2)}) async-start(bf16[16,24,1024]{2,1,0:T(8,128)(2,1)} %bitcast.15), calls=%async_computation.2 | async-start | bytes 1572864 | tf_op jit(solution)/shard_map/all_to_all | solution.py:455

commit v2 on v1

--- a/solution.py
+++ b/solution.py
@@ -11,6 +11,7 @@
 EPSILON = 1e-06
 MASKED = -1000000000.0
 SCALE = HEAD_DIM ** (-0.5)
+LOG2E = 1.4426950408889634
 BF16 = jnp.bfloat16
 F32 = jnp.float32
 VMEM_LIMIT = 56 * 1024 * 1024
@@ -85,41 +86,43 @@
     for copy, weight, result in zip(copies[:3], (wq, wk, wv), (q, k, v)):
         copy.wait()
 
-        @pl.loop(0, inner // 256)
-        def _(n):
-            cols = pl.ds(pl.multiple_of(n * 256, 256), 256)
-            result[:, cols] = dot(normed[...], weight[:, cols]).astype(BF16)
+        result[...] = dot(normed[...], weight[...]).astype(BF16)
 
     lane = lax.broadcasted_iota(jnp.int32, (1, BLOCK), 1)
-
-    @pl.loop(0, inner // HEAD_DIM)
-    def _(h):
-        cols = pl.ds(pl.multiple_of(h * HEAD_DIM, HEAD_DIM), HEAD_DIM)
+    mates, limits = [], []
+    for b in range(blocks):
+        mate, limit = jnp.int32(b), jnp.int32(0)
+        for other in (b - 1, b + 1):
+            if 0 <= other < blocks:
+                same = ids[other] == ids[b]
+                mate = jnp.where(same, other, mate)
+                limit = jnp.where(same, live[other], limit)
+        mates.append(mate)
+        limits.append(limit)
+    seen = [
+        jnp.concatenate(
+            [jnp.broadcast_to(lane < limit, (BLOCK, BLOCK)) for limit in (live[b], limits[b])], axis=1
+        )
+        for b in range(blocks)
+    ]
+    ones = jnp.ones((2 * BLOCK, HEAD_DIM), BF16)
+
+    for h in range(inner // HEAD_DIM):
+        cols = slice(h * HEAD_DIM, (h + 1) * HEAD_DIM)
         for b in range(blocks):
-            low, high = max(0, b - 1), min(blocks, b + 2)
             span = slice(b * BLOCK, (b + 1) * BLOCK)
-            keys = slice(low * BLOCK, high * BLOCK)
-            scores = dot_t(q[span, cols], k[keys, cols]) * SCALE
-            seen = jnp.concatenate(
-                [
-                    jnp.broadcast_to(lane < jnp.where(ids[o] == ids[b], live[o], 0), (BLOCK, BLOCK))
-                    for o in range(low, high)
-                ],
-                axis=1,
-            )
-            scores = jnp.where(seen, scores, MASKED)
+            mate = pl.ds(pl.multiple_of(mates[b] * BLOCK, BLOCK), BLOCK)
+            window = jnp.concatenate([k[span, cols], k[mate, cols]], axis=0)
+            scores = jnp.where(seen[b], dot_t(q[span, cols], window), MASKED)
             top = jnp.max(scores, axis=1, keepdims=True)
-            expo = jnp.exp(scores - top)
-            total = jnp.sum(expo, axis=1, keepdims=True)
-            mixed = dot(expo.astype(BF16), v[keys, cols])
-            context[span, cols] = (mixed / total).astype(BF16)
+            weights = jnp.exp2((scores - top) * (SCALE * LOG2E)).astype(BF16)
+            window = jnp.concatenate([v[span, cols], v[mate, cols]], axis=0)
+            mixed = dot(weights, jnp.concatenate([window, ones], axis=1))
+            context[span, cols] = (mixed[:, :HEAD_DIM] / mixed[:, HEAD_DIM:]).astype(BF16)
 
     copies[3].wait()
 
-    @pl.loop(0, width // 256)
-    def _(n):
-        cols = pl.ds(pl.multiple_of(n * 256, 256), 256)
-        out_ref[cols, :] = dot(context[...], wo[:, cols]).T.astype(BF16)
+    out_ref[...] = dot(context[...], wo[...]).astype(BF16).T
 
 
 def encoder(protein, length, residues, gain, wq, wk, wv, wo):
@@ -143,7 +146,19 @@
 
 
 def query_kernel(
-    state_ref, dec_gain_ref, final_gain_ref, id_row_ref, id_col_ref, wq_ref, wk_ref, out_ref, back_ref, id_ref
+    state_ref,
+    dec_gain_ref,
+    final_gain_ref,
+    gain_col_ref,
+    id_row_ref,
+    id_col_ref,
+    wq_ref,
+    wk_ref,
+    wv_ref,
+    out_ref,
+    back_ref,
+    id_ref,
+    gained_ref,
 ):
     rows = state_ref.shape[0]
     id_row = id_row_ref[...]
@@ -159,6 +174,7 @@
     id_ref[...] = jnp.sum(jnp.where(chosen, id_row.astype(F32), 0.0), axis=1, keepdims=True)
     normed = rms_scaled(state_ref[...].astype(F32), dec_gain_ref[...])
     normed = dot(chosen.astype(F32).astype(BF16), normed).astype(BF16)
+    gained_ref[...] = (wv_ref[...].astype(F32) * gain_col_ref[...]).astype(BF16)
     gain = final_gain_ref[...]
     for pair in range(wq_ref.shape[1] // 256):
         queries = dot(normed, wq_ref[:, pair * 256 : (pair + 1) * 256]).astype(BF16)
@@ -169,7 +185,7 @@
             out_ref[h] = (back * gain).astype(BF16)
 
 
-def query_side(states, dec_gain, final_gain, ids, wq, wk):
+def query_side(states, dec_gain, final_gain, ids, wq, wk, wv):
     rows, width = states.shape
     inner = wq.shape[1]
     heads = inner // HEAD_DIM
@@ -179,15 +195,26 @@
             jax.ShapeDtypeStruct((heads, rows, width), BF16),
             jax.ShapeDtypeStruct((rows, rows), BF16),
             jax.ShapeDtypeStruct((rows, 1), F32),
+            jax.ShapeDtypeStruct((width, inner), BF16),
         ),
-        in_specs=[VMEM] * 7,
-        out_specs=(VMEM,) * 3,
+        in_specs=[VMEM] * 9,
+        out_specs=(VMEM,) * 4,
         compiler_params=pltpu.CompilerParams(vmem_limit_bytes=VMEM_LIMIT),
         cost_estimate=pl.CostEstimate(
             flops=4 * rows * width * inner, bytes_accessed=4 * width * inner + 2 * heads * rows * width, transcendentals=0
         ),
         name="query_side",
-    )(states, dec_gain, final_gain, ids.reshape(1, rows), ids.reshape(rows, 1), wq, wk)
+    )(
+        states,
+        dec_gain.reshape(1, width),
+        final_gain.reshape(1, width),
+        final_gain.reshape(width, 1),
+        ids.reshape(1, rows),
+        ids.reshape(rows, 1),
+        wq,
+        wk,
+        wv,
+    )
 
 
 def placing_kernel(protein_ref, length_ref, group_ref, arrived_ref, own_ref, encoded_ref, placed_ref):
@@ -242,6 +269,7 @@
 
 
 ROW_TILE = 32
+TOGETHER = 4
 
 
 def cross_kernel(
@@ -250,10 +278,11 @@
     query_ref,
     id_ref,
     key_id_ref,
-    gain_ref,
     back_ref,
-    low_hbm,
-    high_hbm,
+    low_ref,
+    low_far_ref,
+    high_ref,
+    high_far_ref,
     wv_hbm,
     wo_hbm,
     out_ref,
@@ -263,20 +292,22 @@
     context,
     wv,
     wo,
+    item_group,
+    item_tile,
     key_sem,
     weight_sems,
 ):
     heads, rows, width = query_ref.shape
     groups, _, span = keys.shape
-    chunks, _, part, _ = low_hbm.shape
+    chunks, _, part, _ = low_ref.shape
     weight_copies = [
         pltpu.make_async_copy(wv_hbm, wv, weight_sems.at[0]),
         pltpu.make_async_copy(wo_hbm, wo, weight_sems.at[1]),
     ]
     key_copies = []
-    for half, source in enumerate((low_hbm, high_hbm)):
+    for piece, source in enumerate((low_ref, low_far_ref, high_ref, high_far_ref)):
         for j in range(chunks):
-            at = pl.multiple_of(origin_ref[half * chunks + j] * (2 * part) + half * part, part)
+            at = pl.multiple_of(origin_ref[piece * chunks + j] * (2 * part) + piece // 2 * part, part)
             key_copies.append(pltpu.make_async_copy(source.at[j], keys.at[:, pl.ds(at, part), :], key_sem))
     for copy in key_copies:
         copy.start()
@@ -294,57 +325,67 @@
         total = jnp.sum(squares, axis=0, keepdims=True)
         key_scale[e] = lax.rsqrt(total / width + EPSILON)
 
-    gain = gain_ref[...]
     flat = heads * ROW_TILE
 
-    @pl.loop(0, groups)
-    def _(e):
+    def listed(e, count):
         first = start_ref[e] // ROW_TILE
-        last = (start_ref[e + 1] + ROW_TILE - 1) // ROW_TILE
-
-        @pl.when(start_ref[e + 1] > start_ref[e])
-        def _():
-            @pl.loop(first, last)
-            def _(i):
-                at = pl.ds(pl.multiple_of(i * ROW_TILE, ROW_TILE), ROW_TILE)
-                ids = id_ref[at, :]
-                scale = key_scale[e]
-                seen = ids == key_id_ref[e]
-                mine = (ids >= (e * 4).astype(F32)) & (ids < (e * 4 + 4).astype(F32))
-                scores = dot(query_ref[:, at, :].reshape(flat, width), keys[e]) * (scale * SCALE)
-                scores = jnp.where(seen[None], scores.reshape(heads, ROW_TILE, span), MASKED)
-                top = jnp.max(scores, axis=2, keepdims=True)
-                expo = jnp.exp(scores - top)
-                total = jnp.sum(expo, axis=2, keepdims=True)
-                weights = (expo * scale[None]).astype(BF16).reshape(flat, span)
-                spread = dot_t(weights, keys[e]).reshape(heads, ROW_TILE, width)
-                spread = (spread * (1.0 / total) * gain[None]).astype(BF16)
-                mixed[:, at, :] = jnp.where(mine[None], spread, mixed[:, at, :])
+        last = jnp.where(start_ref[e + 1] > start_ref[e], (start_ref[e + 1] + ROW_TILE - 1) // ROW_TILE, first)
+
+        def note(i, at):
+            item_group[at] = e
+            item_tile[at] = i
+            return at + 1
+
+        return lax.fori_loop(first, last, note, count)
+
+    items = lax.fori_loop(0, groups, listed, jnp.int32(0))
+    for extra in range(TOGETHER - 1):
+        item_group[items + extra] = item_group[items - 1]
+        item_tile[items + extra] = item_tile[items - 1]
+
+    @pl.loop(0, (items + TOGETHER - 1) // TOGETHER)
+    def _(n):
+        todo = [(item_group[n * TOGETHER + a], item_tile[n * TOGETHER + a]) for a in range(TOGETHER)]
+        spots = [pl.ds(pl.multiple_of(i * ROW_TILE, ROW_TILE), ROW_TILE) for _, i in todo]
+        scores = [
+            dot(query_ref[:, at, :].reshape(flat, width), keys[e]) for (e, _), at in zip(todo, spots)
+        ]
+        weights = []
+        for (e, _), at, raw in zip(todo, spots, scores):
+            scale = key_scale[e]
+            seen = id_ref[at, :] == key_id_ref[e]
+            raw = (raw * (scale * (SCALE * LOG2E))).reshape(heads, ROW_TILE, span)
+            raw = jnp.where(seen[None], raw, MASKED)
+            expo = jnp.exp2(raw - jnp.max(raw, axis=2, keepdims=True))
+            share = 1.0 / jnp.sum(expo, axis=2, keepdims=True)
+            weights.append((expo * scale[None] * share).astype(BF16).reshape(flat, span))
+        spreads = [dot_t(w, keys[e]) for w, (e, _) in zip(weights, todo)]
+        for (e, _), at, spread in zip(todo, spots, spreads):
+            ids = id_ref[at, :]
+            mine = (ids >= (e * 4).astype(F32)) & (ids < (e * 4 + 4).astype(F32))
+            spread = spread.astype(BF16).reshape(heads, ROW_TILE, width)
+            mixed[:, at, :] = jnp.where(mine[None], spread, mixed[:, at, :])
 
     for copy in weight_copies:
         copy.wait()
 
-    @pl.loop(0, heads)
-    def _(h):
-        cols = pl.ds(pl.multiple_of(h * HEAD_DIM, HEAD_DIM), HEAD_DIM)
+    for h in range(heads):
+        cols = slice(h * HEAD_DIM, (h + 1) * HEAD_DIM)
         context[:, cols] = dot(mixed[h], wv[:, cols]).astype(BF16)
 
     context[...] = dot(back_ref[...], context[...]).astype(BF16)
 
-    @pl.loop(0, width // 256)
-    def _(n):
-        cols = pl.ds(pl.multiple_of(n * 256, 256), 256)
-        out_ref[:, cols] = dot(context[...], wo[:, cols]).astype(BF16)
-
-
-def cross(starts, origins, queries, ids, key_ids, gain, back, low, high, wv, wo):
+    out_ref[...] = dot(context[...], wo[...]).astype(BF16)
+
+
+def cross(starts, origins, queries, ids, key_ids, back, pieces, wv, wo):
     heads, rows, width = queries.shape
     groups, span = key_ids.shape[0], key_ids.shape[2]
     inner = wv.shape[1]
     return pl.pallas_call(
         cross_kernel,
         out_shape=jax.ShapeDtypeStruct((rows, width), BF16),
-        in_specs=[SMEM, SMEM] + [VMEM] * 5 + [ANY] * 4,
+        in_specs=[SMEM, SMEM] + [VMEM] * 8 + [ANY] * 2,
         out_specs=VMEM,
         scratch_shapes=[
             pltpu.VMEM((groups, width, span), BF16),
@@ -353,6 +394,8 @@
             pltpu.VMEM((rows, inner), BF16),
             pltpu.VMEM((width, inner), BF16),
             pltpu.VMEM((inner, width), BF16),
+            pltpu.SMEM((rows // ROW_TILE + groups + TOGETHER,), jnp.int32),
+            pltpu.SMEM((rows // ROW_TILE + groups + TOGETHER,), jnp.int32),
             pltpu.SemaphoreType.DMA,
             pltpu.SemaphoreType.DMA((2,)),
         ],
@@ -361,7 +404,7 @@
             flops=8 * rows * width * inner, bytes_accessed=2 * groups * width * span, transcendentals=rows * span * heads
         ),
         name="cross",
-    )(starts, origins, queries, ids, key_ids, gain, back, low, high, wv, wo)
+    )(starts, origins, queries, ids, key_ids, back, *pieces, wv, wo)
 
 
 def exchange(x, groups, tensor, half, step):
@@ -375,10 +418,11 @@
 
 def gathered(low, high, groups, tensor):
     halves = [low[None], high[None]]
-    for step in range(4):
+    for step in range(3):
         got = [exchange(halves[h], groups, tensor, h, step) for h in range(2)]
         halves = [jnp.concatenate([halves[h], got[h]], axis=0) for h in range(2)]
-    return halves
+    got = [exchange(halves[h], groups, tensor, h, 3) for h in range(2)]
+    return halves[0], got[0], halves[1], got[1]
 
 
 def origin_masks():
@@ -426,38 +470,29 @@
     arrived = lax.all_to_all(
         partial_sums.reshape(tensor, slice_width, rows), "tensor", split_axis=0, concat_axis=0, tiled=True
     )
-    queries, back, sorted_ids = query_side(
-        decoder_states, dec_gain.reshape(1, width), final_gain.reshape(1, width), query_protein, cross_query, cross_key
+    queries, back, sorted_ids, gained_value = query_side(
+        decoder_states, dec_gain, final_gain, query_protein, cross_query, cross_key, cross_value
     )
     bounds = 4 * jnp.arange(groups + 1, dtype=jnp.int32)
     starts = jnp.sum((query_protein[None, :] < bounds[:, None]).astype(jnp.int32), axis=1)
     masks = origin_masks()
     origins = tensor_index.astype(jnp.int32) ^ jnp.where(dp_index % 2 == 0, masks[0], masks[1])
     own = lax.dynamic_slice_in_dim(residues, tensor_index * slice_width, slice_width, 1).T
+    share = query_rows // tensor
+    own_rows = lax.dynamic_slice_in_dim(decoder_states, tensor_index * share, share, 0).astype(F32)
+    arrived, own, own_rows, queries, back, sorted_ids, gained_value, starts, origins = lax.optimization_barrier(
+        (arrived, own, own_rows, queries, back, sorted_ids, gained_value, starts, origins)
+    )
     encoded, placed = placing(block_protein, protein_length, decoder_group, arrived, own, groups)
     received = lax.all_to_all(placed, "dp", split_axis=0, concat_axis=0, tiled=True)
-    low, high = gathered(received[:, :part], received[:, part : 2 * part], groups, tensor)
+    pieces = gathered(received[:, :part], received[:, part : 2 * part], groups, tensor)
     key_ids = received[:, slice_width : slice_width + 1].astype(F32)
-    outcome = cross(
-        starts,
-        origins,
-        queries,
-        sorted_ids,
-        key_ids,
-        final_gain.reshape(1, width),
-        back,
-        low,
-        high,
-        cross_value,
-        cross_out,
-    )
-    share = query_rows // tensor
+    outcome = cross(starts, origins, queries, sorted_ids, key_ids, back, pieces, gained_value, cross_out)
     mixed = lax.all_to_all(
         outcome.reshape(tensor, share, width), "tensor", split_axis=0, concat_axis=0, tiled=True
     )
     mixed = mixed.astype(F32).sum(axis=0)
-    own_rows = lax.dynamic_slice_in_dim(decoder_states, tensor_index * share, share, 0)
-    decoded = (own_rows.astype(F32) + mixed).astype(BF16)
+    decoded = (own_rows + mixed).astype(BF16)
     return (encoded.T, decoded)
 
 

time: 152 us -> 130 us (0.86); the launches traced: 149 us -> 129 us
  waiting for transfers between devices: 51.1 us -> 25.8 us
  blocking collectives: 13.6 us -> 30.6 us
  Pallas kernels: 55.4 us -> 40.7 us
  starting transfers between devices: 18.6 us -> 21.5 us
    all_to_all x0 -> x1, blocking collectives: none -> 17.1 us  [body(): lax.all_to_all(outcome.reshape(tensor, share, width), 'tensor', split_axi...]
    all_to_all x1, waiting for transfers between devices: 15.9 us -> 1.11 us  [body(): lax.all_to_all(partial_sums.reshape(tensor, slice_width, rows), 'tensor',...]
    all_to_all x1 -> x0, waiting for transfers between devices: 11.6 us -> none  [body(): lax.all_to_all(outcome.reshape(tensor, share, width), 'tensor', split_axi...]
    pallas_call x1, Pallas kernels: 20.5 us -> 10.4 us  [encoder(): pl.pallas_call(encoder_kernel, out_shape=jax.ShapeDtypeStruct((width, row...]
    ppermute x8, starting transfers between devices: 7.24 us -> 14.3 us  [exchange(): return lax.ppermute(x, ('dp', 'tensor'), pairs)]
    pallas_call x1, Pallas kernels: 23.3 us -> 17.7 us  [cross(): pl.pallas_call(cross_kernel, out_shape=jax.ShapeDtypeStruct((rows, width)...]
    all_to_all x1 -> x0, starting transfers between devices: 4.24 us -> none  [body(): lax.all_to_all(outcome.reshape(tensor, share, width), 'tensor', split_axi...]
    reshape x0 -> x2, local copies, waits for them, and re-layouts: none -> 1.6 us  [the longest x1 1.04 us: query_side(): final_gain.reshape(width, 1)]
  transfers between devices with their start and end apart: 10 -> 9, of which waited for: 7 -> 8; matrix products, arithmetic and copies ran while one was open for 4% -> 5% of each run, Pallas kernels for 6% -> 8%
where the time goes in v2:
time: 130 us; the launch traced here: 129 us
  Pallas kernels  40.7 us (31%)
  blocking collectives  30.6 us (24%)
  waiting for transfers between devices  25.8 us (20%)
  starting transfers between devices  21.5 us (17%)
  local copies, waits for them, and re-layouts  6.23 us (5%)
  other arithmetic  3.75 us (3%)
    ppermute x8, waiting for transfers between devices, exchange(): return lax.ppermute(x, ('dp', 'tensor'), pairs)  24.7 us
    pallas_call x1, Pallas kernels, cross(): pl.pallas_call(cross_kernel, out_shape=jax.ShapeDtypeStruct((rows, width)...  17.7 us
    all_to_all x1, blocking collectives, body(): lax.all_to_all(outcome.reshape(tensor, share, width), 'tensor', split_axi...  17.1 us
    ppermute x8, starting transfers between devices, exchange(): return lax.ppermute(x, ('dp', 'tensor'), pairs)  14.3 us
    all_to_all x1, blocking collectives, body(): lax.all_to_all(placed, 'dp', split_axis=0, concat_axis=0, tiled=True)  13.5 us
    pallas_call x1, Pallas kernels, encoder(): pl.pallas_call(encoder_kernel, out_shape=jax.ShapeDtypeStruct((width, row...  10.4 us
    pallas_call x1, Pallas kernels, query_side(): pl.pallas_call(query_kernel, out_shape=(jax.ShapeDtypeStruct((heads, rows...  10.4 us
    all_to_all x1, starting transfers between devices, body(): lax.all_to_all(partial_sums.reshape(tensor, slice_width, rows), 'tensor',...  7.16 us
  transfers between devices with their start and end apart: 9, of which 8 were waited for; matrix products, arithmetic and copies ran while one was open for 5% of the time, Pallas kernels for 8%

profile of v2, /device:TPU:0, one launch (start us, length us, event | category | flops | bytes accessed | tf_op | source)
XLA Modules:
  0.0 129.4 jit_solution(220513215852221420)
XLA Ops:
  0.6 10.4 %encoder.1 = bf16[1024,512]{1,0:T(8,128)(2,1)} custom-call(s32[4]{0:T(128)} %protein_ref.3, s32[32]{0:T(128)} %length_ref.3, bf16[512,1024]{1,0:T(8,128)(2,1)} %residue_ref.1, f32[1,1024]{1,0:T(1,128)} %bitcast.19, bf16[1024,1024]{1,0:T(8,128)(2,1)} %wq_hbm.1, bf16[1024,1024]{1,0:T(8,128)(2,1)} %wk_hbm.1, bf16[1024,1024]{1,0:T(8,128)(2,1)} %wv_hbm.1, ...), custom_call_target="tpu_custom_call" | custom-call | flops 4294967296 | bytes 8388608 | tf_op jit(solution)/shard_map/encoder/pallas_call | solution.py:131
  11.0 0.0 copy-start.5
  11.1 0.0 copy-start.6
  11.1 7.2 %all-to-all-start = ((bf16[16,64,512]{2,1,0:T(8,128)(2,1)}), bf16[16,64,512]{2,1,0:T(8,128)(2,1)S(1)}, u32[]{:S(2)}, u32[]{:S(2)}) async-start(bf16[16,64,512]{2,1,0:T(8,128)(2,1)} %bitcast.13), calls=%async_computation | async-start | bytes 2097152 | tf_op jit(solution)/shard_map/all_to_all | solution.py:470
  18.2 0.0 copy-done.5
  18.3 0.6 reshape.38.id_row_ref
  18.8 0.8 reshape.41.id_col_ref
  19.6 1.0 constant_dynamic-slice_fusion
  20.6 0.7 copy.28
  21.3 1.0 copy.26.gain_col_ref
  22.4 0.7 convert_reduce_fusion.1.start_ref
  23.1 0.8 dynamic-slice_convert_fusion
  23.9 0.0 copy-start.8
  23.9 10.4 %query_side.1 = (bf16[8,384,1024]{2,1,0:T(8,128)(2,1)}, bf16[384,384]{1,0:T(8,128)(2,1)}, f32[384,1]{1,0:T(8,128)}, bf16[1024,1024]{1,0:T(8,128)(2,1)}) custom-call(bf16[384,1024]{1,0:T(8,128)(2,1)} %state_ref.1, f32[1,1024]{1,0:T(1,128)} %bitcast.17, f32[1,1024]{1,0:T(1,128)} %bitcast.15, f32[1024,1]{1,0:T(8,128)} %copy.26.gain_col_ref, ...), custom_call_target="tpu_custom_call" | custom-call | flops 1610612736 | bytes 10485760 | tf_op jit(solution)/shard_map/query_side/pallas_call | solution.py:192
  34.2 0.0 copy-done.7
  34.2 0.0 copy-done.8
  34.3 0.5 fusion.origin_ref
  34.8 1.1 all-to-all-done.arrived_ref
  35.9 1.1 copy-done.2
  37.0 2.2 %placing.1 = (bf16[64,512]{1,0:T(8,128)(2,1)}, bf16[8,80,256]{2,1,0:T(8,128)(2,1)}) custom-call(s32[4]{0:T(128)} %protein_ref.3, s32[32]{0:T(128)} %length_ref.3, s32[32]{0:T(128)} %group_ref.1, bf16[16,64,512]{2,1,0:T(8,128)(2,1)} %copy-done.2, bf16[64,512]{1,0:T(8,128)(2,1)} %bitcast.14), custom_call_target="tpu_custom_call" | custom-call | tf_op jit(solution)/shard_map/placing/pallas_call | solution.py:258
  39.2 13.5 %all_to_all.15 = bf16[8,80,256]{2,1,0:T(8,128)(2,1)S(1)} all-to-all(bf16[8,80,256]{2,1,0:T(8,128)(2,1)} %get-tuple-element.29), channel_id=1, replica_groups=mesh['dp'=8,'tensor'=16] {'dp'}, dimensions={0} | all-to-all | bytes 655360 | tf_op jit(solution)/shard_map/all_to_all | solution.py:487
  52.8 0.9 collective-permute-start
  53.6 2.1 %collective-permute-start.4 = (bf16[1,8,32,256]{3,2,1,0:T(8,128)(2,1)S(1)}, bf16[1,8,32,256]{3,2,1,0:T(8,128)(2,1)S(1)}, u32[]{:S(2)}, u32[]{:S(2)}) collective-permute-start(bf16[1,8,32,256]{3,2,1,0:T(8,128)(2,1)S(1)} %get-tuple-element.32), channel_id=1, source_target_pairs={{0,3},{1,2},{2,1},{3,0},{4,7},{5,6},{6,5},{7,4},{8,11},{9,10},{10,... | collective-permute-start | bytes 393224 | tf_op jit(solution)/shard_map/ppermute | solution.py:416
  55.7 2.1 %collective-permute-done = bf16[1,8,32,256]{3,2,1,0:T(8,128)(2,1)S(1)} collective-permute-done((bf16[1,8,32,256]{3,2,1,0:T(8,128)(2,1)S(1)}, bf16[1,8,32,256]{3,2,1,0:T(8,128)(2,1)S(1)}, u32[]{:S(2)}, u32[]{:S(2)}) %collective-permute-start) | collective-permute-done | bytes 131104 | tf_op jit(solution)/shard_map/ppermute | solution.py:416
  57.8 2.1 %collective-permute-start.1 = (bf16[2,8,32,256]{3,2,1,0:T(8,128)(2,1)S(1)}, bf16[2,8,32,256]{3,2,1,0:T(8,128)(2,1)S(1)}, u32[]{:S(2)}, u32[]{:S(2)}) collective-permute-start(bf16[2,8,32,256]{3,2,1,0:T(8,128)(2,1)S(1)} %pad_maximum_fusion.4), channel_id=1, source_target_pairs={{0,3},{1,2},{2,1},{3,0},{4,7},{5,6},{6,5},{7,4},{8,11},{9,10},{10,... | collective-permute-start | bytes 786440 | tf_op jit(solution)/shard_map/ppermute | solution.py:416
  59.9 0.0 collective-permute-done.4
  60.0 0.5 collective-permute-start.5
  60.5 5.0 %collective-permute-done.1 = bf16[2,8,32,256]{3,2,1,0:T(8,128)(2,1)S(1)} collective-permute-done((bf16[2,8,32,256]{3,2,1,0:T(8,128)(2,1)S(1)}, bf16[2,8,32,256]{3,2,1,0:T(8,128)(2,1)S(1)}, u32[]{:S(2)}, u32[]{:S(2)}) %collective-permute-start.1) | collective-permute-done | bytes 262176 | tf_op jit(solution)/shard_map/ppermute | solution.py:416
  65.5 0.1 pad_maximum_fusion.2
  65.5 0.9 collective-permute-start.2
  66.4 0.5 collective-permute-done.5
  66.9 0.1 pad_maximum_fusion.3
  67.0 3.4 %collective-permute-start.6 = (bf16[4,8,32,256]{3,2,1,0:T(8,128)(2,1)S(1)}, bf16[4,8,32,256]{3,2,1,0:T(8,128)(2,1)S(1)}, u32[]{:S(2)}, u32[]{:S(2)}) collective-permute-start(bf16[4,8,32,256]{3,2,1,0:T(8,128)(2,1)S(1)} %pad_maximum_fusion.3), channel_id=1, source_target_pairs={{0,12},{1,13},{2,14},{3,15},{4,8},{5,9},{6,10},{7,11},{8,4},{9,5},... | collective-permute-start | bytes 1572872 | tf_op jit(solution)/shard_map/ppermute | solution.py:416
  70.4 4.4 %collective-permute-done.2 = bf16[4,8,32,256]{3,2,1,0:T(8,128)(2,1)S(1)} collective-permute-done((bf16[4,8,32,256]{3,2,1,0:T(8,128)(2,1)S(1)}, bf16[4,8,32,256]{3,2,1,0:T(8,128)(2,1)S(1)}, u32[]{:S(2)}, u32[]{:S(2)}) %collective-permute-start.2) | collective-permute-done | bytes 524320 | tf_op jit(solution)/shard_map/ppermute | solution.py:416
  74.8 0.1 pad_maximum_fusion.low_ref
  74.9 2.1 %collective-permute-start.3 = (bf16[8,8,32,256]{3,2,1,0:T(8,128)(2,1)S(1)}, bf16[8,8,32,256]{3,2,1,0:T(8,128)(2,1)S(1)}, u32[]{:S(2)}, u32[]{:S(2)}) collective-permute-start(bf16[8,8,32,256]{3,2,1,0:T(8,128)(2,1)S(1)} %pad_maximum_fusion.low_ref), channel_id=1, source_target_pairs={{0,12},{1,13},{2,14},{3,15},{4,8},{5,9},{6,10},{7,11},{8,4},{9,5},... | collective-permute-start | bytes 3145736 | tf_op jit(solution)/shard_map/ppermute | solution.py:416
  77.0 0.5 collective-permute-done.6
  77.5 0.1 pad_maximum_fusion.1.high_ref
  77.7 2.4 %collective-permute-start.7 = (bf16[8,8,32,256]{3,2,1,0:T(8,128)(2,1)S(1)}, bf16[8,8,32,256]{3,2,1,0:T(8,128)(2,1)S(1)}, u32[]{:S(2)}, u32[]{:S(2)}) collective-permute-start(bf16[8,8,32,256]{3,2,1,0:T(8,128)(2,1)S(1)} %pad_maximum_fusion.1.high_ref), channel_id=1, source_target_pairs={{0,4},{1,5},{2,6},{3,7},{4,0},{5,1},{6,2},{7,3},{8,12},{9,13},{10,... | collective-permute-start | bytes 3145736 | tf_op jit(solution)/shard_map/ppermute | solution.py:416
  80.0 0.6 slice_convert_fusion.key_id_ref
  80.6 10.4 %collective-permute-done.3.low_far_ref = bf16[8,8,32,256]{3,2,1,0:T(8,128)(2,1)S(1)} collective-permute-done((bf16[8,8,32,256]{3,2,1,0:T(8,128)(2,1)S(1)}, bf16[8,8,32,256]{3,2,1,0:T(8,128)(2,1)S(1)}, u32[]{:S(2)}, u32[]{:S(2)}) %collective-permute-start.3) | collective-permute-done | bytes 1048608 | tf_op jit(solution)/shard_map/ppermute | solution.py:416
  91.0 1.8 %collective-permute-done.7.high_far_ref = bf16[8,8,32,256]{3,2,1,0:T(8,128)(2,1)S(1)} collective-permute-done((bf16[8,8,32,256]{3,2,1,0:T(8,128)(2,1)S(1)}, bf16[8,8,32,256]{3,2,1,0:T(8,128)(2,1)S(1)}, u32[]{:S(2)}, u32[]{:S(2)}) %collective-permute-start.7) | collective-permute-done | bytes 1048608 | tf_op jit(solution)/shard_map/ppermute | solution.py:416
  92.8 0.0 copy-done
  92.8 1.0 copy-done.4
  93.8 17.7 %cross.1 = bf16[384,1024]{1,0:T(8,128)(2,1)} custom-call(s32[9]{0:T(128)} %convert_reduce_fusion.1.start_ref, s32[32]{0:T(128)} %fusion.origin_ref, bf16[8,384,1024]{2,1,0:T(8,128)(2,1)} %get-tuple-element.27.query_ref, f32[384,1]{1,0:T(8,128)} %get-tuple-element.28.id_ref, f32[8,1,256]{2,1,0:T(1,128)} %slice_convert_fusion.key_id_ref, ...), custom_call_target="tpu_custom_call" | custom-call | flops 3221225472 | bytes 4194304 | tf_op jit(solution)/shard_map/cross/pallas_call | solution.py:385
  111.6 17.1 %all_to_all.16 = bf16[16,24,1024]{2,1,0:T(8,128)(2,1)S(1)} all-to-all(bf16[16,24,1024]{2,1,0:T(8,128)(2,1)} %bitcast.12), channel_id=1, replica_groups=mesh['dp'=8,'tensor'=16] {'tensor'}, dimensions={0} | all-to-all | bytes 1572864 | tf_op jit(solution)/shard_map/all_to_all | solution.py:491
  128.7 0.1 convert_reduce_fusion
  128.8 0.6 add_convert_fusion
  (13 shorter events, 0.1 us)
Async XLA Ops:
  11.0 7.2 %copy-start.5 = (s32[384]{0:T(512)S(1)}, s32[384]{0:T(512)}, u32[]{:S(2)}) copy-start(s32[384]{0:T(512)} %param.29) | copy-start | bytes 4612
  11.1 10.3 %copy-start.6 = (f32[1024]{0:T(1024)S(1)}, f32[1024]{0:T(1024)}, u32[]{:S(2)}) copy-start(f32[1024]{0:T(1024)} %param.31) | copy-start | bytes 12292
  11.1 24.8 %all-to-all-start = ((bf16[16,64,512]{2,1,0:T(8,128)(2,1)}), bf16[16,64,512]{2,1,0:T(8,128)(2,1)S(1)}, u32[]{:S(2)}, u32[]{:S(2)}) async-start(bf16[16,64,512]{2,1,0:T(8,128)(2,1)} %bitcast.13), calls=%async_computation | async-start | bytes 2097152 | tf_op jit(solution)/shard_map/all_to_all | solution.py:470
  23.9 10.4 %copy-start.7 = (s32[32]{0:T(128)S(1)}, s32[32]{0:T(128)}, u32[]{:S(2)}) copy-start(s32[32]{0:T(128)} %constant.40.clone) | copy-start | bytes 388
  23.9 10.4 %copy-start.8 = (s32[32]{0:T(128)S(1)}, s32[32]{0:T(128)}, u32[]{:S(2)}) copy-start(s32[32]{0:T(128)} %constant.39.clone) | copy-start | bytes 388
  35.9 1.1 copy-start.2
  52.8 5.0 %collective-permute-start = (bf16[1,8,32,256]{3,2,1,0:T(8,128)(2,1)S(1)}, bf16[1,8,32,256]{3,2,1,0:T(8,128)(2,1)S(1)}, u32[]{:S(2)}, u32[]{:S(2)}) collective-permute-start(bf16[1,8,32,256]{3,2,1,0:T(8,128)(2,1)S(1)} %get-tuple-element.33), channel_id=1, source_target_pairs={{0,1},{1,0},{2,3},{3,2},{4,5},{5,4},{6,7},{7,6},{8,9},{9,8},{10,11... | collective-permute-start | bytes 393224 | tf_op jit(solution)/shard_map/ppermute | solution.py:416
  53.6 6.3 %collective-permute-start.4 = (bf16[1,8,32,256]{3,2,1,0:T(8,128)(2,1)S(1)}, bf16[1,8,32,256]{3,2,1,0:T(8,128)(2,1)S(1)}, u32[]{:S(2)}, u32[]{:S(2)}) collective-permute-start(bf16[1,8,32,256]{3,2,1,0:T(8,128)(2,1)S(1)} %get-tuple-element.32), channel_id=1, source_target_pairs={{0,3},{1,2},{2,1},{3,0},{4,7},{5,6},{6,5},{7,4},{8,11},{9,10},{10,... | collective-permute-start | bytes 393224 | tf_op jit(solution)/shard_map/ppermute | solution.py:416
  57.8 7.7 %collective-permute-start.1 = (bf16[2,8,32,256]{3,2,1,0:T(8,128)(2,1)S(1)}, bf16[2,8,32,256]{3,2,1,0:T(8,128)(2,1)S(1)}, u32[]{:S(2)}, u32[]{:S(2)}) collective-permute-start(bf16[2,8,32,256]{3,2,1,0:T(8,128)(2,1)S(1)} %pad_maximum_fusion.4), channel_id=1, source_target_pairs={{0,3},{1,2},{2,1},{3,0},{4,7},{5,6},{6,5},{7,4},{8,11},{9,10},{10,... | collective-permute-start | bytes 786440 | tf_op jit(solution)/shard_map/ppermute | solution.py:416
  60.0 6.9 %collective-permute-start.5 = (bf16[2,8,32,256]{3,2,1,0:T(8,128)(2,1)S(1)}, bf16[2,8,32,256]{3,2,1,0:T(8,128)(2,1)S(1)}, u32[]{:S(2)}, u32[]{:S(2)}) collective-permute-start(bf16[2,8,32,256]{3,2,1,0:T(8,128)(2,1)S(1)} %pad_maximum_fusion.5), channel_id=1, source_target_pairs={{0,1},{1,0},{2,3},{3,2},{4,5},{5,4},{6,7},{7,6},{8,9},{9,8},{10,11... | collective-permute-start | bytes 786440 | tf_op jit(solution)/shard_map/ppermute | solution.py:416
  65.5 9.3 %collective-permute-start.2 = (bf16[4,8,32,256]{3,2,1,0:T(8,128)(2,1)S(1)}, bf16[4,8,32,256]{3,2,1,0:T(8,128)(2,1)S(1)}, u32[]{:S(2)}, u32[]{:S(2)}) collective-permute-start(bf16[4,8,32,256]{3,2,1,0:T(8,128)(2,1)S(1)} %pad_maximum_fusion.2), channel_id=1, source_target_pairs={{0,4},{1,5},{2,6},{3,7},{4,0},{5,1},{6,2},{7,3},{8,12},{9,13},{10,... | collective-permute-start | bytes 1572872 | tf_op jit(solution)/shard_map/ppermute | solution.py:416
  67.0 10.6 %collective-permute-start.6 = (bf16[4,8,32,256]{3,2,1,0:T(8,128)(2,1)S(1)}, bf16[4,8,32,256]{3,2,1,0:T(8,128)(2,1)S(1)}, u32[]{:S(2)}, u32[]{:S(2)}) collective-permute-start(bf16[4,8,32,256]{3,2,1,0:T(8,128)(2,1)S(1)} %pad_maximum_fusion.3), channel_id=1, source_target_pairs={{0,12},{1,13},{2,14},{3,15},{4,8},{5,9},{6,10},{7,11},{8,4},{9,5},... | collective-permute-start | bytes 1572872 | tf_op jit(solution)/shard_map/ppermute | solution.py:416
  74.9 17.9 %copy-start = (bf16[8,8,32,256]{3,2,1,0:T(8,128)(2,1)}, bf16[8,8,32,256]{3,2,1,0:T(8,128)(2,1)S(1)}, u32[]{:S(2)}) copy-start(bf16[8,8,32,256]{3,2,1,0:T(8,128)(2,1)S(1)} %pad_maximum_fusion.low_ref) | copy-start | bytes 3145732
  74.9 16.1 %collective-permute-start.3 = (bf16[8,8,32,256]{3,2,1,0:T(8,128)(2,1)S(1)}, bf16[8,8,32,256]{3,2,1,0:T(8,128)(2,1)S(1)}, u32[]{:S(2)}, u32[]{:S(2)}) collective-permute-start(bf16[8,8,32,256]{3,2,1,0:T(8,128)(2,1)S(1)} %pad_maximum_fusion.low_ref), channel_id=1, source_target_pairs={{0,12},{1,13},{2,14},{3,15},{4,8},{5,9},{6,10},{7,11},{8,4},{9,5},... | collective-permute-start | bytes 3145736 | tf_op jit(solution)/shard_map/ppermute | solution.py:416
  77.6 15.2 %copy-start.1 = (bf16[8,8,32,256]{3,2,1,0:T(8,128)(2,1)}, bf16[8,8,32,256]{3,2,1,0:T(8,128)(2,1)S(1)}, u32[]{:S(2)}) copy-start(bf16[8,8,32,256]{3,2,1,0:T(8,128)(2,1)S(1)} %pad_maximum_fusion.1.high_ref) | copy-start | bytes 3145732
  77.7 15.2 %collective-permute-start.7 = (bf16[8,8,32,256]{3,2,1,0:T(8,128)(2,1)S(1)}, bf16[8,8,32,256]{3,2,1,0:T(8,128)(2,1)S(1)}, u32[]{:S(2)}, u32[]{:S(2)}) collective-permute-start(bf16[8,8,32,256]{3,2,1,0:T(8,128)(2,1)S(1)} %pad_maximum_fusion.1.high_ref), channel_id=1, source_target_pairs={{0,4},{1,5},{2,6},{3,7},{4,0},{5,1},{6,2},{7,3},{8,12},{9,13},{10,... | collective-permute-start | bytes 3145736 | tf_op jit(solution)/shard_map/ppermute | solution.py:416
  91.0 1.8 %copy-start.3 = (bf16[8,8,32,256]{3,2,1,0:T(8,128)(2,1)}, bf16[8,8,32,256]{3,2,1,0:T(8,128)(2,1)S(1)}, u32[]{:S(2)}) copy-start(bf16[8,8,32,256]{3,2,1,0:T(8,128)(2,1)S(1)} %collective-permute-done.3.low_far_ref) | copy-start | bytes 3145732
  92.8 1.0 copy-start.4

commit v3 on v2

v3 whole, which is shorter than its diff:
```python
import jax
import jax.numpy as jnp
import numpy as np
from jax import lax
from jax.experimental import pallas as pl
from jax.experimental.pallas import tpu as pltpu
from jax.sharding import PartitionSpec as P

HEAD_DIM = 128
BLOCK = 128
EPSILON = 1e-06
MASKED = -1000000000.0
SCALE = HEAD_DIM ** (-0.5)
LOG2E = 1.4426950408889634
BF16 = jnp.bfloat16
F32 = jnp.float32
MASKED_RAW = MASKED / SCALE
MASKED_LOG2 = MASKED * LOG2E
VMEM_LIMIT = 32 * 1024 * 1024
VMEM_ALL = 60 * 1024 * 1024

VMEM = pl.BlockSpec(memory_space=pltpu.VMEM)
SMEM = pl.BlockSpec(memory_space=pltpu.SMEM)
ANY = pl.BlockSpec(memory_space=pl.ANY)

XA, XB, YA, YB = 1, 3, 4, 12
ORDERS = (((XA, XB, YA, YB), (XB, XA, YB, YA)), ((YA, YB, XA, XB), (YB, YA, XB, XA)))


def rms_scaled(x, gain):
    scale = lax.rsqrt(jnp.mean(x * x, axis=1, keepdims=True) + EPSILON)
    return (x * scale * gain).astype(BF16)


def dot(a, b):
    return jnp.dot(a, b, preferred_element_type=F32)


def dot_t(a, b):
    return lax.dot_general(a, b, (((1,), (1,)), ((), ())), preferred_element_type=F32)


def block_facts(blocks, protein_ref, length_ref):
    ids = [protein_ref[b] for b in range(blocks)]
    live = []
    for b in range(blocks):
        offset = jnp.int32(0)
        for other in range(b):
            offset += jnp.where(ids[other] == ids[b], BLOCK, 0)
        live.append(jnp.clip(length_ref[ids[b]] - offset, 0, BLOCK))
    return ids, live


def encoder_kernel(
    protein_hbm,
    length_hbm,
    residue_hbm,
    gain_hbm,
    wq_hbm,
    wk_hbm,
    wv_hbm,
    wo_hbm,
    out_hbm,
    protein_ref,
    length_ref,
    residue_ref,
    gain_ref,
    out_ref,
    wq,
    wk,
    wv,
    wo,
    normed,
    q,
    k,
    v,
    context,
    sems,
):
    copies = [
        pltpu.make_async_copy(src, dst, sems.at[i])
        for i, (src, dst) in enumerate(
            (
                (gain_hbm, gain_ref),
                (residue_hbm, residue_ref),
                (wq_hbm, wq),
                (wk_hbm, wk),
                (wv_hbm, wv),
                (wo_hbm, wo),
                (protein_hbm, protein_ref),
                (length_hbm, length_ref),
            )
        )
    ]
    for copy in copies:
        copy.start()
    rows, width = residue_ref.shape
    blocks = rows // BLOCK
    inner = q.shape[1]
    copies[0].wait()
    copies[1].wait()
    gain = gain_ref[...]
    for b in range(blocks):
        span = slice(b * BLOCK, (b + 1) * BLOCK)
        normed[span, :] = rms_scaled(residue_ref[span, :].astype(F32), gain)
    for copy, weight, result in zip(copies[2:5], (wq, wk, wv), (q, k, v)):
        copy.wait()

        result[...] = dot(normed[...], weight[...]).astype(BF16)

    copies[6].wait()
    copies[7].wait()
    ids, live = block_facts(blocks, protein_ref, length_ref)
    lane = lax.broadcasted_iota(jnp.int32, (1, BLOCK), 1)
    mates, limits = [], []
    for b in range(blocks):
        mate, limit = jnp.int32(b), jnp.int32(0)
        for other in (b - 1, b + 1):
            if 0 <= other < blocks:
                same = ids[other] == ids[b]
                mate = jnp.where(same, other, mate)
                limit = jnp.where(same, live[other], limit)
        mates.append(mate)
        limits.append(limit)
    seen = [
        jnp.concatenate(
            [jnp.broadcast_to(lane < limit, (BLOCK, BLOCK)) for limit in (live[b], limits[b])], axis=1
        )
        for b in range(blocks)
    ]
    ones = jnp.ones((2 * BLOCK, HEAD_DIM), BF16)

    for h in range(inner // HEAD_DIM):
        cols = slice(h * HEAD_DIM, (h + 1) * HEAD_DIM)
        for b in range(blocks):
            span = slice(b * BLOCK, (b + 1) * BLOCK)
            mate = pl.ds(pl.multiple_of(mates[b] * BLOCK, BLOCK), BLOCK)
            window = jnp.concatenate([k[span, cols], k[mate, cols]], axis=0)
            scores = jnp.where(seen[b], dot_t(q[span, cols], window), MASKED_RAW)
            top = jnp.max(scores, axis=1, keepdims=True)
            weights = jnp.exp2((scores - top) * (SCALE * LOG2E)).astype(BF16)
            window = jnp.concatenate([v[span, cols], v[mate, cols]], axis=0)
            mixed = dot(weights, jnp.concatenate([window, ones], axis=1))
            context[span, cols] = (mixed[:, :HEAD_DIM] / mixed[:, HEAD_DIM:]).astype(BF16)

    copies[5].wait()
    half = width // 2
    stores = []
    for n in range(2):
        span = slice(n * half, (n + 1) * half)
        out_ref[span, :] = dot(context[...], wo[:, span]).astype(BF16).T
        stores.append(pltpu.make_async_copy(out_ref.at[span], out_hbm.at[span], sems.at[8 + n]))
        stores[n].start()
    for store in stores:
        store.wait()


def encoder(protein, length, residues, gain, wq, wk, wv, wo):
    rows, width = residues.shape
    inner = wq.shape[1]
    return pl.pallas_call(
        encoder_kernel,
        out_shape=jax.ShapeDtypeStruct((width, rows), BF16),
        in_specs=[ANY] * 8,
        out_specs=ANY,
        scratch_shapes=[
            pltpu.SMEM(protein.shape, jnp.int32),
            pltpu.SMEM(length.shape, jnp.int32),
            pltpu.VMEM((rows, width), BF16),
            pltpu.VMEM((1, width), F32),
            pltpu.VMEM((width, rows), BF16),
        ]
        + [pltpu.VMEM((width, inner), BF16)] * 3
        + [pltpu.VMEM((inner, width), BF16), pltpu.VMEM((rows, width), BF16)]
        + [pltpu.VMEM((rows, inner), BF16)] * 4
        + [pltpu.SemaphoreType.DMA((10,))],
        compiler_params=pltpu.CompilerParams(vmem_limit_bytes=VMEM_ALL),
        cost_estimate=pl.CostEstimate(
            flops=2 * rows * width * inner * 4, bytes_accessed=8 * width * inner, transcendentals=rows * rows * 8
        ),
        name="encoder",
    )(protein, length, residues, gain, wq, wk, wv, wo)


def as_column(row):
    size = row.shape[1]
    down = lax.broadcasted_iota(jnp.int32, (size, size), 0)
    along = lax.broadcasted_iota(jnp.int32, (size, size), 1)
    return jnp.sum(jnp.where(down == along, row, 0.0), axis=1, keepdims=True)


def query_kernel(
    protein_ref,
    length_ref,
    group_ref,
    where_ref,
    state_ref,
    dec_gain_ref,
    final_gain_ref,
    id_ref,
    wq_ref,
    wk_ref,
    wv_ref,
    residue_hbm,
    out_ref,
    back_ref,
    sorted_ref,
    gained_ref,
    own_ref,
    table_ref,
    start_ref,
    key_weight,
    columns,
    turned,
    sem,
):
    rows, width = state_ref.shape
    features = own_ref.shape[0]
    here, core = where_ref[0], where_ref[1]
    lanes = pl.ds(pl.multiple_of(here * features // BLOCK * BLOCK, BLOCK), BLOCK)
    copy = pltpu.make_async_copy(residue_hbm.at[:, lanes], columns, sem)
    copy.start()

    blocks = protein_ref.shape[0]
    slots = table_ref.shape[0] // 3
    each = slots // (start_ref.shape[0] - 1)
    ids, live = block_facts(blocks, protein_ref, length_ref)
    dest = [group_ref[ids[b]] for b in range(blocks)]
    for s in range(slots):
        table_ref[s] = 0
        table_ref[slots + s] = -1
        table_ref[2 * slots + s] = 0
    for b in range(blocks):
        rank = jnp.int32(0)
        for other in range(b):
            rank += jnp.where(dest[other] == dest[b], 1, 0)
        slot = dest[b] * each + rank
        table_ref[slot] = b
        table_ref[slots + slot] = ids[b]
        table_ref[2 * slots + slot] = live[b]

    id_row = id_ref[...].astype(F32)
    for e in range(start_ref.shape[0]):
        start_ref[e] = jnp.sum((id_row < 4.0 * e).astype(F32)).astype(jnp.int32)

    id_col = as_column(id_row)
    down = lax.broadcasted_iota(jnp.int32, (rows, rows), 0)
    along = lax.broadcasted_iota(jnp.int32, (rows, rows), 1)
    before = (id_col < id_row) | ((id_col == id_row) & (down < along))
    place_row = jnp.sum(before.astype(F32), axis=0, keepdims=True).astype(jnp.int32)
    before = (id_row < id_col) | ((id_row == id_col) & (along < down))
    place_col = jnp.sum(before.astype(F32), axis=1, keepdims=True).astype(jnp.int32)
    chosen = down == place_row
    back_ref[...] = (along == place_col).astype(F32).astype(BF16)
    sorted_ref[...] = jnp.sum(jnp.where(chosen, id_row, 0.0), axis=1, keepdims=True)
    normed = rms_scaled(state_ref[...].astype(F32), dec_gain_ref[...])
    normed = dot(chosen.astype(F32).astype(BF16), normed).astype(BF16)

    masks = origin_masks()
    part = features // 2
    gain_parts = [
        as_column(final_gain_ref[:, c * BLOCK : (c + 1) * BLOCK]) for c in range(width // BLOCK)
    ]
    gain_ref = turned
    for c, gain in enumerate(gain_parts):
        gain_ref[c * BLOCK : (c + 1) * BLOCK, :] = gain
    for index in range(width // part):
        origin = here ^ jnp.where(core == 0, int(masks[0, index]), int(masks[1, index]))
        rows_from = pl.ds(
            pl.multiple_of(origin * features + index // (width // features) * part, part), part
        )
        rows_to = slice(index * part, (index + 1) * part)
        gain = gain_ref[rows_from, :]
        key_weight[rows_to, :] = (wk_ref[rows_from, :].astype(F32) * gain).astype(BF16)
        gained_ref[rows_to, :] = (wv_ref[rows_from, :].astype(F32) * gain).astype(BF16)
    for pair in range(wq_ref.shape[1] // 256):
        queries = dot(normed, wq_ref[:, pair * 256 : (pair + 1) * 256]).astype(BF16)
        for side in range(2):
            h = pair * 2 + side
            head = queries[:, side * HEAD_DIM : (side + 1) * HEAD_DIM]
            out_ref[h] = dot_t(head, key_weight[:, h * HEAD_DIM : (h + 1) * HEAD_DIM]).astype(BF16)

    copy.wait()
    flipped = columns[...].astype(F32).T
    odd = here * features % BLOCK > 0
    own_ref[...] = jnp.where(odd, flipped[features:], flipped[:features])


def query_side(protein, length, group, where, states, dec_gain, final_gain, ids, wq, wk, wv, residues, groups):
    rows, width = states.shape
    inner = wq.shape[1]
    heads = inner // HEAD_DIM
    tokens = residues.shape[0]
    features = BLOCK // 2
    slots = groups * (tokens // BLOCK // 2)
    return pl.pallas_call(
        query_kernel,
        out_shape=(
            jax.ShapeDtypeStruct((heads, rows, width), BF16),
            jax.ShapeDtypeStruct((rows, rows), BF16),
            jax.ShapeDtypeStruct((rows, 1), F32),
            jax.ShapeDtypeStruct((width, inner), BF16),
            jax.ShapeDtypeStruct((features, tokens), F32),
            jax.ShapeDtypeStruct((3 * slots,), jnp.int32),
            jax.ShapeDtypeStruct((groups + 1,), jnp.int32),
        ),
        in_specs=[SMEM] * 4 + [VMEM] * 7 + [ANY],
        out_specs=(VMEM,) * 5 + (SMEM,) * 2,
        scratch_shapes=[
            pltpu.VMEM((width, inner), BF16),
            pltpu.VMEM((tokens, BLOCK), BF16),
            pltpu.VMEM((width, 1), F32),
            pltpu.SemaphoreType.DMA,
        ],
        compiler_params=pltpu.CompilerParams(vmem_limit_bytes=VMEM_LIMIT),
        cost_estimate=pl.CostEstimate(
            flops=4 * rows * width * inner, bytes_accessed=6 * width * inner + 2 * heads * rows * width, transcendentals=0
        ),
        name="query_side",
    )(
        protein,
        length,
        group,
        where,
        states,
        dec_gain.reshape(1, width),
        final_gain.reshape(1, width),
        ids.reshape(1, rows),
        wq,
        wk,
        wv,
        residues,
    )


def placing_kernel(table_hbm, arrived_hbm, own_hbm, encoded_ref, placed_ref, table_ref, own_ref, buffer, sems):
    sources, features, rows = buffer.shape
    groups = placed_ref.shape[0]
    each = placed_ref.shape[2] // BLOCK
    slots = groups * each
    copies = [
        pltpu.make_async_copy(arrived_hbm.at[s], buffer.at[s], sems.at[s]) for s in range(sources)
    ]
    table_copy = pltpu.make_async_copy(table_hbm, table_ref, sems.at[sources])
    own_copy = pltpu.make_async_copy(own_hbm, own_ref, sems.at[sources + 1])
    table_copy.start()
    own_copy.start()
    for copy in copies:
        copy.start()
    table_copy.wait()
    lane = lax.broadcasted_iota(jnp.int32, (16, BLOCK), 1)
    for d in range(groups):
        for s in range(each):
            slot = d * each + s
            placed_ref[d, features : features + 16, s * BLOCK : (s + 1) * BLOCK] = (
                jnp.where(lane < table_ref[2 * slots + slot], table_ref[slots + slot], -1).astype(F32).astype(BF16)
            )
    own_copy.wait()
    sums = own_ref[...]
    for s in range(sources):
        copies[s].wait()
        sums = sums + buffer[s].astype(F32)
    encoded_ref[...] = sums.astype(BF16)
    for d in range(groups):
        for s in range(each):
            start = pl.multiple_of(table_ref[d * each + s] * BLOCK, BLOCK)
            placed_ref[d, 0:features, s * BLOCK : (s + 1) * BLOCK] = encoded_ref[:, pl.ds(start, BLOCK)]


def placing(table, arrived, own, groups):
    sources, features, rows = arrived.shape
    each = table.shape[0] // 3 // groups
    return pl.pallas_call(
        placing_kernel,
        out_shape=(
            jax.ShapeDtypeStruct((features, rows), BF16),
            jax.ShapeDtypeStruct((groups, features + 16, each * BLOCK), BF16),
        ),
        in_specs=[ANY, ANY, ANY],
        out_specs=(VMEM, VMEM),
        scratch_shapes=[
            pltpu.SMEM(table.shape, jnp.int32),
            pltpu.VMEM(own.shape, F32),
            pltpu.VMEM(arrived.shape, BF16),
            pltpu.SemaphoreType.DMA((sources + 2,)),
        ],
        compiler_params=pltpu.CompilerParams(vmem_limit_bytes=VMEM_ALL),
        name="placing",
    )(table, arrived, own)


ROW_TILE = 32
TOGETHER = 4


def cross_kernel(
    start_hbm,
    query_ref,
    id_ref,
    key_id_ref,
    back_ref,
    low_ref,
    low_far_ref,
    high_ref,
    high_far_ref,
    wv_ref,
    wo_ref,
    out_hbm,
    out_ref,
    start_ref,
    key_scale,
    mixed,
    context,
    item_group,
    item_tile,
    sems,
):
    start_copy = pltpu.make_async_copy(start_hbm, start_ref, sems.at[0])
    start_copy.start()
    heads, rows, width = query_ref.shape
    chunks, groups, part, span = low_ref.shape
    pieces = (low_ref, low_far_ref, high_ref, high_far_ref)

    def keys(e):
        return jnp.concatenate([piece[:, e].reshape(chunks * part, span) for piece in pieces], axis=0)

    @pl.loop(0, groups)
    def _(e):
        squares = jnp.zeros((8, span), F32)
        for piece in pieces:
            for j in range(chunks):
                values = piece[j, e].astype(F32)
                squares = squares + jnp.sum((values * values).reshape(part // 8, 8, span), axis=0)
        total = jnp.sum(squares, axis=0, keepdims=True)
        key_scale[e] = lax.rsqrt(total / width + EPSILON)

    start_copy.wait()
    flat = heads * ROW_TILE

    def listed(e, count):
        first = start_ref[e] // ROW_TILE
        last = jnp.where(start_ref[e + 1] > start_ref[e], (start_ref[e + 1] + ROW_TILE - 1) // ROW_TILE, first)

        def note(i, at):
            item_group[at] = e
            item_tile[at] = i
            return at + 1

        return lax.fori_loop(first, last, note, count)

    items = lax.fori_loop(0, groups, listed, jnp.int32(0))
    for extra in range(TOGETHER - 1):
        item_group[items + extra] = item_group[items - 1]
        item_tile[items + extra] = item_tile[items - 1]

    @pl.loop(0, (items + TOGETHER - 1) // TOGETHER)
    def _(n):
        todo = [(item_group[n * TOGETHER + a], item_tile[n * TOGETHER + a]) for a in range(TOGETHER)]
        spots = [pl.ds(pl.multiple_of(i * ROW_TILE, ROW_TILE), ROW_TILE) for _, i in todo]
        scores = [
            dot(query_ref[:, at, :].reshape(flat, width), keys(e)) for (e, _), at in zip(todo, spots)
        ]
        weights = []
        for (e, _), at, raw in zip(todo, spots, scores):
            scale = key_scale[e]
            seen = id_ref[at, :] == key_id_ref[e]
            raw = (raw * (scale * (SCALE * LOG2E))).reshape(heads, ROW_TILE, span)
            raw = jnp.where(seen[None], raw, MASKED_LOG2)
            expo = jnp.exp2(raw - jnp.max(raw, axis=2, keepdims=True))
            share = 1.0 / jnp.sum(expo, axis=2, keepdims=True)
            weights.append((expo * scale[None] * share).astype(BF16).reshape(flat, span))
        spreads = [dot_t(w, keys(e)) for w, (e, _) in zip(weights, todo)]
        for (e, _), at, spread in zip(todo, spots, spreads):
            ids = id_ref[at, :]
            mine = (ids >= (e * 4).astype(F32)) & (ids < (e * 4 + 4).astype(F32))
            spread = spread.astype(BF16).reshape(heads, ROW_TILE, width)
            mixed[:, at, :] = jnp.where(mine[None], spread, mixed[:, at, :])

    for h in range(heads):
        cols = slice(h * HEAD_DIM, (h + 1) * HEAD_DIM)
        context[:, cols] = dot(mixed[h], wv_ref[:, cols]).astype(BF16)

    context[...] = dot(back_ref[...], context[...]).astype(BF16)

    half = rows // 2
    stores = []
    for n in range(2):
        span = slice(n * half, (n + 1) * half)
        out_ref[span, :] = dot(context[span, :], wo_ref[...]).astype(BF16)
        stores.append(pltpu.make_async_copy(out_ref.at[span], out_hbm.at[span], sems.at[1 + n]))
        stores[n].start()
    for store in stores:
        store.wait()


def cross(starts, queries, ids, key_ids, back, pieces, wv, wo):
    heads, rows, width = queries.shape
    groups, span = key_ids.shape[0], key_ids.shape[2]
    inner = wv.shape[1]
    items = rows // ROW_TILE + groups + TOGETHER
    return pl.pallas_call(
        cross_kernel,
        out_shape=jax.ShapeDtypeStruct((rows, width), BF16),
        in_specs=[ANY] + [VMEM] * 10,
        out_specs=ANY,
        scratch_shapes=[
            pltpu.VMEM((rows, width), BF16),
            pltpu.SMEM(starts.shape, jnp.int32),
            pltpu.VMEM((groups, 1, span), F32),
            pltpu.VMEM((heads, rows, width), BF16),
            pltpu.VMEM((rows, inner), BF16),
            pltpu.SMEM((items,), jnp.int32),
            pltpu.SMEM((items,), jnp.int32),
            pltpu.SemaphoreType.DMA((3,)),
        ],
        compiler_params=pltpu.CompilerParams(vmem_limit_bytes=VMEM_LIMIT),
        cost_estimate=pl.CostEstimate(
            flops=8 * rows * width * inner, bytes_accessed=2 * groups * width * span, transcendentals=rows * span * heads
        ),
        name="cross",
    )(starts, queries, ids, key_ids, back, *pieces, wv, wo)


def exchange(x, groups, tensor, half, step):
    pairs = [
        (d * tensor + t, d * tensor + (t ^ ORDERS[d % 2][half][step]))
        for d in range(groups)
        for t in range(tensor)
    ]
    return lax.ppermute(x, ("dp", "tensor"), pairs)


def gathered(low, high, groups, tensor):
    halves = [low[None], high[None]]
    for step in range(3):
        got = [exchange(halves[h], groups, tensor, h, step) for h in range(2)]
        halves = [jnp.concatenate([halves[h], got[h]], axis=0) for h in range(2)]
    got = [exchange(halves[h], groups, tensor, h, 3) for h in range(2)]
    return halves[0], got[0], halves[1], got[1]


def origin_masks():
    table = np.zeros((2, 2, 16), np.int32)
    for core in range(2):
        for half in range(2):
            for j in range(16):
                for step in range(4):
                    if j >> step & 1:
                        table[core, half, j] ^= ORDERS[core][half][step]
    return table.reshape(2, 32)


def body(
    residues,
    block_protein,
    protein_length,
    decoder_group,
    enc_gain,
    enc_query,
    enc_key,
    enc_value,
    enc_out,
    decoder_states,
    query_protein,
    dec_gain,
    final_gain,
    cross_query,
    cross_key,
    cross_value,
    cross_out,
):
    groups = lax.axis_size("dp")
    tensor = lax.axis_size("tensor")
    dp_index = lax.axis_index("dp")
    tensor_index = lax.axis_index("tensor")
    rows, width = residues.shape
    query_rows = decoder_states.shape[0]
    slice_width = width // tensor
    part = slice_width // 2

    partial_sums = encoder(
        block_protein, protein_length, residues, enc_gain.reshape(1, width), enc_query, enc_key, enc_value, enc_out
    )
    arrived = lax.all_to_all(
        partial_sums.reshape(tensor, slice_width, rows), "tensor", split_axis=0, concat_axis=0, tiled=True
    )
    where = jnp.stack([tensor_index, dp_index % 2]).astype(jnp.int32)
    queries, back, sorted_ids, gained_value, own, table, starts = query_side(
        block_protein,
        protein_length,
        decoder_group,
        where,
        decoder_states,
        dec_gain,
        final_gain,
        query_protein,
        cross_query,
        cross_key,
        cross_value,
        residues,
        groups,
    )
    share = query_rows // tensor
    own_rows = lax.dynamic_slice_in_dim(decoder_states, tensor_index * share, share, 0).astype(F32)
    arrived, own, queries = lax.optimization_barrier((arrived, own, queries))
    encoded, placed = placing(table, arrived, own, groups)
    received = lax.all_to_all(placed, "dp", split_axis=0, concat_axis=0, tiled=True)
    pieces = gathered(received[:, :part], received[:, part : 2 * part], groups, tensor)
    key_ids = received[:, slice_width : slice_width + 1].astype(F32)
    outcome = cross(starts, queries, sorted_ids, key_ids, back, pieces, gained_value, cross_out)
    mixed = lax.all_to_all(
        outcome.reshape(tensor, share, width), "tensor", split_axis=0, concat_axis=0, tiled=True
    )
    mixed, own_rows = lax.optimization_barrier((mixed, own_rows))
    mixed = mixed.astype(F32).sum(axis=0)
    decoded = (own_rows + mixed).astype(BF16)
    return (encoded.T, decoded)


def solution(mesh):
    in_specs = (
        P("dp", None),
        P("dp"),
        P(),
        P(),
        P(),
        P(None, "tensor"),
        P(None, "tensor"),
        P(None, "tensor"),
        P("tensor", None),
        P("dp", None),
        P("dp"),
        P(),
        P(),
        P(None, "tensor"),
        P(None, "tensor"),
        P(None, "tensor"),
        P("tensor", None),
    )
    out_specs = (P("dp", "tensor"), P(("dp", "tensor"), None))
    return jax.shard_map(body, mesh=mesh, in_specs=in_specs, out_specs=out_specs, check_vma=False)
```

time: 130 us -> 122 us (0.938)
  blocking collectives: 30.6 us -> 13.7 us
  waiting for transfers between devices: 25.8 us -> 38.4 us
  Pallas kernels: 40.7 us -> 30.2 us
  starting transfers between devices: 21.5 us -> 26 us
  local copies, waits for them, and re-layouts: 6.23 us -> 10.4 us
  other arithmetic: 3.75 us -> 2.02 us
    all_to_all x1 -> x0, blocking collectives: 17.1 us -> none  [body(): lax.all_to_all(outcome.reshape(tensor, share, width), 'tensor', split_axi...]
    all_to_all x0 -> x1, waiting for transfers between devices: none -> 10.8 us  [body(): lax.all_to_all(outcome.reshape(tensor, share, width), 'tensor', split_axi...]
    unnamed x19 -> x36, local copies, waits for them, and re-layouts: 2.81 us -> 10.4 us
    all_to_all x0 -> x1, starting transfers between devices: none -> 5.61 us  [body(): lax.all_to_all(outcome.reshape(tensor, share, width), 'tensor', split_axi...]
    pallas_call x1, Pallas kernels: 17.7 us -> 12.6 us  [cross(): pl.pallas_call(cross_kernel, out_shape=jax.ShapeDtypeStruct((rows, width)...]
    pallas_call x1, Pallas kernels: 10.4 us -> 5.71 us  [query_side(): pl.pallas_call(query_kernel, out_shape=(jax.ShapeDtypeStruct((heads, rows...]
    reshape x2 -> x0, local copies, waits for them, and re-layouts: 1.84 us -> none  [the longest x1 1.04 us: query_side(): final_gain.reshape(width, 1)]
    ppermute x8, waiting for transfers between devices: 24.7 us -> 26.1 us  [exchange(): return lax.ppermute(x, ('dp', 'tensor'), pairs)]
  transfers between devices with their start and end apart: 9 -> 10, of which waited for: 8 -> 9; matrix products, arithmetic and copies ran while one was open for 5% -> 1% of each run, Pallas kernels for 8% -> 5%
where the time goes in v3:
time: 122 us
  waiting for transfers between devices  38.4 us (31%)
  Pallas kernels  30.2 us (25%)
  starting transfers between devices  26 us (21%)
  blocking collectives  13.7 us (11%)
  local copies, waits for them, and re-layouts  10.4 us (9%)
  other arithmetic  2.02 us (2%)
    ppermute x8, waiting for transfers between devices, exchange(): return lax.ppermute(x, ('dp', 'tensor'), pairs)  26.1 us
    all_to_all x1, blocking collectives, body(): lax.all_to_all(placed, 'dp', split_axis=0, concat_axis=0, tiled=True)  13.7 us
    ppermute x8, starting transfers between devices, exchange(): return lax.ppermute(x, ('dp', 'tensor'), pairs)  13.1 us
    pallas_call x1, Pallas kernels, cross(): pl.pallas_call(cross_kernel, out_shape=jax.ShapeDtypeStruct((rows, width)...  12.6 us
    all_to_all x1, waiting for transfers between devices, body(): lax.all_to_all(outcome.reshape(tensor, share, width), 'tensor', split_axi...  10.8 us
    unnamed x36, local copies, waits for them, and re-layouts  10.4 us
    pallas_call x1, Pallas kernels, encoder(): pl.pallas_call(encoder_kernel, out_shape=jax.ShapeDtypeStruct((width, row...  9.65 us
    all_to_all x1, starting transfers between devices, body(): lax.all_to_all(partial_sums.reshape(tensor, slice_width, rows), 'tensor',...  7.34 us
  transfers between devices with their start and end apart: 10, of which 9 were waited for; matrix products, arithmetic and copies ran while one was open for 1% of the time, Pallas kernels for 5%

profile of v3, /device:TPU:0, one launch (start us, length us, event | category | flops | bytes accessed | tf_op | source)
XLA Modules:
  0.0 121.6 jit_solution(13335218717882207115)
XLA Ops:
  0.6 9.6 %encoder.1 = bf16[1024,512]{1,0:T(8,128)(2,1)} custom-call(s32[4]{0:T(128)} %protein_hbm.1, s32[32]{0:T(128)} %length_hbm.1, bf16[512,1024]{1,0:T(8,128)(2,1)} %residue_hbm.3, f32[1,1024]{1,0:T(1,128)} %bitcast.16, bf16[1024,1024]{1,0:T(8,128)(2,1)} %wq_hbm.1, bf16[1024,1024]{1,0:T(8,128)(2,1)} %wk_hbm.1, bf16[1024,1024]{1,0:T(8,128)(2,1)} %wv_hbm.1, ...), custom_call_target="tpu_custom_call" | custom-call | flops 4294967296 | bytes 8388608 | tf_op jit(solution)/shard_map/encoder/pallas_call | solution.py:161
  10.3 0.0 copy-start.17
  10.3 0.0 copy-start.6
  10.3 0.0 copy-start.11
  10.3 0.0 copy-start.12
  10.3 0.0 copy-start.13
  10.3 0.0 copy-start.14
  10.4 7.3 %all-to-all-start = ((bf16[16,64,512]{2,1,0:T(8,128)(2,1)}), bf16[16,64,512]{2,1,0:T(8,128)(2,1)}, u32[]{:S(2)}, u32[]{:S(2)}) async-start(bf16[16,64,512]{2,1,0:T(8,128)(2,1)} %bitcast.14), calls=%async_computation | async-start | bytes 2097152 | tf_op jit(solution)/shard_map/all_to_all | solution.py:584
  17.8 0.1 pad_add_fusion.where_ref
  17.9 0.0 copy-start.3
  17.9 1.6 %copy-done.3 = bf16[1024,1024]{1,0:T(8,128)(2,1)S(1)} copy-done((bf16[1024,1024]{1,0:T(8,128)(2,1)S(1)}, bf16[1024,1024]{1,0:T(8,128)(2,1)}, u32[]{:S(2)}) %copy-start.3) | copy-done | bytes 2097176
  19.5 1.6 %copy-done.4 = bf16[1024,1024]{1,0:T(8,128)(2,1)S(1)} copy-done((bf16[1024,1024]{1,0:T(8,128)(2,1)S(1)}, bf16[1024,1024]{1,0:T(8,128)(2,1)}, u32[]{:S(2)}) %copy-start.4) | copy-done | bytes 2097176
  21.1 1.6 %copy-done.5 = bf16[1024,1024]{1,0:T(8,128)(2,1)S(1)} copy-done((bf16[1024,1024]{1,0:T(8,128)(2,1)S(1)}, bf16[1024,1024]{1,0:T(8,128)(2,1)}, u32[]{:S(2)}) %copy-start.5) | copy-done | bytes 2097176
  22.6 1.1 copy-done.7
  23.8 5.7 %query_side.1 = (bf16[8,384,1024]{2,1,0:T(8,128)(2,1)S(1)}, bf16[384,384]{1,0:T(8,128)(2,1)S(1)}, f32[384,1]{1,0:T(8,128)S(1)}, bf16[1024,1024]{1,0:T(8,128)(2,1...) custom-call(s32[4]{0:T(128)S(1)} %copy-done.13, s32[32]{0:T(128)S(1)} %copy-done.14, s32[32]{0:T(128)S(1)} %copy-done.15, ...), custom_call_target="tpu_custom_call" | custom-call | flops 1610612736 | bytes 12582912 | tf_op jit(solution)/shard_map/query_side/pallas_call | solution.py:296
  29.5 2.6 %copy-done = bf16[8,384,1024]{2,1,0:T(8,128)(2,1)} copy-done((bf16[8,384,1024]{2,1,0:T(8,128)(2,1)}, bf16[8,384,1024]{2,1,0:T(8,128)(2,1)S(1)}, u32[]{:S(2)}) %copy-start) | copy-done | bytes 6291480
  32.1 0.7 copy-done.8
  32.8 0.7 copy-done.10
  33.5 0.5 copy-done.16
  34.0 1.5 %all-to-all-done.arrived_hbm = bf16[16,64,512]{2,1,0:T(8,128)(2,1)} async-done(((bf16[16,64,512]{2,1,0:T(8,128)(2,1)}), bf16[16,64,512]{2,1,0:T(8,128)(2,1)}, u32[]{:S(2)}, u32[]{:S(2)}) %all-to-all-start) | async-done | bytes 1048608 | tf_op jit(solution)/shard_map/all_to_all | solution.py:584
  35.4 2.3 %placing.1 = (bf16[64,512]{1,0:T(8,128)(2,1)}, bf16[8,80,256]{2,1,0:T(8,128)(2,1)}) custom-call(s32[48]{0:T(128)} %copy-done.16, bf16[16,64,512]{2,1,0:T(8,128)(2,1)} %all-to-all-done.arrived_hbm, f32[64,512]{1,0:T(8,128)} %copy-done.10), custom_call_target="tpu_custom_call" | custom-call | tf_op jit(solution)/shard_map/placing/pallas_call | solution.py:373
  37.7 0.0 copy-start.2
  37.7 13.7 %all_to_all.15 = bf16[8,80,256]{2,1,0:T(8,128)(2,1)S(1)} all-to-all(bf16[8,80,256]{2,1,0:T(8,128)(2,1)} %get-tuple-element.25), channel_id=1, replica_groups=mesh['dp'=8,'tensor'=16] {'dp'}, dimensions={0} | all-to-all | bytes 655360 | tf_op jit(solution)/shard_map/all_to_all | solution.py:607
  51.4 0.5 collective-permute-start
  51.9 2.1 %collective-permute-start.4 = (bf16[1,8,32,256]{3,2,1,0:T(8,128)(2,1)S(1)}, bf16[1,8,32,256]{3,2,1,0:T(8,128)(2,1)S(1)}, u32[]{:S(2)}, u32[]{:S(2)}) collective-permute-start(bf16[1,8,32,256]{3,2,1,0:T(8,128)(2,1)S(1)} %get-tuple-element.30), channel_id=1, source_target_pairs={{0,3},{1,2},{2,1},{3,0},{4,7},{5,6},{6,5},{7,4},{8,11},{9,10},{10,... | collective-permute-start | bytes 393224 | tf_op jit(solution)/shard_map/ppermute | solution.py:530
  54.0 2.5 %collective-permute-done = bf16[1,8,32,256]{3,2,1,0:T(8,128)(2,1)S(1)} collective-permute-done((bf16[1,8,32,256]{3,2,1,0:T(8,128)(2,1)S(1)}, bf16[1,8,32,256]{3,2,1,0:T(8,128)(2,1)S(1)}, u32[]{:S(2)}, u32[]{:S(2)}) %collective-permute-start) | collective-permute-done | bytes 131104 | tf_op jit(solution)/shard_map/ppermute | solution.py:530
  56.5 1.7 %collective-permute-start.1 = (bf16[2,8,32,256]{3,2,1,0:T(8,128)(2,1)S(1)}, bf16[2,8,32,256]{3,2,1,0:T(8,128)(2,1)S(1)}, u32[]{:S(2)}, u32[]{:S(2)}) collective-permute-start(bf16[2,8,32,256]{3,2,1,0:T(8,128)(2,1)S(1)} %pad_maximum_fusion.4), channel_id=1, source_target_pairs={{0,3},{1,2},{2,1},{3,0},{4,7},{5,6},{6,5},{7,4},{8,11},{9,10},{10,... | collective-permute-start | bytes 786440 | tf_op jit(solution)/shard_map/ppermute | solution.py:530
  58.2 0.6 collective-permute-start.5
  58.8 5.4 %collective-permute-done.1 = bf16[2,8,32,256]{3,2,1,0:T(8,128)(2,1)S(1)} collective-permute-done((bf16[2,8,32,256]{3,2,1,0:T(8,128)(2,1)S(1)}, bf16[2,8,32,256]{3,2,1,0:T(8,128)(2,1)S(1)}, u32[]{:S(2)}, u32[]{:S(2)}) %collective-permute-start.1) | collective-permute-done | bytes 262176 | tf_op jit(solution)/shard_map/ppermute | solution.py:530
  64.2 0.1 pad_maximum_fusion.2
  64.2 0.5 collective-permute-start.2
  64.7 0.2 collective-permute-done.5
  64.8 0.1 pad_maximum_fusion.3
  64.9 3.7 %collective-permute-start.6 = (bf16[4,8,32,256]{3,2,1,0:T(8,128)(2,1)S(1)}, bf16[4,8,32,256]{3,2,1,0:T(8,128)(2,1)S(1)}, u32[]{:S(2)}, u32[]{:S(2)}) collective-permute-start(bf16[4,8,32,256]{3,2,1,0:T(8,128)(2,1)S(1)} %pad_maximum_fusion.3), channel_id=1, source_target_pairs={{0,12},{1,13},{2,14},{3,15},{4,8},{5,9},{6,10},{7,11},{8,4},{9,5},... | collective-permute-start | bytes 1572872 | tf_op jit(solution)/shard_map/ppermute | solution.py:530
  68.6 4.8 %collective-permute-done.2 = bf16[4,8,32,256]{3,2,1,0:T(8,128)(2,1)S(1)} collective-permute-done((bf16[4,8,32,256]{3,2,1,0:T(8,128)(2,1)S(1)}, bf16[4,8,32,256]{3,2,1,0:T(8,128)(2,1)S(1)}, u32[]{:S(2)}, u32[]{:S(2)}) %collective-permute-start.2) | collective-permute-done | bytes 524320 | tf_op jit(solution)/shard_map/ppermute | solution.py:530
  73.5 0.1 pad_maximum_fusion.low_ref
  73.6 1.7 %collective-permute-start.3 = (bf16[8,8,32,256]{3,2,1,0:T(8,128)(2,1)S(1)}, bf16[8,8,32,256]{3,2,1,0:T(8,128)(2,1)S(1)}, u32[]{:S(2)}, u32[]{:S(2)}) collective-permute-start(bf16[8,8,32,256]{3,2,1,0:T(8,128)(2,1)S(1)} %pad_maximum_fusion.low_ref), channel_id=1, source_target_pairs={{0,12},{1,13},{2,14},{3,15},{4,8},{5,9},{6,10},{7,11},{8,4},{9,5},... | collective-permute-start | bytes 3145736 | tf_op jit(solution)/shard_map/ppermute | solution.py:530
  75.3 0.5 collective-permute-done.6
  75.8 0.1 pad_maximum_fusion.1.high_ref
  75.9 2.4 %collective-permute-start.7 = (bf16[8,8,32,256]{3,2,1,0:T(8,128)(2,1)S(1)}, bf16[8,8,32,256]{3,2,1,0:T(8,128)(2,1)S(1)}, u32[]{:S(2)}, u32[]{:S(2)}) collective-permute-start(bf16[8,8,32,256]{3,2,1,0:T(8,128)(2,1)S(1)} %pad_maximum_fusion.1.high_ref), channel_id=1, source_target_pairs={{0,4},{1,5},{2,6},{3,7},{4,0},{5,1},{6,2},{7,3},{8,12},{9,13},{10,... | collective-permute-start | bytes 3145736 | tf_op jit(solution)/shard_map/ppermute | solution.py:530
  78.3 11.4 %collective-permute-done.3.low_far_ref = bf16[8,8,32,256]{3,2,1,0:T(8,128)(2,1)S(1)} collective-permute-done((bf16[8,8,32,256]{3,2,1,0:T(8,128)(2,1)S(1)}, bf16[8,8,32,256]{3,2,1,0:T(8,128)(2,1)S(1)}, u32[]{:S(2)}, u32[]{:S(2)}) %collective-permute-start.3) | collective-permute-done | bytes 1048608 | tf_op jit(solution)/shard_map/ppermute | solution.py:530
  89.7 1.4 %collective-permute-done.7.high_far_ref = bf16[8,8,32,256]{3,2,1,0:T(8,128)(2,1)S(1)} collective-permute-done((bf16[8,8,32,256]{3,2,1,0:T(8,128)(2,1)S(1)}, bf16[8,8,32,256]{3,2,1,0:T(8,128)(2,1)S(1)}, u32[]{:S(2)}, u32[]{:S(2)}) %collective-permute-start.7) | collective-permute-done | bytes 1048608 | tf_op jit(solution)/shard_map/ppermute | solution.py:530
  91.1 12.6 %cross.1 = bf16[384,1024]{1,0:T(8,128)(2,1)} custom-call(s32[9]{0:T(128)S(1)} %get-tuple-element.22.start_hbm, bf16[8,384,1024]{2,1,0:T(8,128)(2,1)S(1)} %copy-done.1, f32[384,1]{1,0:T(8,128)S(1)} %copy-done.9, f32[8,1,256]{2,1,0:T(1,128)S(1)} %slice_convert_fusion.key_id_ref, bf16[384,384]{1,0:T(8,128)(2,1)S(1)} %get-tuple-element.26.back_ref, ...), custom_call_target="tpu_custom_call" | custom-call | flops 3221225472 | bytes 4194304 | tf_op jit(solution)/shard_map/cross/pallas_call | solution.py:501
  103.6 5.6 %all-to-all-start.2 = ((bf16[16,24,1024]{2,1,0:T(8,128)(2,1)}), bf16[16,24,1024]{2,1,0:T(8,128)(2,1)S(1)}, u32[]{:S(2)}, u32[]{:S(2)}) async-start(bf16[16,24,1024]{2,1,0:T(8,128)(2,1)} %bitcast.9), calls=%async_computation.2 | async-start | bytes 1572864 | tf_op jit(solution)/shard_map/all_to_all | solution.py:611
  109.2 0.8 dynamic-slice_convert_fusion
  110.1 10.8 %all-to-all-done.2 = bf16[16,24,1024]{2,1,0:T(8,128)(2,1)S(1)} async-done(((bf16[16,24,1024]{2,1,0:T(8,128)(2,1)}), bf16[16,24,1024]{2,1,0:T(8,128)(2,1)S(1)}, u32[]{:S(2)}, u32[]{:S(2)}) %all-to-all-start.2) | async-done | bytes 786464 | tf_op jit(solution)/shard_map/all_to_all | solution.py:611
  120.8 0.1 convert_reduce_fusion
  121.0 0.6 add_convert_fusion
  (26 shorter events, 0.1 us)
Async XLA Ops:
  10.3 7.4 %copy-start.17 = (s32[384]{0:T(512)S(1)}, s32[384]{0:T(512)}, u32[]{:S(2)}) copy-start(s32[384]{0:T(512)} %param.27) | copy-start | bytes 4612
  10.3 7.5 %copy-start.6 = (bf16[512,1024]{1,0:T(8,128)(2,1)S(1)}, bf16[512,1024]{1,0:T(8,128)(2,1)}, u32[]{:S(2)}) copy-start(bf16[512,1024]{1,0:T(8,128)(2,1)} %residue_hbm.3) | copy-start | bytes 3145732
  10.3 7.5 %copy-start.11 = (f32[1024]{0:T(1024)S(1)}, f32[1024]{0:T(1024)}, u32[]{:S(2)}) copy-start(f32[1024]{0:T(1024)} %param.28) | copy-start | bytes 12292
  10.3 7.5 %copy-start.12 = (f32[1024]{0:T(1024)S(1)}, f32[1024]{0:T(1024)}, u32[]{:S(2)}) copy-start(f32[1024]{0:T(1024)} %param.29) | copy-start | bytes 12292
  10.3 7.5 %copy-start.13 = (s32[4]{0:T(128)S(1)}, s32[4]{0:T(128)}, u32[]{:S(2)}) copy-start(s32[4]{0:T(128)} %protein_hbm.1) | copy-start | bytes 52
  10.3 7.5 %copy-start.14 = (s32[32]{0:T(128)S(1)}, s32[32]{0:T(128)}, u32[]{:S(2)}) copy-start(s32[32]{0:T(128)} %length_hbm.1) | copy-start | bytes 388
  10.4 7.5 %copy-start.15 = (s32[32]{0:T(128)S(1)}, s32[32]{0:T(128)}, u32[]{:S(2)}) copy-start(s32[32]{0:T(128)} %group_ref.1) | copy-start | bytes 388
  10.4 25.1 %all-to-all-start = ((bf16[16,64,512]{2,1,0:T(8,128)(2,1)}), bf16[16,64,512]{2,1,0:T(8,128)(2,1)}, u32[]{:S(2)}, u32[]{:S(2)}) async-start(bf16[16,64,512]{2,1,0:T(8,128)(2,1)} %bitcast.14), calls=%async_computation | async-start | bytes 2097152 | tf_op jit(solution)/shard_map/all_to_all | solution.py:584
  17.9 1.6 %copy-start.3 = (bf16[1024,1024]{1,0:T(8,128)(2,1)S(1)}, bf16[1024,1024]{1,0:T(8,128)(2,1)}, u32[]{:S(2)}) copy-start(bf16[1024,1024]{1,0:T(8,128)(2,1)} %wq_ref.1) | copy-start | bytes 6291460
  19.5 1.6 %copy-start.4 = (bf16[1024,1024]{1,0:T(8,128)(2,1)S(1)}, bf16[1024,1024]{1,0:T(8,128)(2,1)}, u32[]{:S(2)}) copy-start(bf16[1024,1024]{1,0:T(8,128)(2,1)} %wk_ref.1) | copy-start | bytes 6291460
  21.1 1.6 %copy-start.5 = (bf16[1024,1024]{1,0:T(8,128)(2,1)S(1)}, bf16[1024,1024]{1,0:T(8,128)(2,1)}, u32[]{:S(2)}) copy-start(bf16[1024,1024]{1,0:T(8,128)(2,1)} %wv_ref.1) | copy-start | bytes 6291460
  22.6 1.1 copy-start.7
  29.5 2.6 %copy-start = (bf16[8,384,1024]{2,1,0:T(8,128)(2,1)}, bf16[8,384,1024]{2,1,0:T(8,128)(2,1)S(1)}, u32[]{:S(2)}) copy-start(bf16[8,384,1024]{2,1,0:T(8,128)(2,1)S(1)} %get-tuple-element.23.query_ref) | copy-start | bytes 18874372
  32.1 0.7 copy-start.8
  32.8 0.7 copy-start.10
  33.5 0.5 copy-start.16
  35.4 55.6 %copy-start.9 = (f32[384,1]{1,0:T(8,128)S(1)}, f32[384,1]{1,0:T(8,128)}, u32[]{:S(2)}) copy-start(f32[384,1]{1,0:T(8,128)} %copy-done.8) | copy-start | bytes 4612
  37.7 53.3 %copy-start.2 = (bf16[1024,1024]{1,0:T(8,128)(2,1)S(1)}, bf16[1024,1024]{1,0:T(8,128)(2,1)}, u32[]{:S(2)}) copy-start(bf16[1024,1024]{1,0:T(8,128)(2,1)} %wo_ref.1) | copy-start | bytes 6291460
  51.4 5.0 %collective-permute-start = (bf16[1,8,32,256]{3,2,1,0:T(8,128)(2,1)S(1)}, bf16[1,8,32,256]{3,2,1,0:T(8,128)(2,1)S(1)}, u32[]{:S(2)}, u32[]{:S(2)}) collective-permute-start(bf16[1,8,32,256]{3,2,1,0:T(8,128)(2,1)S(1)} %get-tuple-element.31), channel_id=1, source_target_pairs={{0,1},{1,0},{2,3},{3,2},{4,5},{5,4},{6,7},{7,6},{8,9},{9,8},{10,11... | collective-permute-start | bytes 393224 | tf_op jit(solution)/shard_map/ppermute | solution.py:530
  51.9 6.3 %collective-permute-start.4 = (bf16[1,8,32,256]{3,2,1,0:T(8,128)(2,1)S(1)}, bf16[1,8,32,256]{3,2,1,0:T(8,128)(2,1)S(1)}, u32[]{:S(2)}, u32[]{:S(2)}) collective-permute-start(bf16[1,8,32,256]{3,2,1,0:T(8,128)(2,1)S(1)} %get-tuple-element.30), channel_id=1, source_target_pairs={{0,3},{1,2},{2,1},{3,0},{4,7},{5,6},{6,5},{7,4},{8,11},{9,10},{10,... | collective-permute-start | bytes 393224 | tf_op jit(solution)/shard_map/ppermute | solution.py:530
  56.5 7.7 %collective-permute-start.1 = (bf16[2,8,32,256]{3,2,1,0:T(8,128)(2,1)S(1)}, bf16[2,8,32,256]{3,2,1,0:T(8,128)(2,1)S(1)}, u32[]{:S(2)}, u32[]{:S(2)}) collective-permute-start(bf16[2,8,32,256]{3,2,1,0:T(8,128)(2,1)S(1)} %pad_maximum_fusion.4), channel_id=1, source_target_pairs={{0,3},{1,2},{2,1},{3,0},{4,7},{5,6},{6,5},{7,4},{8,11},{9,10},{10,... | collective-permute-start | bytes 786440 | tf_op jit(solution)/shard_map/ppermute | solution.py:530
  58.2 6.6 %collective-permute-start.5 = (bf16[2,8,32,256]{3,2,1,0:T(8,128)(2,1)S(1)}, bf16[2,8,32,256]{3,2,1,0:T(8,128)(2,1)S(1)}, u32[]{:S(2)}, u32[]{:S(2)}) collective-permute-start(bf16[2,8,32,256]{3,2,1,0:T(8,128)(2,1)S(1)} %pad_maximum_fusion.5), channel_id=1, source_target_pairs={{0,1},{1,0},{2,3},{3,2},{4,5},{5,4},{6,7},{7,6},{8,9},{9,8},{10,11... | collective-permute-start | bytes 786440 | tf_op jit(solution)/shard_map/ppermute | solution.py:530
  64.2 26.9 %copy-start.1 = (bf16[8,384,1024]{2,1,0:T(8,128)(2,1)S(1)}, bf16[8,384,1024]{2,1,0:T(8,128)(2,1)}, u32[]{:S(2)}) copy-start(bf16[8,384,1024]{2,1,0:T(8,128)(2,1)} %copy-done) | copy-start | bytes 18874372
  64.2 9.3 %collective-permute-start.2 = (bf16[4,8,32,256]{3,2,1,0:T(8,128)(2,1)S(1)}, bf16[4,8,32,256]{3,2,1,0:T(8,128)(2,1)S(1)}, u32[]{:S(2)}, u32[]{:S(2)}) collective-permute-start(bf16[4,8,32,256]{3,2,1,0:T(8,128)(2,1)S(1)} %pad_maximum_fusion.2), channel_id=1, source_target_pairs={{0,4},{1,5},{2,6},{3,7},{4,0},{5,1},{6,2},{7,3},{8,12},{9,13},{10,... | collective-permute-start | bytes 1572872 | tf_op jit(solution)/shard_map/ppermute | solution.py:530
  64.9 10.9 %collective-permute-start.6 = (bf16[4,8,32,256]{3,2,1,0:T(8,128)(2,1)S(1)}, bf16[4,8,32,256]{3,2,1,0:T(8,128)(2,1)S(1)}, u32[]{:S(2)}, u32[]{:S(2)}) collective-permute-start(bf16[4,8,32,256]{3,2,1,0:T(8,128)(2,1)S(1)} %pad_maximum_fusion.3), channel_id=1, source_target_pairs={{0,12},{1,13},{2,14},{3,15},{4,8},{5,9},{6,10},{7,11},{8,4},{9,5},... | collective-permute-start | bytes 1572872 | tf_op jit(solution)/shard_map/ppermute | solution.py:530
  73.6 16.1 %collective-permute-start.3 = (bf16[8,8,32,256]{3,2,1,0:T(8,128)(2,1)S(1)}, bf16[8,8,32,256]{3,2,1,0:T(8,128)(2,1)S(1)}, u32[]{:S(2)}, u32[]{:S(2)}) collective-permute-start(bf16[8,8,32,256]{3,2,1,0:T(8,128)(2,1)S(1)} %pad_maximum_fusion.low_ref), channel_id=1, source_target_pairs={{0,12},{1,13},{2,14},{3,15},{4,8},{5,9},{6,10},{7,11},{8,4},{9,5},... | collective-permute-start | bytes 3145736 | tf_op jit(solution)/shard_map/ppermute | solution.py:530
  75.9 15.1 %collective-permute-start.7 = (bf16[8,8,32,256]{3,2,1,0:T(8,128)(2,1)S(1)}, bf16[8,8,32,256]{3,2,1,0:T(8,128)(2,1)S(1)}, u32[]{:S(2)}, u32[]{:S(2)}) collective-permute-start(bf16[8,8,32,256]{3,2,1,0:T(8,128)(2,1)S(1)} %pad_maximum_fusion.1.high_ref), channel_id=1, source_target_pairs={{0,4},{1,5},{2,6},{3,7},{4,0},{5,1},{6,2},{7,3},{8,12},{9,13},{10,... | collective-permute-start | bytes 3145736 | tf_op jit(solution)/shard_map/ppermute | solution.py:530
  103.6 17.2 %all-to-all-start.2 = ((bf16[16,24,1024]{2,1,0:T(8,128)(2,1)}), bf16[16,24,1024]{2,1,0:T(8,128)(2,1)S(1)}, u32[]{:S(2)}, u32[]{:S(2)}) async-start(bf16[16,24,1024]{2,1,0:T(8,128)(2,1)} %bitcast.9), calls=%async_computation.2 | async-start | bytes 1572864 | tf_op jit(solution)/shard_map/all_to_all | solution.py:611

commit v4 on v3

--- a/solution.py
+++ b/solution.py
@@ -18,6 +18,8 @@
 MASKED_LOG2 = MASKED * LOG2E
 VMEM_LIMIT = 32 * 1024 * 1024
 VMEM_ALL = 60 * 1024 * 1024
+VMEM_NEAR = 24 * 1024 * 1024
+VMEM_PLACING = 8 * 1024 * 1024
 
 VMEM = pl.BlockSpec(memory_space=pltpu.VMEM)
 SMEM = pl.BlockSpec(memory_space=pltpu.SMEM)
@@ -207,6 +209,7 @@
     sorted_ref,
     gained_ref,
     own_ref,
+    key_id_ref,
     table_ref,
     start_ref,
     key_weight,
@@ -222,22 +225,35 @@
     copy.start()
 
     blocks = protein_ref.shape[0]
-    slots = table_ref.shape[0] // 3
-    each = slots // (start_ref.shape[0] - 1)
-    ids, live = block_facts(blocks, protein_ref, length_ref)
-    dest = [group_ref[ids[b]] for b in range(blocks)]
+    slots = table_ref.shape[0]
+    groups = key_id_ref.shape[0]
+    each = slots // groups
+    dest = [group_ref[protein_ref[b]] for b in range(blocks)]
     for s in range(slots):
         table_ref[s] = 0
-        table_ref[slots + s] = -1
-        table_ref[2 * slots + s] = 0
     for b in range(blocks):
         rank = jnp.int32(0)
         for other in range(b):
             rank += jnp.where(dest[other] == dest[b], 1, 0)
-        slot = dest[b] * each + rank
-        table_ref[slot] = b
-        table_ref[slots + slot] = ids[b]
-        table_ref[2 * slots + slot] = live[b]
+        table_ref[dest[b] * each + rank] = b
+
+    lane = lax.broadcasted_iota(jnp.int32, (1, BLOCK), 1)
+    proteins = length_ref.shape[0] // groups
+    for e in range(groups):
+        taken = jnp.int32(0)
+        names, limits = [jnp.int32(-1)] * each, [jnp.int32(0)] * each
+        for p in range(e * proteins, (e + 1) * proteins):
+            size = length_ref[p]
+            count = lax.shift_right_logical(size + (BLOCK - 1), 7)
+            wanted = group_ref[p] == where_ref[2]
+            for s in range(each):
+                offset = s - taken
+                here_too = wanted & (offset >= 0) & (offset < count)
+                names[s] = jnp.where(here_too, p, names[s])
+                limits[s] = jnp.where(here_too, jnp.clip(size - offset * BLOCK, 0, BLOCK), limits[s])
+            taken += jnp.where(wanted, count, 0)
+        for s in range(each):
+            key_id_ref[e, :, s * BLOCK : (s + 1) * BLOCK] = jnp.where(lane < limits[s], names[s], -1).astype(F32)
 
     id_row = id_ref[...].astype(F32)
     for e in range(start_ref.shape[0]):
@@ -269,7 +285,10 @@
         rows_from = pl.ds(
             pl.multiple_of(origin * features + index // (width // features) * part, part), part
         )
-        rows_to = slice(index * part, (index + 1) * part)
+        half, chunk = divmod(index, width // features)
+        far, chunk = divmod(chunk, width // features // 2)
+        place = (far * 2 + half) * (width // features // 2) + chunk
+        rows_to = slice(place * part, (place + 1) * part)
         gain = gain_ref[rows_from, :]
         key_weight[rows_to, :] = (wk_ref[rows_from, :].astype(F32) * gain).astype(BF16)
         gained_ref[rows_to, :] = (wv_ref[rows_from, :].astype(F32) * gain).astype(BF16)
@@ -301,11 +320,12 @@
             jax.ShapeDtypeStruct((rows, 1), F32),
             jax.ShapeDtypeStruct((width, inner), BF16),
             jax.ShapeDtypeStruct((features, tokens), F32),
-            jax.ShapeDtypeStruct((3 * slots,), jnp.int32),
+            jax.ShapeDtypeStruct((groups, 1, slots // groups * BLOCK), F32),
+            jax.ShapeDtypeStruct((slots,), jnp.int32),
             jax.ShapeDtypeStruct((groups + 1,), jnp.int32),
         ),
         in_specs=[SMEM] * 4 + [VMEM] * 7 + [ANY],
-        out_specs=(VMEM,) * 5 + (SMEM,) * 2,
+        out_specs=(VMEM,) * 6 + (SMEM,) * 2,
         scratch_shapes=[
             pltpu.VMEM((width, inner), BF16),
             pltpu.VMEM((tokens, BLOCK), BF16),
@@ -333,58 +353,31 @@
     )
 
 
-def placing_kernel(table_hbm, arrived_hbm, own_hbm, encoded_ref, placed_ref, table_ref, own_ref, buffer, sems):
-    sources, features, rows = buffer.shape
+def placing_kernel(table_ref, arrived_ref, own_ref, encoded_ref, placed_ref):
     groups = placed_ref.shape[0]
     each = placed_ref.shape[2] // BLOCK
-    slots = groups * each
-    copies = [
-        pltpu.make_async_copy(arrived_hbm.at[s], buffer.at[s], sems.at[s]) for s in range(sources)
-    ]
-    table_copy = pltpu.make_async_copy(table_hbm, table_ref, sems.at[sources])
-    own_copy = pltpu.make_async_copy(own_hbm, own_ref, sems.at[sources + 1])
-    table_copy.start()
-    own_copy.start()
-    for copy in copies:
-        copy.start()
-    table_copy.wait()
-    lane = lax.broadcasted_iota(jnp.int32, (16, BLOCK), 1)
-    for d in range(groups):
-        for s in range(each):
-            slot = d * each + s
-            placed_ref[d, features : features + 16, s * BLOCK : (s + 1) * BLOCK] = (
-                jnp.where(lane < table_ref[2 * slots + slot], table_ref[slots + slot], -1).astype(F32).astype(BF16)
-            )
-    own_copy.wait()
     sums = own_ref[...]
-    for s in range(sources):
-        copies[s].wait()
-        sums = sums + buffer[s].astype(F32)
+    for s in range(arrived_ref.shape[0]):
+        sums = sums + arrived_ref[s].astype(F32)
     encoded_ref[...] = sums.astype(BF16)
     for d in range(groups):
         for s in range(each):
             start = pl.multiple_of(table_ref[d * each + s] * BLOCK, BLOCK)
-            placed_ref[d, 0:features, s * BLOCK : (s + 1) * BLOCK] = encoded_ref[:, pl.ds(start, BLOCK)]
+            placed_ref[d, :, s * BLOCK : (s + 1) * BLOCK] = encoded_ref[:, pl.ds(start, BLOCK)]
 
 
 def placing(table, arrived, own, groups):
-    sources, features, rows = arrived.shape
-    each = table.shape[0] // 3 // groups
+    _, features, rows = arrived.shape
+    each = table.shape[0] // groups
     return pl.pallas_call(
         placing_kernel,
         out_shape=(
             jax.ShapeDtypeStruct((features, rows), BF16),
-            jax.ShapeDtypeStruct((groups, features + 16, each * BLOCK), BF16),
+            jax.ShapeDtypeStruct((groups, features, each * BLOCK), BF16),
         ),
-        in_specs=[ANY, ANY, ANY],
+        in_specs=[SMEM, VMEM, VMEM],
         out_specs=(VMEM, VMEM),
-        scratch_shapes=[
-            pltpu.SMEM(table.shape, jnp.int32),
-            pltpu.VMEM(own.shape, F32),
-            pltpu.VMEM(arrived.shape, BF16),
-            pltpu.SemaphoreType.DMA((sources + 2,)),
-        ],
-        compiler_params=pltpu.CompilerParams(vmem_limit_bytes=VMEM_ALL),
+        compiler_params=pltpu.CompilerParams(vmem_limit_bytes=VMEM_PLACING),
         name="placing",
     )(table, arrived, own)
 
@@ -393,72 +386,136 @@
 TOGETHER = 4
 
 
+def stacked(pieces, e):
+    chunks, _, part, span = pieces[0].shape
+    return jnp.concatenate([piece[:, e].reshape(chunks * part, span) for piece in pieces], axis=0)
+
+
+def square_sums(pieces, e):
+    chunks, _, part, span = pieces[0].shape
+    squares = jnp.zeros((8, span), F32)
+    for piece in pieces:
+        for j in range(chunks):
+            values = piece[j, e].astype(F32)
+            squares = squares + jnp.sum((values * values).reshape(part // 8, 8, span), axis=0)
+    return squares
+
+
+def tile_spot(i):
+    return pl.ds(pl.multiple_of(i * ROW_TILE, ROW_TILE), ROW_TILE)
+
+
+def near_kernel(start_ref, query_ref, low_ref, high_ref, score_ref, square_ref, work_ref):
+    heads, rows, _ = query_ref.shape
+    groups = low_ref.shape[1]
+    near = 2 * low_ref.shape[0] * low_ref.shape[2]
+    flat = heads * ROW_TILE
+    room = (work_ref.shape[0] - 1) // 2
+    pieces = (low_ref, high_ref)
+
+    def listed(e, count):
+        first = start_ref[e] // ROW_TILE
+        last = jnp.where(start_ref[e + 1] > start_ref[e], (start_ref[e + 1] + ROW_TILE - 1) // ROW_TILE, first)
+
+        def note(i, at):
+            work_ref[at] = e
+            work_ref[room + at] = i
+            return at + 1
+
+        return lax.fori_loop(first, last, note, count)
+
+    items = lax.fori_loop(0, groups, listed, jnp.int32(0))
+    for extra in range(TOGETHER - 1):
+        work_ref[items + extra] = work_ref[items - 1]
+        work_ref[room + items + extra] = work_ref[room + items - 1]
+    work_ref[2 * room] = (items + TOGETHER - 1) // TOGETHER
+
+    @pl.loop(0, groups)
+    def _(e):
+        square_ref[e] = square_sums(pieces, e)
+
+    @pl.loop(0, work_ref[2 * room])
+    def _(n):
+        for a in range(TOGETHER):
+            e, i = work_ref[n * TOGETHER + a], work_ref[room + n * TOGETHER + a]
+            query = query_ref[:, tile_spot(i), 0:near].reshape(flat, near)
+            score_ref[n * TOGETHER + a] = dot(query, stacked(pieces, e))
+
+
+def work_room(rows, groups):
+    return rows // ROW_TILE + groups + TOGETHER
+
+
+def near_scores(starts, queries, low, high):
+    heads, rows, width = queries.shape
+    groups, span = low.shape[1], low.shape[3]
+    flat = heads * ROW_TILE
+    most = rows // ROW_TILE + groups - 1
+    most = -(-most // TOGETHER) * TOGETHER
+    return pl.pallas_call(
+        near_kernel,
+        out_shape=(
+            jax.ShapeDtypeStruct((most, flat, span), F32),
+            jax.ShapeDtypeStruct((groups, 8, span), F32),
+            jax.ShapeDtypeStruct((2 * work_room(rows, groups) + 1,), jnp.int32),
+        ),
+        in_specs=[SMEM] + [VMEM] * 3,
+        out_specs=(VMEM, VMEM, SMEM),
+        compiler_params=pltpu.CompilerParams(vmem_limit_bytes=VMEM_NEAR),
+        cost_estimate=pl.CostEstimate(
+            flops=most * flat * span * width, bytes_accessed=4 * most * flat * span, transcendentals=0
+        ),
+        name="near_scores",
+    )(starts, queries, low, high)
+
+
 def cross_kernel(
-    start_hbm,
+    work_hbm,
     query_ref,
+    score_ref,
+    square_ref,
     id_ref,
     key_id_ref,
     back_ref,
     low_ref,
+    high_ref,
     low_far_ref,
-    high_ref,
     high_far_ref,
     wv_ref,
     wo_ref,
     out_hbm,
     out_ref,
-    start_ref,
+    work_ref,
     key_scale,
     mixed,
     context,
-    item_group,
-    item_tile,
     sems,
 ):
-    start_copy = pltpu.make_async_copy(start_hbm, start_ref, sems.at[0])
-    start_copy.start()
+    work_copy = pltpu.make_async_copy(work_hbm, work_ref, sems.at[0])
+    work_copy.start()
     heads, rows, width = query_ref.shape
     chunks, groups, part, span = low_ref.shape
-    pieces = (low_ref, low_far_ref, high_ref, high_far_ref)
-
-    def keys(e):
-        return jnp.concatenate([piece[:, e].reshape(chunks * part, span) for piece in pieces], axis=0)
+    near = 2 * chunks * part
+    room = (work_ref.shape[0] - 1) // 2
+    pieces = (low_ref, high_ref, low_far_ref, high_far_ref)
 
     @pl.loop(0, groups)
     def _(e):
-        squares = jnp.zeros((8, span), F32)
-        for piece in pieces:
-            for j in range(chunks):
-                values = piece[j, e].astype(F32)
-                squares = squares + jnp.sum((values * values).reshape(part // 8, 8, span), axis=0)
+        squares = square_ref[e] + square_sums(pieces[2:], e)
         total = jnp.sum(squares, axis=0, keepdims=True)
         key_scale[e] = lax.rsqrt(total / width + EPSILON)
 
-    start_copy.wait()
+    work_copy.wait()
     flat = heads * ROW_TILE
 
-    def listed(e, count):
-        first = start_ref[e] // ROW_TILE
-        last = jnp.where(start_ref[e + 1] > start_ref[e], (start_ref[e + 1] + ROW_TILE - 1) // ROW_TILE, first)
-
-        def note(i, at):
-            item_group[at] = e
-            item_tile[at] = i
-            return at + 1
-
-        return lax.fori_loop(first, last, note, count)
-
-    items = lax.fori_loop(0, groups, listed, jnp.int32(0))
-    for extra in range(TOGETHER - 1):
-        item_group[items + extra] = item_group[items - 1]
-        item_tile[items + extra] = item_tile[items - 1]
-
-    @pl.loop(0, (items + TOGETHER - 1) // TOGETHER)
+    @pl.loop(0, work_ref[2 * room])
     def _(n):
-        todo = [(item_group[n * TOGETHER + a], item_tile[n * TOGETHER + a]) for a in range(TOGETHER)]
-        spots = [pl.ds(pl.multiple_of(i * ROW_TILE, ROW_TILE), ROW_TILE) for _, i in todo]
+        numbers = [n * TOGETHER + a for a in range(TOGETHER)]
+        todo = [(work_ref[at], work_ref[room + at]) for at in numbers]
+        spots = [tile_spot(i) for _, i in todo]
         scores = [
-            dot(query_ref[:, at, :].reshape(flat, width), keys(e)) for (e, _), at in zip(todo, spots)
+            dot(query_ref[:, at, near:].reshape(flat, width - near), stacked(pieces[2:], e)) + score_ref[number]
+            for (e, _), at, number in zip(todo, spots, numbers)
         ]
         weights = []
         for (e, _), at, raw in zip(todo, spots, scores):
@@ -469,7 +526,7 @@
             expo = jnp.exp2(raw - jnp.max(raw, axis=2, keepdims=True))
             share = 1.0 / jnp.sum(expo, axis=2, keepdims=True)
             weights.append((expo * scale[None] * share).astype(BF16).reshape(flat, span))
-        spreads = [dot_t(w, keys(e)) for w, (e, _) in zip(weights, todo)]
+        spreads = [dot_t(w, stacked(pieces, e)) for w, (e, _) in zip(weights, todo)]
         for (e, _), at, spread in zip(todo, spots, spreads):
             ids = id_ref[at, :]
             mine = (ids >= (e * 4).astype(F32)) & (ids < (e * 4 + 4).astype(F32))
@@ -493,24 +550,21 @@
         store.wait()
 
 
-def cross(starts, queries, ids, key_ids, back, pieces, wv, wo):
+def cross(work, queries, scores, squares, ids, key_ids, back, pieces, wv, wo):
     heads, rows, width = queries.shape
     groups, span = key_ids.shape[0], key_ids.shape[2]
     inner = wv.shape[1]
-    items = rows // ROW_TILE + groups + TOGETHER
     return pl.pallas_call(
         cross_kernel,
         out_shape=jax.ShapeDtypeStruct((rows, width), BF16),
-        in_specs=[ANY] + [VMEM] * 10,
+        in_specs=[ANY] + [VMEM] * 12,
         out_specs=ANY,
         scratch_shapes=[
             pltpu.VMEM((rows, width), BF16),
-            pltpu.SMEM(starts.shape, jnp.int32),
+            pltpu.SMEM(work.shape, jnp.int32),
             pltpu.VMEM((groups, 1, span), F32),
             pltpu.VMEM((heads, rows, width), BF16),
             pltpu.VMEM((rows, inner), BF16),
-            pltpu.SMEM((items,), jnp.int32),
-            pltpu.SMEM((items,), jnp.int32),
             pltpu.SemaphoreType.DMA((3,)),
         ],
         compiler_params=pltpu.CompilerParams(vmem_limit_bytes=VMEM_LIMIT),
@@ -518,7 +572,7 @@
             flops=8 * rows * width * inner, bytes_accessed=2 * groups * width * span, transcendentals=rows * span * heads
         ),
         name="cross",
-    )(starts, queries, ids, key_ids, back, *pieces, wv, wo)
+    )(work, queries, scores, squares, ids, key_ids, back, *pieces, wv, wo)
 
 
 def exchange(x, groups, tensor, half, step):
@@ -536,7 +590,7 @@
         got = [exchange(halves[h], groups, tensor, h, step) for h in range(2)]
         halves = [jnp.concatenate([halves[h], got[h]], axis=0) for h in range(2)]
     got = [exchange(halves[h], groups, tensor, h, 3) for h in range(2)]
-    return halves[0], got[0], halves[1], got[1]
+    return halves, got
 
 
 def origin_masks():
@@ -584,8 +638,8 @@
     arrived = lax.all_to_all(
         partial_sums.reshape(tensor, slice_width, rows), "tensor", split_axis=0, concat_axis=0, tiled=True
     )
-    where = jnp.stack([tensor_index, dp_index % 2]).astype(jnp.int32)
-    queries, back, sorted_ids, gained_value, own, table, starts = query_side(
+    where = jnp.stack([tensor_index, dp_index % 2, dp_index]).astype(jnp.int32)
+    queries, back, sorted_ids, gained_value, own, key_ids, table, starts = query_side(
         block_protein,
         protein_length,
         decoder_group,
@@ -605,9 +659,11 @@
     arrived, own, queries = lax.optimization_barrier((arrived, own, queries))
     encoded, placed = placing(table, arrived, own, groups)
     received = lax.all_to_all(placed, "dp", split_axis=0, concat_axis=0, tiled=True)
-    pieces = gathered(received[:, :part], received[:, part : 2 * part], groups, tensor)
-    key_ids = received[:, slice_width : slice_width + 1].astype(F32)
-    outcome = cross(starts, queries, sorted_ids, key_ids, back, pieces, gained_value, cross_out)
+    near, far = gathered(received[:, :part], received[:, part:], groups, tensor)
+    scores, squares, work = near_scores(starts, queries, *near)
+    outcome = cross(
+        work, queries, scores, squares, sorted_ids, key_ids, back, (*near, *far), gained_value, cross_out
+    )
     mixed = lax.all_to_all(
         outcome.reshape(tensor, share, width), "tensor", split_axis=0, concat_axis=0, tiled=True
     )

time: 122 us -> 121 us (level)
  waiting for transfers between devices: 38.4 us -> 33.8 us
  Pallas kernels: 30.2 us -> 32.1 us
  starting transfers between devices: 26 us -> 27.7 us
  local copies, waits for them, and re-layouts: 10.4 us -> 11.9 us
    ppermute x8, waiting for transfers between devices: 26.1 us -> 22.2 us  [exchange(): return lax.ppermute(x, ('dp', 'tensor'), pairs)]
    pallas_call x0 -> x1, Pallas kernels: none -> 3.46 us  [near_scores(): pl.pallas_call(near_kernel, out_shape=(jax.ShapeDtypeStruct((most, flat,...]
    ppermute x8, starting transfers between devices: 13.1 us -> 14.8 us  [exchange(): return lax.ppermute(x, ('dp', 'tensor'), pairs)]
    unnamed x36 -> x40, local copies, waits for them, and re-layouts: 10.4 us -> 11.9 us
  transfers between devices with their start and end apart: 10 -> 10, of which waited for: 9 -> 9; matrix products, arithmetic and copies ran while one was open for 1% -> 1% of each run, Pallas kernels for 5% -> 8%
where the time goes in v4:
time: 121 us
  waiting for transfers between devices  33.8 us (28%)
  Pallas kernels  32.1 us (27%)
  starting transfers between devices  27.7 us (23%)
  blocking collectives  12.6 us (10%)
  local copies, waits for them, and re-layouts  11.9 us (10%)
  other arithmetic  2.01 us (2%)
    ppermute x8, waiting for transfers between devices, exchange(): return lax.ppermute(x, ('dp', 'tensor'), pairs)  22.2 us
    ppermute x8, starting transfers between devices, exchange(): return lax.ppermute(x, ('dp', 'tensor'), pairs)  14.8 us
    all_to_all x1, blocking collectives, body(): lax.all_to_all(placed, 'dp', split_axis=0, concat_axis=0, tiled=True)  12.6 us
    pallas_call x1, Pallas kernels, cross(): pl.pallas_call(cross_kernel, out_shape=jax.ShapeDtypeStruct((rows, width)...  11.9 us
    unnamed x40, local copies, waits for them, and re-layouts  11.9 us
    all_to_all x1, waiting for transfers between devices, body(): lax.all_to_all(outcome.reshape(tensor, share, width), 'tensor', split_axi...  10.8 us
    pallas_call x1, Pallas kernels, encoder(): pl.pallas_call(encoder_kernel, out_shape=jax.ShapeDtypeStruct((width, row...  9.59 us
    all_to_all x1, starting transfers between devices, body(): lax.all_to_all(partial_sums.reshape(tensor, slice_width, rows), 'tensor',...  7.29 us
  transfers between devices with their start and end apart: 10, of which 9 were waited for; matrix products, arithmetic and copies ran while one was open for 1% of the time, Pallas kernels for 8%

profile of v4, /device:TPU:0, one launch (start us, length us, event | category | flops | bytes accessed | tf_op | source)
XLA Modules:
  0.0 120.9 jit_solution(8127772786254574706)
XLA Ops:
  0.6 9.6 %encoder.1 = bf16[1024,512]{1,0:T(8,128)(2,1)} custom-call(s32[4]{0:T(128)} %protein_hbm.1, s32[32]{0:T(128)} %length_hbm.1, bf16[512,1024]{1,0:T(8,128)(2,1)} %residue_hbm.3, f32[1,1024]{1,0:T(1,128)} %bitcast.17, bf16[1024,1024]{1,0:T(8,128)(2,1)} %wq_hbm.1, bf16[1024,1024]{1,0:T(8,128)(2,1)} %wk_hbm.1, bf16[1024,1024]{1,0:T(8,128)(2,1)} %wv_hbm.1, ...), custom_call_target="tpu_custom_call" | custom-call | flops 4294967296 | bytes 8388608 | tf_op jit(solution)/shard_map/encoder/pallas_call | solution.py:163
  10.2 0.0 copy-start.19
  10.2 0.0 copy-start.2
  10.3 0.0 copy-start.14
  10.3 0.0 copy-start.15
  10.3 0.0 copy-start.16
  10.3 0.0 copy-start.18
  10.3 7.3 %all-to-all-start = ((bf16[16,64,512]{2,1,0:T(8,128)(2,1)}), bf16[16,64,512]{2,1,0:T(8,128)(2,1)S(1)}, u32[]{:S(2)}, u32[]{:S(2)}) async-start(bf16[16,64,512]{2,1,0:T(8,128)(2,1)} %bitcast.15), calls=%async_computation | async-start | bytes 2097152 | tf_op jit(solution)/shard_map/all_to_all | solution.py:638
  17.6 0.1 pad_add_fusion.where_ref
  17.8 1.6 %copy-done.3 = bf16[1024,1024]{1,0:T(8,128)(2,1)S(1)} copy-done((bf16[1024,1024]{1,0:T(8,128)(2,1)S(1)}, bf16[1024,1024]{1,0:T(8,128)(2,1)}, u32[]{:S(2)}) %copy-start.3) | copy-done | bytes 2097176
  19.4 1.6 %copy-done.4 = bf16[1024,1024]{1,0:T(8,128)(2,1)S(1)} copy-done((bf16[1024,1024]{1,0:T(8,128)(2,1)S(1)}, bf16[1024,1024]{1,0:T(8,128)(2,1)}, u32[]{:S(2)}) %copy-start.4) | copy-done | bytes 2097176
  21.0 1.2 %copy-done.8 = bf16[512,1024]{1,0:T(8,128)(2,1)S(1)} copy-done((bf16[512,1024]{1,0:T(8,128)(2,1)S(1)}, bf16[512,1024]{1,0:T(8,128)(2,1)}, u32[]{:S(2)}) %copy-start.8) | copy-done | bytes 1048600
  22.2 1.1 copy-done.9
  23.3 5.8 %query_side.1 = (bf16[8,384,1024]{2,1,0:T(8,128)(2,1)S(1)}, bf16[384,384]{1,0:T(8,128)(2,1)S(1)}, f32[384,1]{1,0:T(8,128)S(1)}, bf16[1024,1024]{1,0:T(8,128)(2,1...) custom-call(s32[4]{0:T(128)S(1)} %copy-done.16, s32[32]{0:T(128)S(1)} %copy-done.17, ...), custom_call_target="tpu_custom_call" | custom-call | flops 1610612736 | bytes 12582912 | tf_op jit(solution)/shard_map/query_side/pallas_call | solution.py:315
  29.1 2.6 %copy-done = bf16[8,384,1024]{2,1,0:T(8,128)(2,1)} copy-done((bf16[8,384,1024]{2,1,0:T(8,128)(2,1)}, bf16[8,384,1024]{2,1,0:T(8,128)(2,1)S(1)}, u32[]{:S(2)}) %copy-start) | copy-done | bytes 6291480
  31.8 1.4 %copy-done.6 = bf16[1024,1024]{1,0:T(8,128)(2,1)} copy-done((bf16[1024,1024]{1,0:T(8,128)(2,1)}, bf16[1024,1024]{1,0:T(8,128)(2,1)S(1)}, u32[]{:S(2)}) %copy-start.6) | copy-done | bytes 2097176
  33.2 0.7 copy-done.10
  33.8 0.6 copy-done.12
  34.5 0.8 all-to-all-done.arrived_ref
  35.3 0.9 copy-done.13
  36.2 1.3 %placing.1 = (bf16[64,512]{1,0:T(8,128)(2,1)}, bf16[8,64,256]{2,1,0:T(8,128)(2,1)S(1)}) custom-call(s32[16]{0:T(128)S(1)} %get-tuple-element.20.table_ref, bf16[16,64,512]{2,1,0:T(8,128)(2,1)S(1)} %all-to-all-done.arrived_ref, f32[64,512]{1,0:T(8,128)S(1)} %copy-done.13), custom_call_target="tpu_custom_call" | custom-call | tf_op jit(solution)/shard_map/placing/pallas_call | solution.py:372
  37.5 12.6 %all_to_all.15 = bf16[8,64,256]{2,1,0:T(8,128)(2,1)S(1)} all-to-all(bf16[8,64,256]{2,1,0:T(8,128)(2,1)S(1)} %get-tuple-element.28), channel_id=1, replica_groups=mesh['dp'=8,'tensor'=16] {'dp'}, dimensions={0} | all-to-all | bytes 524288 | tf_op jit(solution)/shard_map/all_to_all | solution.py:661
  50.2 1.2 %collective-permute-start = (bf16[1,8,32,256]{3,2,1,0:T(8,128)(2,1)S(1)}, bf16[1,8,32,256]{3,2,1,0:T(8,128)(2,1)S(1)}, u32[]{:S(2)}, u32[]{:S(2)}) collective-permute-start(bf16[1,8,32,256]{3,2,1,0:T(8,128)(2,1)S(1)} %get-tuple-element.39), channel_id=1, source_target_pairs={{0,1},{1,0},{2,3},{3,2},{4,5},{5,4},{6,7},{7,6},{8,9},{9,8},{10,11... | collective-permute-start | bytes 393224 | tf_op jit(solution)/shard_map/ppermute | solution.py:584
  51.4 2.1 %collective-permute-start.3 = (bf16[1,8,32,256]{3,2,1,0:T(8,128)(2,1)S(1)}, bf16[1,8,32,256]{3,2,1,0:T(8,128)(2,1)S(1)}, u32[]{:S(2)}, u32[]{:S(2)}) collective-permute-start(bf16[1,8,32,256]{3,2,1,0:T(8,128)(2,1)S(1)} %get-tuple-element.38), channel_id=1, source_target_pairs={{0,3},{1,2},{2,1},{3,0},{4,7},{5,6},{6,5},{7,4},{8,11},{9,10},{10,... | collective-permute-start | bytes 393224 | tf_op jit(solution)/shard_map/ppermute | solution.py:584
  53.4 1.8 %collective-permute-done = bf16[1,8,32,256]{3,2,1,0:T(8,128)(2,1)S(1)} collective-permute-done((bf16[1,8,32,256]{3,2,1,0:T(8,128)(2,1)S(1)}, bf16[1,8,32,256]{3,2,1,0:T(8,128)(2,1)S(1)}, u32[]{:S(2)}, u32[]{:S(2)}) %collective-permute-start) | collective-permute-done | bytes 131104 | tf_op jit(solution)/shard_map/ppermute | solution.py:584
  55.2 2.4 %collective-permute-start.1 = (bf16[2,8,32,256]{3,2,1,0:T(8,128)(2,1)S(1)}, bf16[2,8,32,256]{3,2,1,0:T(8,128)(2,1)S(1)}, u32[]{:S(2)}, u32[]{:S(2)}) collective-permute-start(bf16[2,8,32,256]{3,2,1,0:T(8,128)(2,1)S(1)} %pad_maximum_fusion.4), channel_id=1, source_target_pairs={{0,3},{1,2},{2,1},{3,0},{4,7},{5,6},{6,5},{7,4},{8,11},{9,10},{10,... | collective-permute-start | bytes 786440 | tf_op jit(solution)/shard_map/ppermute | solution.py:584
  57.7 0.5 collective-permute-start.4
  58.2 4.7 %collective-permute-done.1 = bf16[2,8,32,256]{3,2,1,0:T(8,128)(2,1)S(1)} collective-permute-done((bf16[2,8,32,256]{3,2,1,0:T(8,128)(2,1)S(1)}, bf16[2,8,32,256]{3,2,1,0:T(8,128)(2,1)S(1)}, u32[]{:S(2)}, u32[]{:S(2)}) %collective-permute-start.1) | collective-permute-done | bytes 262176 | tf_op jit(solution)/shard_map/ppermute | solution.py:584
  62.9 0.1 pad_maximum_fusion.2
  63.0 1.2 collective-permute-start.2
  64.2 1.4 %collective-permute-done.4 = bf16[2,8,32,256]{3,2,1,0:T(8,128)(2,1)S(1)} collective-permute-done((bf16[2,8,32,256]{3,2,1,0:T(8,128)(2,1)S(1)}, bf16[2,8,32,256]{3,2,1,0:T(8,128)(2,1)S(1)}, u32[]{:S(2)}, u32[]{:S(2)}) %collective-permute-start.4) | collective-permute-done | bytes 262176 | tf_op jit(solution)/shard_map/ppermute | solution.py:584
  65.6 0.1 pad_maximum_fusion.3
  65.6 3.1 %collective-permute-start.5 = (bf16[4,8,32,256]{3,2,1,0:T(8,128)(2,1)S(1)}, bf16[4,8,32,256]{3,2,1,0:T(8,128)(2,1)S(1)}, u32[]{:S(2)}, u32[]{:S(2)}) collective-permute-start(bf16[4,8,32,256]{3,2,1,0:T(8,128)(2,1)S(1)} %pad_maximum_fusion.3), channel_id=1, source_target_pairs={{0,12},{1,13},{2,14},{3,15},{4,8},{5,9},{6,10},{7,11},{8,4},{9,5},... | collective-permute-start | bytes 1572872 | tf_op jit(solution)/shard_map/ppermute | solution.py:584
  68.7 3.5 %collective-permute-done.2 = bf16[4,8,32,256]{3,2,1,0:T(8,128)(2,1)S(1)} collective-permute-done((bf16[4,8,32,256]{3,2,1,0:T(8,128)(2,1)S(1)}, bf16[4,8,32,256]{3,2,1,0:T(8,128)(2,1)S(1)}, u32[]{:S(2)}, u32[]{:S(2)}) %collective-permute-start.2) | collective-permute-done | bytes 524320 | tf_op jit(solution)/shard_map/ppermute | solution.py:584
  72.2 0.1 pad_maximum_fusion.low_ref
  72.3 2.4 %collective-permute-start.6 = (bf16[8,8,32,256]{3,2,1,0:T(8,128)(2,1)S(1)}, bf16[8,8,32,256]{3,2,1,0:T(8,128)(2,1)S(1)}, u32[]{:S(2)}, u32[]{:S(2)}) collective-permute-start(bf16[8,8,32,256]{3,2,1,0:T(8,128)(2,1)S(1)} %pad_maximum_fusion.low_ref), channel_id=1, source_target_pairs={{0,12},{1,13},{2,14},{3,15},{4,8},{5,9},{6,10},{7,11},{8,4},{9,5},... | collective-permute-start | bytes 3145736 | tf_op jit(solution)/shard_map/ppermute | solution.py:584
  74.8 1.3 %collective-permute-done.5 = bf16[4,8,32,256]{3,2,1,0:T(8,128)(2,1)S(1)} collective-permute-done((bf16[4,8,32,256]{3,2,1,0:T(8,128)(2,1)S(1)}, bf16[4,8,32,256]{3,2,1,0:T(8,128)(2,1)S(1)}, u32[]{:S(2)}, u32[]{:S(2)}) %collective-permute-start.5) | collective-permute-done | bytes 524320 | tf_op jit(solution)/shard_map/ppermute | solution.py:584
  76.1 0.1 pad_maximum_fusion.1.high_ref
  76.2 1.9 %collective-permute-start.7 = (bf16[8,8,32,256]{3,2,1,0:T(8,128)(2,1)S(1)}, bf16[8,8,32,256]{3,2,1,0:T(8,128)(2,1)S(1)}, u32[]{:S(2)}, u32[]{:S(2)}) collective-permute-start(bf16[8,8,32,256]{3,2,1,0:T(8,128)(2,1)S(1)} %pad_maximum_fusion.1.high_ref), channel_id=1, source_target_pairs={{0,4},{1,5},{2,6},{3,7},{4,0},{5,1},{6,2},{7,3},{8,12},{9,13},{10,... | collective-permute-start | bytes 3145736 | tf_op jit(solution)/shard_map/ppermute | solution.py:584
  78.1 3.5 %near_scores.1 = (f32[20,256,256]{2,1,0:T(8,128)S(1)}, f32[8,8,256]{2,1,0:T(8,128)S(1)}, s32[49]{0:T(128)S(1)}) custom-call(s32[9]{0:T(128)S(1)} %get-tuple-element.26.start_ref, bf16[8,384,1024]{2,1,0:T(8,128)(2,1)S(1)} %copy-done.1, bf16[8,8,32,256]{3,2,1,0:T(8,128)(2,1)S(1)} %pad_maximum_fusion.low_ref, bf16[8,8,32,256]{3,2,1,0:T(8,128)(2,1)S(1)} %pad_maximum_fusion.1.high_ref), custom_call_target="tpu_custom_call" | custom-call | flops 1342177280 | bytes 5242880 | tf_op jit(solution)/shard_map/near_scores/pallas_call | solution.py:455
  81.6 6.8 %collective-permute-done.6.low_far_ref = bf16[8,8,32,256]{3,2,1,0:T(8,128)(2,1)S(1)} collective-permute-done((bf16[8,8,32,256]{3,2,1,0:T(8,128)(2,1)S(1)}, bf16[8,8,32,256]{3,2,1,0:T(8,128)(2,1)S(1)}, u32[]{:S(2)}, u32[]{:S(2)}) %collective-permute-start.6) | collective-permute-done | bytes 1048608 | tf_op jit(solution)/shard_map/ppermute | solution.py:584
  88.4 2.7 %collective-permute-done.7.high_far_ref = bf16[8,8,32,256]{3,2,1,0:T(8,128)(2,1)S(1)} collective-permute-done((bf16[8,8,32,256]{3,2,1,0:T(8,128)(2,1)S(1)}, bf16[8,8,32,256]{3,2,1,0:T(8,128)(2,1)S(1)}, u32[]{:S(2)}, u32[]{:S(2)}) %collective-permute-start.7) | collective-permute-done | bytes 1048608 | tf_op jit(solution)/shard_map/ppermute | solution.py:584
  91.1 11.9 %cross.1 = bf16[384,1024]{1,0:T(8,128)(2,1)} custom-call(s32[49]{0:T(128)S(1)} %get-tuple-element.29.work_hbm, bf16[8,384,1024]{2,1,0:T(8,128)(2,1)S(1)} %copy-done.1, f32[20,256,256]{2,1,0:T(8,128)S(1)} %get-tuple-element.30.score_ref, f32[8,8,256]{2,1,0:T(8,128)S(1)} %get-tuple-element.31.square_ref, f32[384,1]{1,0:T(8,128)S(1)} %copy-done.11, ...), custom_call_target="tpu_custom_call" | custom-call | flops 3221225472 | bytes 4194304 | tf_op jit(solution)/shard_map/cross/pallas_call | solution.py:557
  103.0 5.6 %all-to-all-start.2 = ((bf16[16,24,1024]{2,1,0:T(8,128)(2,1)}), bf16[16,24,1024]{2,1,0:T(8,128)(2,1)S(1)}, u32[]{:S(2)}, u32[]{:S(2)}) async-start(bf16[16,24,1024]{2,1,0:T(8,128)(2,1)} %bitcast.10), calls=%async_computation.2 | async-start | bytes 1572864 | tf_op jit(solution)/shard_map/all_to_all | solution.py:667
  108.6 0.8 dynamic-slice_convert_fusion
  109.4 10.8 %all-to-all-done.2 = bf16[16,24,1024]{2,1,0:T(8,128)(2,1)S(1)} async-done(((bf16[16,24,1024]{2,1,0:T(8,128)(2,1)}), bf16[16,24,1024]{2,1,0:T(8,128)(2,1)S(1)}, u32[]{:S(2)}, u32[]{:S(2)}) %all-to-all-start.2) | async-done | bytes 786464 | tf_op jit(solution)/shard_map/all_to_all | solution.py:667
  120.2 0.1 convert_reduce_fusion
  120.3 0.6 add_convert_fusion
  (30 shorter events, 0.1 us)
Async XLA Ops:
  10.2 7.4 %copy-start.19 = (s32[384]{0:T(512)S(1)}, s32[384]{0:T(512)}, u32[]{:S(2)}) copy-start(s32[384]{0:T(512)} %param.27) | copy-start | bytes 4612
  10.2 7.5 %copy-start.2 = (bf16[1024,1024]{1,0:T(8,128)(2,1)S(1)}, bf16[1024,1024]{1,0:T(8,128)(2,1)}, u32[]{:S(2)}) copy-start(bf16[1024,1024]{1,0:T(8,128)(2,1)} %wq_ref.1) | copy-start | bytes 6291460
  10.3 7.5 %copy-start.14 = (f32[1024]{0:T(1024)S(1)}, f32[1024]{0:T(1024)}, u32[]{:S(2)}) copy-start(f32[1024]{0:T(1024)} %param.28) | copy-start | bytes 12292
  10.3 7.5 %copy-start.15 = (f32[1024]{0:T(1024)S(1)}, f32[1024]{0:T(1024)}, u32[]{:S(2)}) copy-start(f32[1024]{0:T(1024)} %param.29) | copy-start | bytes 12292
  10.3 7.5 %copy-start.16 = (s32[4]{0:T(128)S(1)}, s32[4]{0:T(128)}, u32[]{:S(2)}) copy-start(s32[4]{0:T(128)} %protein_hbm.1) | copy-start | bytes 52
  10.3 7.5 %copy-start.17 = (s32[32]{0:T(128)S(1)}, s32[32]{0:T(128)}, u32[]{:S(2)}) copy-start(s32[32]{0:T(128)} %length_hbm.1) | copy-start | bytes 388
  10.3 7.5 %copy-start.18 = (s32[32]{0:T(128)S(1)}, s32[32]{0:T(128)}, u32[]{:S(2)}) copy-start(s32[32]{0:T(128)} %group_ref.1) | copy-start | bytes 388
  10.3 25.0 %all-to-all-start = ((bf16[16,64,512]{2,1,0:T(8,128)(2,1)}), bf16[16,64,512]{2,1,0:T(8,128)(2,1)S(1)}, u32[]{:S(2)}, u32[]{:S(2)}) async-start(bf16[16,64,512]{2,1,0:T(8,128)(2,1)} %bitcast.15), calls=%async_computation | async-start | bytes 2097152 | tf_op jit(solution)/shard_map/all_to_all | solution.py:638
  17.8 1.6 %copy-start.3 = (bf16[1024,1024]{1,0:T(8,128)(2,1)S(1)}, bf16[1024,1024]{1,0:T(8,128)(2,1)}, u32[]{:S(2)}) copy-start(bf16[1024,1024]{1,0:T(8,128)(2,1)} %wk_ref.1) | copy-start | bytes 6291460
  19.4 1.6 %copy-start.4 = (bf16[1024,1024]{1,0:T(8,128)(2,1)S(1)}, bf16[1024,1024]{1,0:T(8,128)(2,1)}, u32[]{:S(2)}) copy-start(bf16[1024,1024]{1,0:T(8,128)(2,1)} %wv_ref.1) | copy-start | bytes 6291460
  21.0 1.2 %copy-start.8 = (bf16[512,1024]{1,0:T(8,128)(2,1)S(1)}, bf16[512,1024]{1,0:T(8,128)(2,1)}, u32[]{:S(2)}) copy-start(bf16[512,1024]{1,0:T(8,128)(2,1)} %residue_hbm.3) | copy-start | bytes 3145732
  22.2 1.1 copy-start.9
  29.1 2.6 %copy-start = (bf16[8,384,1024]{2,1,0:T(8,128)(2,1)}, bf16[8,384,1024]{2,1,0:T(8,128)(2,1)S(1)}, u32[]{:S(2)}) copy-start(bf16[8,384,1024]{2,1,0:T(8,128)(2,1)S(1)} %get-tuple-element.27.query_ref) | copy-start | bytes 18874372
  31.8 1.4 %copy-start.6 = (bf16[1024,1024]{1,0:T(8,128)(2,1)}, bf16[1024,1024]{1,0:T(8,128)(2,1)S(1)}, u32[]{:S(2)}) copy-start(bf16[1024,1024]{1,0:T(8,128)(2,1)S(1)} %get-tuple-element.35.wv_ref) | copy-start | bytes 6291460
  33.2 0.7 copy-start.10
  33.8 0.6 copy-start.12
  35.3 0.9 copy-start.13
  50.2 5.0 %collective-permute-start = (bf16[1,8,32,256]{3,2,1,0:T(8,128)(2,1)S(1)}, bf16[1,8,32,256]{3,2,1,0:T(8,128)(2,1)S(1)}, u32[]{:S(2)}, u32[]{:S(2)}) collective-permute-start(bf16[1,8,32,256]{3,2,1,0:T(8,128)(2,1)S(1)} %get-tuple-element.39), channel_id=1, source_target_pairs={{0,1},{1,0},{2,3},{3,2},{4,5},{5,4},{6,7},{7,6},{8,9},{9,8},{10,11... | collective-permute-start | bytes 393224 | tf_op jit(solution)/shard_map/ppermute | solution.py:584
  51.4 6.3 %collective-permute-start.3 = (bf16[1,8,32,256]{3,2,1,0:T(8,128)(2,1)S(1)}, bf16[1,8,32,256]{3,2,1,0:T(8,128)(2,1)S(1)}, u32[]{:S(2)}, u32[]{:S(2)}) collective-permute-start(bf16[1,8,32,256]{3,2,1,0:T(8,128)(2,1)S(1)} %get-tuple-element.38), channel_id=1, source_target_pairs={{0,3},{1,2},{2,1},{3,0},{4,7},{5,6},{6,5},{7,4},{8,11},{9,10},{10,... | collective-permute-start | bytes 393224 | tf_op jit(solution)/shard_map/ppermute | solution.py:584
  55.2 7.7 %collective-permute-start.1 = (bf16[2,8,32,256]{3,2,1,0:T(8,128)(2,1)S(1)}, bf16[2,8,32,256]{3,2,1,0:T(8,128)(2,1)S(1)}, u32[]{:S(2)}, u32[]{:S(2)}) collective-permute-start(bf16[2,8,32,256]{3,2,1,0:T(8,128)(2,1)S(1)} %pad_maximum_fusion.4), channel_id=1, source_target_pairs={{0,3},{1,2},{2,1},{3,0},{4,7},{5,6},{6,5},{7,4},{8,11},{9,10},{10,... | collective-permute-start | bytes 786440 | tf_op jit(solution)/shard_map/ppermute | solution.py:584
  57.7 7.9 %collective-permute-start.4 = (bf16[2,8,32,256]{3,2,1,0:T(8,128)(2,1)S(1)}, bf16[2,8,32,256]{3,2,1,0:T(8,128)(2,1)S(1)}, u32[]{:S(2)}, u32[]{:S(2)}) collective-permute-start(bf16[2,8,32,256]{3,2,1,0:T(8,128)(2,1)S(1)} %pad_maximum_fusion.5), channel_id=1, source_target_pairs={{0,1},{1,0},{2,3},{3,2},{4,5},{5,4},{6,7},{7,6},{8,9},{9,8},{10,11... | collective-permute-start | bytes 786440 | tf_op jit(solution)/shard_map/ppermute | solution.py:584
  62.9 15.2 %copy-start.1 = (bf16[8,384,1024]{2,1,0:T(8,128)(2,1)S(1)}, bf16[8,384,1024]{2,1,0:T(8,128)(2,1)}, u32[]{:S(2)}) copy-start(bf16[8,384,1024]{2,1,0:T(8,128)(2,1)} %copy-done) | copy-start | bytes 18874372
  63.0 9.3 %collective-permute-start.2 = (bf16[4,8,32,256]{3,2,1,0:T(8,128)(2,1)S(1)}, bf16[4,8,32,256]{3,2,1,0:T(8,128)(2,1)S(1)}, u32[]{:S(2)}, u32[]{:S(2)}) collective-permute-start(bf16[4,8,32,256]{3,2,1,0:T(8,128)(2,1)S(1)} %pad_maximum_fusion.2), channel_id=1, source_target_pairs={{0,4},{1,5},{2,6},{3,7},{4,0},{5,1},{6,2},{7,3},{8,12},{9,13},{10,... | collective-permute-start | bytes 1572872 | tf_op jit(solution)/shard_map/ppermute | solution.py:584
  65.6 10.5 %collective-permute-start.5 = (bf16[4,8,32,256]{3,2,1,0:T(8,128)(2,1)S(1)}, bf16[4,8,32,256]{3,2,1,0:T(8,128)(2,1)S(1)}, u32[]{:S(2)}, u32[]{:S(2)}) collective-permute-start(bf16[4,8,32,256]{3,2,1,0:T(8,128)(2,1)S(1)} %pad_maximum_fusion.3), channel_id=1, source_target_pairs={{0,12},{1,13},{2,14},{3,15},{4,8},{5,9},{6,10},{7,11},{8,4},{9,5},... | collective-permute-start | bytes 1572872 | tf_op jit(solution)/shard_map/ppermute | solution.py:584
  72.3 16.1 %collective-permute-start.6 = (bf16[8,8,32,256]{3,2,1,0:T(8,128)(2,1)S(1)}, bf16[8,8,32,256]{3,2,1,0:T(8,128)(2,1)S(1)}, u32[]{:S(2)}, u32[]{:S(2)}) collective-permute-start(bf16[8,8,32,256]{3,2,1,0:T(8,128)(2,1)S(1)} %pad_maximum_fusion.low_ref), channel_id=1, source_target_pairs={{0,12},{1,13},{2,14},{3,15},{4,8},{5,9},{6,10},{7,11},{8,4},{9,5},... | collective-permute-start | bytes 3145736 | tf_op jit(solution)/shard_map/ppermute | solution.py:584
  76.2 14.9 %collective-permute-start.7 = (bf16[8,8,32,256]{3,2,1,0:T(8,128)(2,1)S(1)}, bf16[8,8,32,256]{3,2,1,0:T(8,128)(2,1)S(1)}, u32[]{:S(2)}, u32[]{:S(2)}) collective-permute-start(bf16[8,8,32,256]{3,2,1,0:T(8,128)(2,1)S(1)} %pad_maximum_fusion.1.high_ref), channel_id=1, source_target_pairs={{0,4},{1,5},{2,6},{3,7},{4,0},{5,1},{6,2},{7,3},{8,12},{9,13},{10,... | collective-permute-start | bytes 3145736 | tf_op jit(solution)/shard_map/ppermute | solution.py:584
  78.1 13.0 %copy-start.5 = (bf16[1024,1024]{1,0:T(8,128)(2,1)S(1)}, bf16[1024,1024]{1,0:T(8,128)(2,1)}, u32[]{:S(2)}) copy-start(bf16[1024,1024]{1,0:T(8,128)(2,1)} %wo_ref.1) | copy-start | bytes 6291460
  78.1 13.0 %copy-start.7 = (bf16[1024,1024]{1,0:T(8,128)(2,1)S(1)}, bf16[1024,1024]{1,0:T(8,128)(2,1)}, u32[]{:S(2)}) copy-start(bf16[1024,1024]{1,0:T(8,128)(2,1)} %copy-done.6) | copy-start | bytes 6291460
  78.1 13.0 %copy-start.11 = (f32[384,1]{1,0:T(8,128)S(1)}, f32[384,1]{1,0:T(8,128)}, u32[]{:S(2)}) copy-start(f32[384,1]{1,0:T(8,128)} %copy-done.10) | copy-start | bytes 4612
  103.0 17.2 %all-to-all-start.2 = ((bf16[16,24,1024]{2,1,0:T(8,128)(2,1)}), bf16[16,24,1024]{2,1,0:T(8,128)(2,1)S(1)}, u32[]{:S(2)}, u32[]{:S(2)}) async-start(bf16[16,24,1024]{2,1,0:T(8,128)(2,1)} %bitcast.10), calls=%async_computation.2 | async-start | bytes 1572864 | tf_op jit(solution)/shard_map/all_to_all | solution.py:667

commit v5 on v4

--- a/solution.py
+++ b/solution.py
@@ -26,7 +26,8 @@
 ANY = pl.BlockSpec(memory_space=pl.ANY)
 
 XA, XB, YA, YB = 1, 3, 4, 12
-ORDERS = (((XA, XB, YA, YB), (XB, XA, YB, YA)), ((YA, YB, XA, XB), (YB, YA, XB, XA)))
+ORDERS = ((XA, XB, YA, YB), (XB, XA, YB, YA), (YA, YB, XA, XB), (YB, YA, XB, XA))
+CHAINS = len(ORDERS)
 
 
 def rms_scaled(x, gain):
@@ -219,7 +220,7 @@
 ):
     rows, width = state_ref.shape
     features = own_ref.shape[0]
-    here, core = where_ref[0], where_ref[1]
+    here = where_ref[0]
     lanes = pl.ds(pl.multiple_of(here * features // BLOCK * BLOCK, BLOCK), BLOCK)
     copy = pltpu.make_async_copy(residue_hbm.at[:, lanes], columns, sem)
     copy.start()
@@ -245,7 +246,7 @@
         for p in range(e * proteins, (e + 1) * proteins):
             size = length_ref[p]
             count = lax.shift_right_logical(size + (BLOCK - 1), 7)
-            wanted = group_ref[p] == where_ref[2]
+            wanted = group_ref[p] == where_ref[1]
             for s in range(each):
                 offset = s - taken
                 here_too = wanted & (offset >= 0) & (offset < count)
@@ -273,7 +274,7 @@
     normed = dot(chosen.astype(F32).astype(BF16), normed).astype(BF16)
 
     masks = origin_masks()
-    part = features // 2
+    part = features // CHAINS
     gain_parts = [
         as_column(final_gain_ref[:, c * BLOCK : (c + 1) * BLOCK]) for c in range(width // BLOCK)
     ]
@@ -281,13 +282,13 @@
     for c, gain in enumerate(gain_parts):
         gain_ref[c * BLOCK : (c + 1) * BLOCK, :] = gain
     for index in range(width // part):
-        origin = here ^ jnp.where(core == 0, int(masks[0, index]), int(masks[1, index]))
+        origin = here ^ int(masks[index])
         rows_from = pl.ds(
             pl.multiple_of(origin * features + index // (width // features) * part, part), part
         )
         half, chunk = divmod(index, width // features)
         far, chunk = divmod(chunk, width // features // 2)
-        place = (far * 2 + half) * (width // features // 2) + chunk
+        place = (far * CHAINS + half) * (width // features // 2) + chunk
         rows_to = slice(place * part, (place + 1) * part)
         gain = gain_ref[rows_from, :]
         key_weight[rows_to, :] = (wk_ref[rows_from, :].astype(F32) * gain).astype(BF16)
@@ -405,13 +406,13 @@
     return pl.ds(pl.multiple_of(i * ROW_TILE, ROW_TILE), ROW_TILE)
 
 
-def near_kernel(start_ref, query_ref, low_ref, high_ref, score_ref, square_ref, work_ref):
+def near_kernel(start_ref, query_ref, *refs):
+    pieces, (score_ref, square_ref, work_ref) = refs[:CHAINS], refs[CHAINS:]
     heads, rows, _ = query_ref.shape
-    groups = low_ref.shape[1]
-    near = 2 * low_ref.shape[0] * low_ref.shape[2]
+    groups = pieces[0].shape[1]
+    near = CHAINS * pieces[0].shape[0] * pieces[0].shape[2]
     flat = heads * ROW_TILE
     room = (work_ref.shape[0] - 1) // 2
-    pieces = (low_ref, high_ref)
 
     def listed(e, count):
         first = start_ref[e] // ROW_TILE
@@ -446,9 +447,9 @@
     return rows // ROW_TILE + groups + TOGETHER
 
 
-def near_scores(starts, queries, low, high):
+def near_scores(starts, queries, pieces):
     heads, rows, width = queries.shape
-    groups, span = low.shape[1], low.shape[3]
+    groups, span = pieces[0].shape[1], pieces[0].shape[3]
     flat = heads * ROW_TILE
     most = rows // ROW_TILE + groups - 1
     most = -(-most // TOGETHER) * TOGETHER
@@ -459,14 +460,14 @@
             jax.ShapeDtypeStruct((groups, 8, span), F32),
             jax.ShapeDtypeStruct((2 * work_room(rows, groups) + 1,), jnp.int32),
         ),
-        in_specs=[SMEM] + [VMEM] * 3,
+        in_specs=[SMEM] + [VMEM] * (1 + CHAINS),
         out_specs=(VMEM, VMEM, SMEM),
         compiler_params=pltpu.CompilerParams(vmem_limit_bytes=VMEM_NEAR),
         cost_estimate=pl.CostEstimate(
             flops=most * flat * span * width, bytes_accessed=4 * most * flat * span, transcendentals=0
         ),
         name="near_scores",
-    )(starts, queries, low, high)
+    )(starts, queries, *pieces)
 
 
 def cross_kernel(
@@ -477,31 +478,22 @@
     id_ref,
     key_id_ref,
     back_ref,
-    low_ref,
-    high_ref,
-    low_far_ref,
-    high_far_ref,
     wv_ref,
     wo_ref,
-    out_hbm,
-    out_ref,
-    work_ref,
-    key_scale,
-    mixed,
-    context,
-    sems,
+    *refs,
 ):
+    pieces, rest = refs[: 2 * CHAINS], refs[2 * CHAINS :]
+    out_hbm, out_ref, work_ref, key_scale, mixed, context, sems = rest
     work_copy = pltpu.make_async_copy(work_hbm, work_ref, sems.at[0])
     work_copy.start()
     heads, rows, width = query_ref.shape
-    chunks, groups, part, span = low_ref.shape
-    near = 2 * chunks * part
+    chunks, groups, part, span = pieces[0].shape
+    near = CHAINS * chunks * part
     room = (work_ref.shape[0] - 1) // 2
-    pieces = (low_ref, high_ref, low_far_ref, high_far_ref)
 
     @pl.loop(0, groups)
     def _(e):
-        squares = square_ref[e] + square_sums(pieces[2:], e)
+        squares = square_ref[e] + square_sums(pieces[CHAINS:], e)
         total = jnp.sum(squares, axis=0, keepdims=True)
         key_scale[e] = lax.rsqrt(total / width + EPSILON)
 
@@ -514,7 +506,7 @@
         todo = [(work_ref[at], work_ref[room + at]) for at in numbers]
         spots = [tile_spot(i) for _, i in todo]
         scores = [
-            dot(query_ref[:, at, near:].reshape(flat, width - near), stacked(pieces[2:], e)) + score_ref[number]
+            dot(query_ref[:, at, near:].reshape(flat, width - near), stacked(pieces[CHAINS:], e)) + score_ref[number]
             for (e, _), at, number in zip(todo, spots, numbers)
         ]
         weights = []
@@ -557,7 +549,7 @@
     return pl.pallas_call(
         cross_kernel,
         out_shape=jax.ShapeDtypeStruct((rows, width), BF16),
-        in_specs=[ANY] + [VMEM] * 12,
+        in_specs=[ANY] + [VMEM] * (8 + 2 * CHAINS),
         out_specs=ANY,
         scratch_shapes=[
             pltpu.VMEM((rows, width), BF16),
@@ -572,36 +564,32 @@
             flops=8 * rows * width * inner, bytes_accessed=2 * groups * width * span, transcendentals=rows * span * heads
         ),
         name="cross",
-    )(work, queries, scores, squares, ids, key_ids, back, *pieces, wv, wo)
-
-
-def exchange(x, groups, tensor, half, step):
-    pairs = [
-        (d * tensor + t, d * tensor + (t ^ ORDERS[d % 2][half][step]))
-        for d in range(groups)
-        for t in range(tensor)
-    ]
+    )(work, queries, scores, squares, ids, key_ids, back, wv, wo, *pieces)
+
+
+def exchange(x, groups, tensor, chain, step):
+    pairs = [(d * tensor + t, d * tensor + (t ^ ORDERS[chain][step])) for d in range(groups) for t in range(tensor)]
     return lax.ppermute(x, ("dp", "tensor"), pairs)
 
 
-def gathered(low, high, groups, tensor):
-    halves = [low[None], high[None]]
+def gathered(x, groups, tensor):
+    part = x.shape[1] // CHAINS
+    held = [x[None, :, c * part : (c + 1) * part] for c in range(CHAINS)]
     for step in range(3):
-        got = [exchange(halves[h], groups, tensor, h, step) for h in range(2)]
-        halves = [jnp.concatenate([halves[h], got[h]], axis=0) for h in range(2)]
-    got = [exchange(halves[h], groups, tensor, h, 3) for h in range(2)]
-    return halves, got
+        got = [exchange(held[c], groups, tensor, c, step) for c in range(CHAINS)]
+        held = [jnp.concatenate([held[c], got[c]], axis=0) for c in range(CHAINS)]
+    got = [exchange(held[c], groups, tensor, c, 3) for c in range(CHAINS)]
+    return held, got
 
 
 def origin_masks():
-    table = np.zeros((2, 2, 16), np.int32)
-    for core in range(2):
-        for half in range(2):
-            for j in range(16):
-                for step in range(4):
-                    if j >> step & 1:
-                        table[core, half, j] ^= ORDERS[core][half][step]
-    return table.reshape(2, 32)
+    table = np.zeros((CHAINS, 16), np.int32)
+    for chain in range(CHAINS):
+        for j in range(16):
+            for step in range(4):
+                if j >> step & 1:
+                    table[chain, j] ^= ORDERS[chain][step]
+    return table.reshape(-1)
 
 
 def body(
@@ -630,7 +618,6 @@
     rows, width = residues.shape
     query_rows = decoder_states.shape[0]
     slice_width = width // tensor
-    part = slice_width // 2
 
     partial_sums = encoder(
         block_protein, protein_length, residues, enc_gain.reshape(1, width), enc_query, enc_key, enc_value, enc_out
@@ -638,7 +625,7 @@
     arrived = lax.all_to_all(
         partial_sums.reshape(tensor, slice_width, rows), "tensor", split_axis=0, concat_axis=0, tiled=True
     )
-    where = jnp.stack([tensor_index, dp_index % 2, dp_index]).astype(jnp.int32)
+    where = jnp.stack([tensor_index, dp_index]).astype(jnp.int32)
     queries, back, sorted_ids, gained_value, own, key_ids, table, starts = query_side(
         block_protein,
         protein_length,
@@ -659,8 +646,8 @@
     arrived, own, queries = lax.optimization_barrier((arrived, own, queries))
     encoded, placed = placing(table, arrived, own, groups)
     received = lax.all_to_all(placed, "dp", split_axis=0, concat_axis=0, tiled=True)
-    near, far = gathered(received[:, :part], received[:, part:], groups, tensor)
-    scores, squares, work = near_scores(starts, queries, *near)
+    near, far = gathered(received, groups, tensor)
+    scores, squares, work = near_scores(starts, queries, near)
     outcome = cross(
         work, queries, scores, squares, sorted_ids, key_ids, back, (*near, *far), gained_value, cross_out
     )

time: 121 us -> 116 us (0.959); the launches traced: 121 us -> 114 us
  waiting for transfers between devices: 33.8 us -> 23.5 us
  starting transfers between devices: 27.7 us -> 33.1 us
  Pallas kernels: 32.1 us -> 29.9 us
    ppermute x8 -> x16, waiting for transfers between devices: 22.2 us -> 11.8 us  [exchange(): return lax.ppermute(x, ('dp', 'tensor'), pairs)]
    ppermute x8 -> x16, starting transfers between devices: 14.8 us -> 22.2 us  [exchange(): return lax.ppermute(x, ('dp', 'tensor'), pairs)]
    all_to_all x1, starting transfers between devices: 5.63 us -> 3.62 us  [body(): lax.all_to_all(outcome.reshape(tensor, share, width), 'tensor', split_axi...]
    pallas_call x1, Pallas kernels: 11.9 us -> 10.1 us  [cross(): pl.pallas_call(cross_kernel, out_shape=jax.ShapeDtypeStruct((rows, width)...]
  transfers between devices with their start and end apart: 10 -> 18, of which waited for: 9 -> 8; matrix products, arithmetic and copies ran while one was open for 1% -> 1% of each run, Pallas kernels for 8% -> 8%
where the time goes in v5:
time: 116 us; the launch traced here: 114 us
  starting transfers between devices  33.1 us (29%)
  Pallas kernels  29.9 us (26%)
  waiting for transfers between devices  23.5 us (20%)
  blocking collectives  12.6 us (11%)
  local copies, waits for them, and re-layouts  11.9 us (10%)
  other arithmetic  2.03 us (2%)
    ppermute x16, starting transfers between devices, exchange(): return lax.ppermute(x, ('dp', 'tensor'), pairs)  22.2 us
    all_to_all x1, blocking collectives, body(): lax.all_to_all(placed, 'dp', split_axis=0, concat_axis=0, tiled=True)  12.6 us
    unnamed x40, local copies, waits for them, and re-layouts  11.9 us
    ppermute x16, waiting for transfers between devices, exchange(): return lax.ppermute(x, ('dp', 'tensor'), pairs)  11.8 us
    all_to_all x1, waiting for transfers between devices, body(): lax.all_to_all(outcome.reshape(tensor, share, width), 'tensor', split_axi...  10.6 us
    pallas_call x1, Pallas kernels, cross(): pl.pallas_call(cross_kernel, out_shape=jax.ShapeDtypeStruct((rows, width)...  10.1 us
    pallas_call x1, Pallas kernels, encoder(): pl.pallas_call(encoder_kernel, out_shape=jax.ShapeDtypeStruct((width, row...  9.59 us
    all_to_all x1, starting transfers between devices, body(): lax.all_to_all(partial_sums.reshape(tensor, slice_width, rows), 'tensor',...  7.29 us
  transfers between devices with their start and end apart: 18, of which 8 were waited for; matrix products, arithmetic and copies ran while one was open for 1% of the time, Pallas kernels for 8%

profile of v5, /device:TPU:0, one launch (start us, length us, event | category | flops | bytes accessed | tf_op | source)
XLA Modules:
  0.0 113.9 jit_solution(1620085480753880348)
XLA Ops:
  0.6 9.6 %encoder.1 = bf16[1024,512]{1,0:T(8,128)(2,1)} custom-call(s32[4]{0:T(128)} %protein_hbm.1, s32[32]{0:T(128)} %length_hbm.1, bf16[512,1024]{1,0:T(8,128)(2,1)} %residue_hbm.3, f32[1,1024]{1,0:T(1,128)} %bitcast.20, bf16[1024,1024]{1,0:T(8,128)(2,1)} %wq_hbm.1, bf16[1024,1024]{1,0:T(8,128)(2,1)} %wk_hbm.1, bf16[1024,1024]{1,0:T(8,128)(2,1)} %wv_hbm.1, ...), custom_call_target="tpu_custom_call" | custom-call | flops 4294967296 | bytes 8388608 | tf_op jit(solution)/shard_map/encoder/pallas_call | solution.py:164
  10.3 7.3 %all-to-all-start = ((bf16[16,64,512]{2,1,0:T(8,128)(2,1)}), bf16[16,64,512]{2,1,0:T(8,128)(2,1)S(1)}, u32[]{:S(2)}, u32[]{:S(2)}) async-start(bf16[16,64,512]{2,1,0:T(8,128)(2,1)} %bitcast.18), calls=%async_computation | async-start | bytes 2097152 | tf_op jit(solution)/shard_map/all_to_all | solution.py:625
  17.6 0.1 pad_add_fusion.where_ref
  17.8 1.6 %copy-done.3 = bf16[1024,1024]{1,0:T(8,128)(2,1)S(1)} copy-done((bf16[1024,1024]{1,0:T(8,128)(2,1)S(1)}, bf16[1024,1024]{1,0:T(8,128)(2,1)}, u32[]{:S(2)}) %copy-start.3) | copy-done | bytes 2097176
  19.4 1.6 %copy-done.4 = bf16[1024,1024]{1,0:T(8,128)(2,1)S(1)} copy-done((bf16[1024,1024]{1,0:T(8,128)(2,1)S(1)}, bf16[1024,1024]{1,0:T(8,128)(2,1)}, u32[]{:S(2)}) %copy-start.4) | copy-done | bytes 2097176
  20.9 1.2 %copy-done.8 = bf16[512,1024]{1,0:T(8,128)(2,1)S(1)} copy-done((bf16[512,1024]{1,0:T(8,128)(2,1)S(1)}, bf16[512,1024]{1,0:T(8,128)(2,1)}, u32[]{:S(2)}) %copy-start.8) | copy-done | bytes 1048600
  22.2 1.1 copy-done.9
  23.3 5.5 %query_side.1 = (bf16[8,384,1024]{2,1,0:T(8,128)(2,1)S(1)}, bf16[384,384]{1,0:T(8,128)(2,1)S(1)}, f32[384,1]{1,0:T(8,128)S(1)}, bf16[1024,1024]{1,0:T(8,128)(2,1...) custom-call(s32[4]{0:T(128)S(1)} %copy-done.16, s32[32]{0:T(128)S(1)} %copy-done.17, ...), custom_call_target="tpu_custom_call" | custom-call | flops 1610612736 | bytes 12582912 | tf_op jit(solution)/shard_map/query_side/pallas_call | solution.py:316
  28.8 2.6 %copy-done = bf16[8,384,1024]{2,1,0:T(8,128)(2,1)} copy-done((bf16[8,384,1024]{2,1,0:T(8,128)(2,1)}, bf16[8,384,1024]{2,1,0:T(8,128)(2,1)S(1)}, u32[]{:S(2)}) %copy-start) | copy-done | bytes 6291480
  31.5 1.4 %copy-done.6 = bf16[1024,1024]{1,0:T(8,128)(2,1)} copy-done((bf16[1024,1024]{1,0:T(8,128)(2,1)}, bf16[1024,1024]{1,0:T(8,128)(2,1)S(1)}, u32[]{:S(2)}) %copy-start.6) | copy-done | bytes 2097176
  32.9 0.7 copy-done.10
  33.6 0.6 copy-done.12
  34.2 1.1 all-to-all-done.arrived_ref
  35.3 0.9 copy-done.13
  36.2 1.3 %placing.1 = (bf16[64,512]{1,0:T(8,128)(2,1)}, bf16[8,64,256]{2,1,0:T(8,128)(2,1)S(1)}) custom-call(s32[16]{0:T(128)S(1)} %get-tuple-element.20.table_ref, bf16[16,64,512]{2,1,0:T(8,128)(2,1)S(1)} %all-to-all-done.arrived_ref, f32[64,512]{1,0:T(8,128)S(1)} %copy-done.13), custom_call_target="tpu_custom_call" | custom-call | tf_op jit(solution)/shard_map/placing/pallas_call | solution.py:373
  37.5 12.6 %all_to_all.15 = bf16[8,64,256]{2,1,0:T(8,128)(2,1)S(1)} all-to-all(bf16[8,64,256]{2,1,0:T(8,128)(2,1)S(1)} %get-tuple-element.28), channel_id=1, replica_groups=mesh['dp'=8,'tensor'=16] {'dp'}, dimensions={0} | all-to-all | bytes 524288 | tf_op jit(solution)/shard_map/all_to_all | solution.py:648
  50.2 0.9 collective-permute-start
  51.1 2.1 %collective-permute-start.3 = (bf16[1,8,16,256]{3,2,1,0:T(8,128)(2,1)S(1)}, bf16[1,8,16,256]{3,2,1,0:T(8,128)(2,1)S(1)}, u32[]{:S(2)}, u32[]{:S(2)}) collective-permute-start(bf16[1,8,16,256]{3,2,1,0:T(8,128)(2,1)S(1)} %get-tuple-element.40), channel_id=1, source_target_pairs={{0,3},{1,2},{2,1},{3,0},{4,7},{5,6},{6,5},{7,4},{8,11},{9,10},{10,... | collective-permute-start | bytes 196616 | tf_op jit(solution)/shard_map/ppermute | solution.py:572
  53.1 1.5 %collective-permute-start.6 = (bf16[1,8,16,256]{3,2,1,0:T(8,128)(2,1)S(1)}, bf16[1,8,16,256]{3,2,1,0:T(8,128)(2,1)S(1)}, u32[]{:S(2)}, u32[]{:S(2)}) collective-permute-start(bf16[1,8,16,256]{3,2,1,0:T(8,128)(2,1)S(1)} %get-tuple-element.39), channel_id=1, source_target_pairs={{0,4},{1,5},{2,6},{3,7},{4,0},{5,1},{6,2},{7,3},{8,12},{9,13},{10,... | collective-permute-start | bytes 196616 | tf_op jit(solution)/shard_map/ppermute | solution.py:572
  54.6 2.1 %collective-permute-start.9 = (bf16[1,8,16,256]{3,2,1,0:T(8,128)(2,1)S(1)}, bf16[1,8,16,256]{3,2,1,0:T(8,128)(2,1)S(1)}, u32[]{:S(2)}, u32[]{:S(2)}) collective-permute-start(bf16[1,8,16,256]{3,2,1,0:T(8,128)(2,1)S(1)} %get-tuple-element.38), channel_id=1, source_target_pairs={{0,12},{1,13},{2,14},{3,15},{4,8},{5,9},{6,10},{7,11},{8,4},{9,5},... | collective-permute-start | bytes 196616 | tf_op jit(solution)/shard_map/ppermute | solution.py:572
  56.7 1.4 %collective-permute-start.1 = (bf16[2,8,16,256]{3,2,1,0:T(8,128)(2,1)S(1)}, bf16[2,8,16,256]{3,2,1,0:T(8,128)(2,1)S(1)}, u32[]{:S(2)}, u32[]{:S(2)}) collective-permute-start(bf16[2,8,16,256]{3,2,1,0:T(8,128)(2,1)S(1)} %pad_maximum_fusion.8), channel_id=1, source_target_pairs={{0,3},{1,2},{2,1},{3,0},{4,7},{5,6},{6,5},{7,4},{8,11},{9,10},{10,... | collective-permute-start | bytes 393224 | tf_op jit(solution)/shard_map/ppermute | solution.py:572
  58.2 0.1 collective-permute-start.4
  58.3 1.9 %collective-permute-start.7 = (bf16[2,8,16,256]{3,2,1,0:T(8,128)(2,1)S(1)}, bf16[2,8,16,256]{3,2,1,0:T(8,128)(2,1)S(1)}, u32[]{:S(2)}, u32[]{:S(2)}) collective-permute-start(bf16[2,8,16,256]{3,2,1,0:T(8,128)(2,1)S(1)} %pad_maximum_fusion.10), channel_id=1, source_target_pairs={{0,12},{1,13},{2,14},{3,15},{4,8},{5,9},{6,10},{7,11},{8,4},{9,5},... | collective-permute-start | bytes 393224 | tf_op jit(solution)/shard_map/ppermute | solution.py:572
  60.2 0.3 collective-permute-start.10
  60.5 2.6 %collective-permute-done.1 = bf16[2,8,16,256]{3,2,1,0:T(8,128)(2,1)S(1)} collective-permute-done((bf16[2,8,16,256]{3,2,1,0:T(8,128)(2,1)S(1)}, bf16[2,8,16,256]{3,2,1,0:T(8,128)(2,1)S(1)}, u32[]{:S(2)}, u32[]{:S(2)}) %collective-permute-start.1) | collective-permute-done | bytes 131104 | tf_op jit(solution)/shard_map/ppermute | solution.py:572
  63.2 0.6 collective-permute-start.2
  63.9 1.1 collective-permute-start.5
  65.0 3.1 %collective-permute-start.8 = (bf16[4,8,16,256]{3,2,1,0:T(8,128)(2,1)S(1)}, bf16[4,8,16,256]{3,2,1,0:T(8,128)(2,1)S(1)}, u32[]{:S(2)}, u32[]{:S(2)}) collective-permute-start(bf16[4,8,16,256]{3,2,1,0:T(8,128)(2,1)S(1)} %pad_maximum_fusion.6), channel_id=1, source_target_pairs={{0,1},{1,0},{2,3},{3,2},{4,5},{5,4},{6,7},{7,6},{8,9},{9,8},{10,11... | collective-permute-start | bytes 786440 | tf_op jit(solution)/shard_map/ppermute | solution.py:572
  68.1 2.1 %collective-permute-start.11 = (bf16[4,8,16,256]{3,2,1,0:T(8,128)(2,1)S(1)}, bf16[4,8,16,256]{3,2,1,0:T(8,128)(2,1)S(1)}, u32[]{:S(2)}, u32[]{:S(2)}) collective-permute-start(bf16[4,8,16,256]{3,2,1,0:T(8,128)(2,1)S(1)} %pad_maximum_fusion.7), channel_id=1, source_target_pairs={{0,3},{1,2},{2,1},{3,0},{4,7},{5,6},{6,5},{7,4},{8,11},{9,10},{10,... | collective-permute-start | bytes 786440 | tf_op jit(solution)/shard_map/ppermute | solution.py:572
  70.2 0.1 pad_maximum_fusion.refs_0_
  70.3 1.4 %collective-permute-start.12 = (bf16[8,8,16,256]{3,2,1,0:T(8,128)(2,1)S(1)}, bf16[8,8,16,256]{3,2,1,0:T(8,128)(2,1)S(1)}, u32[]{:S(2)}, u32[]{:S(2)}) collective-permute-start(bf16[8,8,16,256]{3,2,1,0:T(8,128)(2,1)S(1)} %pad_maximum_fusion.refs_0_), channel_id=1, source_target_pairs={{0,12},{1,13},{2,14},{3,15},{4,8},{5,9},{6,10},{7,11},{8,4},{9,5},... | collective-permute-start | bytes 1572872 | tf_op jit(solution)/shard_map/ppermute | solution.py:572
  71.7 0.1 pad_maximum_fusion.1.refs_1_
  71.7 0.8 collective-permute-start.13
  72.6 0.4 collective-permute-done.8
  73.0 2.7 %collective-permute-start.14 = (bf16[8,8,16,256]{3,2,1,0:T(8,128)(2,1)S(1)}, bf16[8,8,16,256]{3,2,1,0:T(8,128)(2,1)S(1)}, u32[]{:S(2)}, u32[]{:S(2)}) collective-permute-start(bf16[8,8,16,256]{3,2,1,0:T(8,128)(2,1)S(1)} %pad_maximum_fusion.2.refs_2_), channel_id=1, source_target_pairs={{0,3},{1,2},{2,1},{3,0},{4,7},{5,6},{6,5},{7,4},{8,11},{9,10},{10,... | collective-permute-start | bytes 1572872 | tf_op jit(solution)/shard_map/ppermute | solution.py:572
  75.7 2.9 %collective-permute-done.11 = bf16[4,8,16,256]{3,2,1,0:T(8,128)(2,1)S(1)} collective-permute-done((bf16[4,8,16,256]{3,2,1,0:T(8,128)(2,1)S(1)}, bf16[4,8,16,256]{3,2,1,0:T(8,128)(2,1)S(1)}, u32[]{:S(2)}, u32[]{:S(2)}) %collective-permute-start.11) | collective-permute-done | bytes 262176 | tf_op jit(solution)/shard_map/ppermute | solution.py:572
  78.6 0.1 pad_maximum_fusion.3.refs_3_
  78.6 0.1 collective-permute-start.15
  78.8 3.3 %near_scores.1 = (f32[20,256,256]{2,1,0:T(8,128)S(1)}, f32[8,8,256]{2,1,0:T(8,128)S(1)}, s32[49]{0:T(128)S(1)}) custom-call(s32[9]{0:T(128)S(1)} %get-tuple-element.26.start_ref, bf16[8,384,1024]{2,1,0:T(8,128)(2,1)S(1)} %copy-done.1, bf16[8,8,16,256]{3,2,1,0:T(8,128)(2,1)S(1)} %pad_maximum_fusion.refs_0_, ...), custom_call_target="tpu_custom_call" | custom-call | flops 1342177280 | bytes 5242880 | tf_op jit(solution)/shard_map/near_scores/pallas_call | solution.py:456
  82.0 1.0 collective-permute-done.12.refs_4_
  83.0 3.5 %collective-permute-done.14.refs_6_ = bf16[8,8,16,256]{3,2,1,0:T(8,128)(2,1)S(1)} collective-permute-done((bf16[8,8,16,256]{3,2,1,0:T(8,128)(2,1)S(1)}, bf16[8,8,16,256]{3,2,1,0:T(8,128)(2,1)S(1)}, u32[]{:S(2)}, u32[]{:S(2)}) %collective-permute-start.14) | collective-permute-done | bytes 524320 | tf_op jit(solution)/shard_map/ppermute | solution.py:572
  86.5 1.3 %collective-permute-done.15.refs_7_ = bf16[8,8,16,256]{3,2,1,0:T(8,128)(2,1)S(1)} collective-permute-done((bf16[8,8,16,256]{3,2,1,0:T(8,128)(2,1)S(1)}, bf16[8,8,16,256]{3,2,1,0:T(8,128)(2,1)S(1)}, u32[]{:S(2)}, u32[]{:S(2)}) %collective-permute-start.15) | collective-permute-done | bytes 524320 | tf_op jit(solution)/shard_map/ppermute | solution.py:572
  87.9 10.1 %cross.1 = bf16[384,1024]{1,0:T(8,128)(2,1)} custom-call(s32[49]{0:T(128)S(1)} %get-tuple-element.29.work_hbm, bf16[8,384,1024]{2,1,0:T(8,128)(2,1)S(1)} %copy-done.1, f32[20,256,256]{2,1,0:T(8,128)S(1)} %get-tuple-element.30.score_ref, f32[8,8,256]{2,1,0:T(8,128)S(1)} %get-tuple-element.31.square_ref, f32[384,1]{1,0:T(8,128)S(1)} %copy-done.11, ...), custom_call_target="tpu_custom_call" | custom-call | flops 3221225472 | bytes 4194304 | tf_op jit(solution)/shard_map/cross/pallas_call | solution.py:549
  98.0 3.6 %all-to-all-start.2 = ((bf16[16,24,1024]{2,1,0:T(8,128)(2,1)}), bf16[16,24,1024]{2,1,0:T(8,128)(2,1)S(1)}, u32[]{:S(2)}, u32[]{:S(2)}) async-start(bf16[16,24,1024]{2,1,0:T(8,128)(2,1)} %bitcast.11), calls=%async_computation.2 | async-start | bytes 1572864 | tf_op jit(solution)/shard_map/all_to_all | solution.py:654
  101.7 0.8 dynamic-slice_convert_fusion
  102.5 10.6 %all-to-all-done.2 = bf16[16,24,1024]{2,1,0:T(8,128)(2,1)S(1)} async-done(((bf16[16,24,1024]{2,1,0:T(8,128)(2,1)}), bf16[16,24,1024]{2,1,0:T(8,128)(2,1)S(1)}, u32[]{:S(2)}, u32[]{:S(2)}) %all-to-all-start.2) | async-done | bytes 786464 | tf_op jit(solution)/shard_map/all_to_all | solution.py:654
  113.1 0.1 convert_reduce_fusion
  113.3 0.6 add_convert_fusion
  (52 shorter events, 0.3 us)
Async XLA Ops:
  10.2 7.4 %copy-start.19 = (s32[384]{0:T(512)S(1)}, s32[384]{0:T(512)}, u32[]{:S(2)}) copy-start(s32[384]{0:T(512)} %param.27) | copy-start | bytes 4612
  10.2 7.5 %copy-start.2 = (bf16[1024,1024]{1,0:T(8,128)(2,1)S(1)}, bf16[1024,1024]{1,0:T(8,128)(2,1)}, u32[]{:S(2)}) copy-start(bf16[1024,1024]{1,0:T(8,128)(2,1)} %wq_ref.1) | copy-start | bytes 6291460
  10.3 7.5 %copy-start.14 = (f32[1024]{0:T(1024)S(1)}, f32[1024]{0:T(1024)}, u32[]{:S(2)}) copy-start(f32[1024]{0:T(1024)} %param.28) | copy-start | bytes 12292
  10.3 7.5 %copy-start.15 = (f32[1024]{0:T(1024)S(1)}, f32[1024]{0:T(1024)}, u32[]{:S(2)}) copy-start(f32[1024]{0:T(1024)} %param.29) | copy-start | bytes 12292
  10.3 7.4 %copy-start.16 = (s32[4]{0:T(128)S(1)}, s32[4]{0:T(128)}, u32[]{:S(2)}) copy-start(s32[4]{0:T(128)} %protein_hbm.1) | copy-start | bytes 52
  10.3 7.4 %copy-start.17 = (s32[32]{0:T(128)S(1)}, s32[32]{0:T(128)}, u32[]{:S(2)}) copy-start(s32[32]{0:T(128)} %length_hbm.1) | copy-start | bytes 388
  10.3 7.4 %copy-start.18 = (s32[32]{0:T(128)S(1)}, s32[32]{0:T(128)}, u32[]{:S(2)}) copy-start(s32[32]{0:T(128)} %group_ref.1) | copy-start | bytes 388
  10.3 25.0 %all-to-all-start = ((bf16[16,64,512]{2,1,0:T(8,128)(2,1)}), bf16[16,64,512]{2,1,0:T(8,128)(2,1)S(1)}, u32[]{:S(2)}, u32[]{:S(2)}) async-start(bf16[16,64,512]{2,1,0:T(8,128)(2,1)} %bitcast.18), calls=%async_computation | async-start | bytes 2097152 | tf_op jit(solution)/shard_map/all_to_all | solution.py:625
  17.8 1.6 %copy-start.3 = (bf16[1024,1024]{1,0:T(8,128)(2,1)S(1)}, bf16[1024,1024]{1,0:T(8,128)(2,1)}, u32[]{:S(2)}) copy-start(bf16[1024,1024]{1,0:T(8,128)(2,1)} %wk_ref.1) | copy-start | bytes 6291460
  19.3 1.6 %copy-start.4 = (bf16[1024,1024]{1,0:T(8,128)(2,1)S(1)}, bf16[1024,1024]{1,0:T(8,128)(2,1)}, u32[]{:S(2)}) copy-start(bf16[1024,1024]{1,0:T(8,128)(2,1)} %wv_ref.1) | copy-start | bytes 6291460
  20.9 1.2 %copy-start.8 = (bf16[512,1024]{1,0:T(8,128)(2,1)S(1)}, bf16[512,1024]{1,0:T(8,128)(2,1)}, u32[]{:S(2)}) copy-start(bf16[512,1024]{1,0:T(8,128)(2,1)} %residue_hbm.3) | copy-start | bytes 3145732
  22.2 1.1 copy-start.9
  28.8 2.6 %copy-start = (bf16[8,384,1024]{2,1,0:T(8,128)(2,1)}, bf16[8,384,1024]{2,1,0:T(8,128)(2,1)S(1)}, u32[]{:S(2)}) copy-start(bf16[8,384,1024]{2,1,0:T(8,128)(2,1)S(1)} %get-tuple-element.27.query_ref) | copy-start | bytes 18874372
  31.5 1.4 %copy-start.6 = (bf16[1024,1024]{1,0:T(8,128)(2,1)}, bf16[1024,1024]{1,0:T(8,128)(2,1)S(1)}, u32[]{:S(2)}) copy-start(bf16[1024,1024]{1,0:T(8,128)(2,1)S(1)} %get-tuple-element.35.wv_ref) | copy-start | bytes 6291460
  32.9 0.7 copy-start.10
  33.6 0.7 copy-start.12
  35.3 0.9 copy-start.13
  50.2 6.5 %collective-permute-start = (bf16[1,8,16,256]{3,2,1,0:T(8,128)(2,1)S(1)}, bf16[1,8,16,256]{3,2,1,0:T(8,128)(2,1)S(1)}, u32[]{:S(2)}, u32[]{:S(2)}) collective-permute-start(bf16[1,8,16,256]{3,2,1,0:T(8,128)(2,1)S(1)} %get-tuple-element.41), channel_id=1, source_target_pairs={{0,1},{1,0},{2,3},{3,2},{4,5},{5,4},{6,7},{7,6},{8,9},{9,8},{10,11... | collective-permute-start | bytes 196616 | tf_op jit(solution)/shard_map/ppermute | solution.py:572
  51.1 7.1 %collective-permute-start.3 = (bf16[1,8,16,256]{3,2,1,0:T(8,128)(2,1)S(1)}, bf16[1,8,16,256]{3,2,1,0:T(8,128)(2,1)S(1)}, u32[]{:S(2)}, u32[]{:S(2)}) collective-permute-start(bf16[1,8,16,256]{3,2,1,0:T(8,128)(2,1)S(1)} %get-tuple-element.40), channel_id=1, source_target_pairs={{0,3},{1,2},{2,1},{3,0},{4,7},{5,6},{6,5},{7,4},{8,11},{9,10},{10,... | collective-permute-start | bytes 196616 | tf_op jit(solution)/shard_map/ppermute | solution.py:572
  53.1 5.1 %collective-permute-start.6 = (bf16[1,8,16,256]{3,2,1,0:T(8,128)(2,1)S(1)}, bf16[1,8,16,256]{3,2,1,0:T(8,128)(2,1)S(1)}, u32[]{:S(2)}, u32[]{:S(2)}) collective-permute-start(bf16[1,8,16,256]{3,2,1,0:T(8,128)(2,1)S(1)} %get-tuple-element.39), channel_id=1, source_target_pairs={{0,4},{1,5},{2,6},{3,7},{4,0},{5,1},{6,2},{7,3},{8,12},{9,13},{10,... | collective-permute-start | bytes 196616 | tf_op jit(solution)/shard_map/ppermute | solution.py:572
  54.6 5.6 %collective-permute-start.9 = (bf16[1,8,16,256]{3,2,1,0:T(8,128)(2,1)S(1)}, bf16[1,8,16,256]{3,2,1,0:T(8,128)(2,1)S(1)}, u32[]{:S(2)}, u32[]{:S(2)}) collective-permute-start(bf16[1,8,16,256]{3,2,1,0:T(8,128)(2,1)S(1)} %get-tuple-element.38), channel_id=1, source_target_pairs={{0,12},{1,13},{2,14},{3,15},{4,8},{5,9},{6,10},{7,11},{8,4},{9,5},... | collective-permute-start | bytes 196616 | tf_op jit(solution)/shard_map/ppermute | solution.py:572
  56.7 6.4 %collective-permute-start.1 = (bf16[2,8,16,256]{3,2,1,0:T(8,128)(2,1)S(1)}, bf16[2,8,16,256]{3,2,1,0:T(8,128)(2,1)S(1)}, u32[]{:S(2)}, u32[]{:S(2)}) collective-permute-start(bf16[2,8,16,256]{3,2,1,0:T(8,128)(2,1)S(1)} %pad_maximum_fusion.8), channel_id=1, source_target_pairs={{0,3},{1,2},{2,1},{3,0},{4,7},{5,6},{6,5},{7,4},{8,11},{9,10},{10,... | collective-permute-start | bytes 393224 | tf_op jit(solution)/shard_map/ppermute | solution.py:572
  58.2 5.7 %collective-permute-start.4 = (bf16[2,8,16,256]{3,2,1,0:T(8,128)(2,1)S(1)}, bf16[2,8,16,256]{3,2,1,0:T(8,128)(2,1)S(1)}, u32[]{:S(2)}, u32[]{:S(2)}) collective-permute-start(bf16[2,8,16,256]{3,2,1,0:T(8,128)(2,1)S(1)} %pad_maximum_fusion.9), channel_id=1, source_target_pairs={{0,1},{1,0},{2,3},{3,2},{4,5},{5,4},{6,7},{7,6},{8,9},{9,8},{10,11... | collective-permute-start | bytes 393224 | tf_op jit(solution)/shard_map/ppermute | solution.py:572
  58.3 6.6 %collective-permute-start.7 = (bf16[2,8,16,256]{3,2,1,0:T(8,128)(2,1)S(1)}, bf16[2,8,16,256]{3,2,1,0:T(8,128)(2,1)S(1)}, u32[]{:S(2)}, u32[]{:S(2)}) collective-permute-start(bf16[2,8,16,256]{3,2,1,0:T(8,128)(2,1)S(1)} %pad_maximum_fusion.10), channel_id=1, source_target_pairs={{0,12},{1,13},{2,14},{3,15},{4,8},{5,9},{6,10},{7,11},{8,4},{9,5},... | collective-permute-start | bytes 393224 | tf_op jit(solution)/shard_map/ppermute | solution.py:572
  60.2 7.8 %collective-permute-start.10 = (bf16[2,8,16,256]{3,2,1,0:T(8,128)(2,1)S(1)}, bf16[2,8,16,256]{3,2,1,0:T(8,128)(2,1)S(1)}, u32[]{:S(2)}, u32[]{:S(2)}) collective-permute-start(bf16[2,8,16,256]{3,2,1,0:T(8,128)(2,1)S(1)} %pad_maximum_fusion.11), channel_id=1, source_target_pairs={{0,4},{1,5},{2,6},{3,7},{4,0},{5,1},{6,2},{7,3},{8,12},{9,13},{10,... | collective-permute-start | bytes 393224 | tf_op jit(solution)/shard_map/ppermute | solution.py:572
  63.1 15.6 %copy-start.1 = (bf16[8,384,1024]{2,1,0:T(8,128)(2,1)S(1)}, bf16[8,384,1024]{2,1,0:T(8,128)(2,1)}, u32[]{:S(2)}) copy-start(bf16[8,384,1024]{2,1,0:T(8,128)(2,1)} %copy-done) | copy-start | bytes 18874372
  63.2 7.1 %collective-permute-start.2 = (bf16[4,8,16,256]{3,2,1,0:T(8,128)(2,1)S(1)}, bf16[4,8,16,256]{3,2,1,0:T(8,128)(2,1)S(1)}, u32[]{:S(2)}, u32[]{:S(2)}) collective-permute-start(bf16[4,8,16,256]{3,2,1,0:T(8,128)(2,1)S(1)} %pad_maximum_fusion.4), channel_id=1, source_target_pairs={{0,4},{1,5},{2,6},{3,7},{4,0},{5,1},{6,2},{7,3},{8,12},{9,13},{10,... | collective-permute-start | bytes 786440 | tf_op jit(solution)/shard_map/ppermute | solution.py:572
  63.9 7.8 %collective-permute-start.5 = (bf16[4,8,16,256]{3,2,1,0:T(8,128)(2,1)S(1)}, bf16[4,8,16,256]{3,2,1,0:T(8,128)(2,1)S(1)}, u32[]{:S(2)}, u32[]{:S(2)}) collective-permute-start(bf16[4,8,16,256]{3,2,1,0:T(8,128)(2,1)S(1)} %pad_maximum_fusion.5), channel_id=1, source_target_pairs={{0,12},{1,13},{2,14},{3,15},{4,8},{5,9},{6,10},{7,11},{8,4},{9,5},... | collective-permute-start | bytes 786440 | tf_op jit(solution)/shard_map/ppermute | solution.py:572
  65.0 8.0 %collective-permute-start.8 = (bf16[4,8,16,256]{3,2,1,0:T(8,128)(2,1)S(1)}, bf16[4,8,16,256]{3,2,1,0:T(8,128)(2,1)S(1)}, u32[]{:S(2)}, u32[]{:S(2)}) collective-permute-start(bf16[4,8,16,256]{3,2,1,0:T(8,128)(2,1)S(1)} %pad_maximum_fusion.6), channel_id=1, source_target_pairs={{0,1},{1,0},{2,3},{3,2},{4,5},{5,4},{6,7},{7,6},{8,9},{9,8},{10,11... | collective-permute-start | bytes 786440 | tf_op jit(solution)/shard_map/ppermute | solution.py:572
  68.1 10.5 %collective-permute-start.11 = (bf16[4,8,16,256]{3,2,1,0:T(8,128)(2,1)S(1)}, bf16[4,8,16,256]{3,2,1,0:T(8,128)(2,1)S(1)}, u32[]{:S(2)}, u32[]{:S(2)}) collective-permute-start(bf16[4,8,16,256]{3,2,1,0:T(8,128)(2,1)S(1)} %pad_maximum_fusion.7), channel_id=1, source_target_pairs={{0,3},{1,2},{2,1},{3,0},{4,7},{5,6},{6,5},{7,4},{8,11},{9,10},{10,... | collective-permute-start | bytes 786440 | tf_op jit(solution)/shard_map/ppermute | solution.py:572
  70.3 12.7 %collective-permute-start.12 = (bf16[8,8,16,256]{3,2,1,0:T(8,128)(2,1)S(1)}, bf16[8,8,16,256]{3,2,1,0:T(8,128)(2,1)S(1)}, u32[]{:S(2)}, u32[]{:S(2)}) collective-permute-start(bf16[8,8,16,256]{3,2,1,0:T(8,128)(2,1)S(1)} %pad_maximum_fusion.refs_0_), channel_id=1, source_target_pairs={{0,12},{1,13},{2,14},{3,15},{4,8},{5,9},{6,10},{7,11},{8,4},{9,5},... | collective-permute-start | bytes 1572872 | tf_op jit(solution)/shard_map/ppermute | solution.py:572
  71.7 11.3 %collective-permute-start.13 = (bf16[8,8,16,256]{3,2,1,0:T(8,128)(2,1)S(1)}, bf16[8,8,16,256]{3,2,1,0:T(8,128)(2,1)S(1)}, u32[]{:S(2)}, u32[]{:S(2)}) collective-permute-start(bf16[8,8,16,256]{3,2,1,0:T(8,128)(2,1)S(1)} %pad_maximum_fusion.1.refs_1_), channel_id=1, source_target_pairs={{0,4},{1,5},{2,6},{3,7},{4,0},{5,1},{6,2},{7,3},{8,12},{9,13},{10,... | collective-permute-start | bytes 1572872 | tf_op jit(solution)/shard_map/ppermute | solution.py:572
  73.0 13.5 %collective-permute-start.14 = (bf16[8,8,16,256]{3,2,1,0:T(8,128)(2,1)S(1)}, bf16[8,8,16,256]{3,2,1,0:T(8,128)(2,1)S(1)}, u32[]{:S(2)}, u32[]{:S(2)}) collective-permute-start(bf16[8,8,16,256]{3,2,1,0:T(8,128)(2,1)S(1)} %pad_maximum_fusion.2.refs_2_), channel_id=1, source_target_pairs={{0,3},{1,2},{2,1},{3,0},{4,7},{5,6},{6,5},{7,4},{8,11},{9,10},{10,... | collective-permute-start | bytes 1572872 | tf_op jit(solution)/shard_map/ppermute | solution.py:572
  78.6 9.3 %collective-permute-start.15 = (bf16[8,8,16,256]{3,2,1,0:T(8,128)(2,1)S(1)}, bf16[8,8,16,256]{3,2,1,0:T(8,128)(2,1)S(1)}, u32[]{:S(2)}, u32[]{:S(2)}) collective-permute-start(bf16[8,8,16,256]{3,2,1,0:T(8,128)(2,1)S(1)} %pad_maximum_fusion.3.refs_3_), channel_id=1, source_target_pairs={{0,1},{1,0},{2,3},{3,2},{4,5},{5,4},{6,7},{7,6},{8,9},{9,8},{10,11... | collective-permute-start | bytes 1572872 | tf_op jit(solution)/shard_map/ppermute | solution.py:572
  78.7 9.2 %copy-start.5 = (bf16[1024,1024]{1,0:T(8,128)(2,1)S(1)}, bf16[1024,1024]{1,0:T(8,128)(2,1)}, u32[]{:S(2)}) copy-start(bf16[1024,1024]{1,0:T(8,128)(2,1)} %wo_ref.1) | copy-start | bytes 6291460
  78.7 9.2 %copy-start.7 = (bf16[1024,1024]{1,0:T(8,128)(2,1)S(1)}, bf16[1024,1024]{1,0:T(8,128)(2,1)}, u32[]{:S(2)}) copy-start(bf16[1024,1024]{1,0:T(8,128)(2,1)} %copy-done.6) | copy-start | bytes 6291460
  78.7 9.1 %copy-start.11 = (f32[384,1]{1,0:T(8,128)S(1)}, f32[384,1]{1,0:T(8,128)}, u32[]{:S(2)}) copy-start(f32[384,1]{1,0:T(8,128)} %copy-done.10) | copy-start | bytes 4612
  98.0 15.1 %all-to-all-start.2 = ((bf16[16,24,1024]{2,1,0:T(8,128)(2,1)}), bf16[16,24,1024]{2,1,0:T(8,128)(2,1)S(1)}, u32[]{:S(2)}, u32[]{:S(2)}) async-start(bf16[16,24,1024]{2,1,0:T(8,128)(2,1)} %bitcast.11), calls=%async_computation.2 | async-start | bytes 1572864 | tf_op jit(solution)/shard_map/all_to_all | solution.py:654

commit v6 on v5

--- a/solution.py
+++ b/solution.py
@@ -26,7 +26,7 @@
 ANY = pl.BlockSpec(memory_space=pl.ANY)
 
 XA, XB, YA, YB = 1, 3, 4, 12
-ORDERS = ((XA, XB, YA, YB), (XB, XA, YB, YA), (YA, YB, XA, XB), (YB, YA, XB, XA))
+ORDERS = ((XA, YA, XB, YB), (YA, XA, YB, XB), (XB, YB, XA, YA), (YB, XB, YA, XA))
 CHAINS = len(ORDERS)
 
 

time: 116 us -> 116 us (level)
  waiting for transfers between devices: 23.5 us -> 18.5 us
  starting transfers between devices: 33.1 us -> 36.5 us
  Pallas kernels: 29.9 us -> 32.2 us
    ppermute x16, waiting for transfers between devices: 11.8 us -> 6.66 us  [exchange(): return lax.ppermute(x, ('dp', 'tensor'), pairs)]
    ppermute x16, starting transfers between devices: 22.2 us -> 24.4 us  [exchange(): return lax.ppermute(x, ('dp', 'tensor'), pairs)]
    pallas_call x1, Pallas kernels: 10.1 us -> 12.1 us  [cross(): pl.pallas_call(cross_kernel, out_shape=jax.ShapeDtypeStruct((rows, width)...]
    all_to_all x1, starting transfers between devices: 3.62 us -> 4.82 us  [body(): lax.all_to_all(outcome.reshape(tensor, share, width), 'tensor', split_axi...]
  transfers between devices with their start and end apart: 18 -> 18, of which waited for: 8 -> 9; matrix products, arithmetic and copies ran while one was open for 1% -> 1% of each run, Pallas kernels for 8% -> 8%
where the time goes in v6:
time: 116 us; the launch traced here: 115 us
  starting transfers between devices  36.5 us (31%)
  Pallas kernels  32.2 us (28%)
  waiting for transfers between devices  18.5 us (16%)
  blocking collectives  12.6 us (11%)
  local copies, waits for them, and re-layouts  11.9 us (10%)
  other arithmetic  2.03 us (2%)
    ppermute x16, starting transfers between devices, exchange(): return lax.ppermute(x, ('dp', 'tensor'), pairs)  24.4 us
    all_to_all x1, blocking collectives, body(): lax.all_to_all(placed, 'dp', split_axis=0, concat_axis=0, tiled=True)  12.6 us
    pallas_call x1, Pallas kernels, cross(): pl.pallas_call(cross_kernel, out_shape=jax.ShapeDtypeStruct((rows, width)...  12.1 us
    unnamed x40, local copies, waits for them, and re-layouts  11.9 us
    all_to_all x1, waiting for transfers between devices, body(): lax.all_to_all(outcome.reshape(tensor, share, width), 'tensor', split_axi...  10.8 us
    pallas_call x1, Pallas kernels, encoder(): pl.pallas_call(encoder_kernel, out_shape=jax.ShapeDtypeStruct((width, row...  9.59 us
    all_to_all x1, starting transfers between devices, body(): lax.all_to_all(partial_sums.reshape(tensor, slice_width, rows), 'tensor',...  7.29 us
    ppermute x16, waiting for transfers between devices, exchange(): return lax.ppermute(x, ('dp', 'tensor'), pairs)  6.66 us
  transfers between devices with their start and end apart: 18, of which 9 were waited for; matrix products, arithmetic and copies ran while one was open for 1% of the time, Pallas kernels for 8%

profile of v6, /device:TPU:0, one launch (start us, length us, event | category | flops | bytes accessed | tf_op | source)
XLA Modules:
  0.0 114.7 jit_solution(17948510670245490345)
XLA Ops:
  0.6 9.6 %encoder.1 = bf16[1024,512]{1,0:T(8,128)(2,1)} custom-call(s32[4]{0:T(128)} %protein_hbm.1, s32[32]{0:T(128)} %length_hbm.1, bf16[512,1024]{1,0:T(8,128)(2,1)} %residue_hbm.3, f32[1,1024]{1,0:T(1,128)} %bitcast.20, bf16[1024,1024]{1,0:T(8,128)(2,1)} %wq_hbm.1, bf16[1024,1024]{1,0:T(8,128)(2,1)} %wk_hbm.1, bf16[1024,1024]{1,0:T(8,128)(2,1)} %wv_hbm.1, ...), custom_call_target="tpu_custom_call" | custom-call | flops 4294967296 | bytes 8388608 | tf_op jit(solution)/shard_map/encoder/pallas_call | solution.py:164
  10.3 7.3 %all-to-all-start = ((bf16[16,64,512]{2,1,0:T(8,128)(2,1)}), bf16[16,64,512]{2,1,0:T(8,128)(2,1)S(1)}, u32[]{:S(2)}, u32[]{:S(2)}) async-start(bf16[16,64,512]{2,1,0:T(8,128)(2,1)} %bitcast.18), calls=%async_computation | async-start | bytes 2097152 | tf_op jit(solution)/shard_map/all_to_all | solution.py:625
  17.6 0.1 pad_add_fusion.where_ref
  17.8 1.6 %copy-done.3 = bf16[1024,1024]{1,0:T(8,128)(2,1)S(1)} copy-done((bf16[1024,1024]{1,0:T(8,128)(2,1)S(1)}, bf16[1024,1024]{1,0:T(8,128)(2,1)}, u32[]{:S(2)}) %copy-start.3) | copy-done | bytes 2097176
  19.4 1.6 %copy-done.4 = bf16[1024,1024]{1,0:T(8,128)(2,1)S(1)} copy-done((bf16[1024,1024]{1,0:T(8,128)(2,1)S(1)}, bf16[1024,1024]{1,0:T(8,128)(2,1)}, u32[]{:S(2)}) %copy-start.4) | copy-done | bytes 2097176
  20.9 1.2 %copy-done.8 = bf16[512,1024]{1,0:T(8,128)(2,1)S(1)} copy-done((bf16[512,1024]{1,0:T(8,128)(2,1)S(1)}, bf16[512,1024]{1,0:T(8,128)(2,1)}, u32[]{:S(2)}) %copy-start.8) | copy-done | bytes 1048600
  22.2 1.1 copy-done.9
  23.3 5.5 %query_side.1 = (bf16[8,384,1024]{2,1,0:T(8,128)(2,1)S(1)}, bf16[384,384]{1,0:T(8,128)(2,1)S(1)}, f32[384,1]{1,0:T(8,128)S(1)}, bf16[1024,1024]{1,0:T(8,128)(2,1...) custom-call(s32[4]{0:T(128)S(1)} %copy-done.16, s32[32]{0:T(128)S(1)} %copy-done.17, ...), custom_call_target="tpu_custom_call" | custom-call | flops 1610612736 | bytes 12582912 | tf_op jit(solution)/shard_map/query_side/pallas_call | solution.py:316
  28.8 2.6 %copy-done = bf16[8,384,1024]{2,1,0:T(8,128)(2,1)} copy-done((bf16[8,384,1024]{2,1,0:T(8,128)(2,1)}, bf16[8,384,1024]{2,1,0:T(8,128)(2,1)S(1)}, u32[]{:S(2)}) %copy-start) | copy-done | bytes 6291480
  31.5 1.4 %copy-done.6 = bf16[1024,1024]{1,0:T(8,128)(2,1)} copy-done((bf16[1024,1024]{1,0:T(8,128)(2,1)}, bf16[1024,1024]{1,0:T(8,128)(2,1)S(1)}, u32[]{:S(2)}) %copy-start.6) | copy-done | bytes 2097176
  32.9 0.7 copy-done.10
  33.6 0.6 copy-done.12
  34.2 1.1 all-to-all-done.arrived_ref
  35.3 0.9 copy-done.13
  36.2 1.3 %placing.1 = (bf16[64,512]{1,0:T(8,128)(2,1)}, bf16[8,64,256]{2,1,0:T(8,128)(2,1)S(1)}) custom-call(s32[16]{0:T(128)S(1)} %get-tuple-element.20.table_ref, bf16[16,64,512]{2,1,0:T(8,128)(2,1)S(1)} %all-to-all-done.arrived_ref, f32[64,512]{1,0:T(8,128)S(1)} %copy-done.13), custom_call_target="tpu_custom_call" | custom-call | tf_op jit(solution)/shard_map/placing/pallas_call | solution.py:373
  37.5 12.6 %all_to_all.15 = bf16[8,64,256]{2,1,0:T(8,128)(2,1)S(1)} all-to-all(bf16[8,64,256]{2,1,0:T(8,128)(2,1)S(1)} %get-tuple-element.28), channel_id=1, replica_groups=mesh['dp'=8,'tensor'=16] {'dp'}, dimensions={0} | all-to-all | bytes 524288 | tf_op jit(solution)/shard_map/all_to_all | solution.py:648
  50.2 0.9 collective-permute-start
  51.1 1.5 %collective-permute-start.3 = (bf16[1,8,16,256]{3,2,1,0:T(8,128)(2,1)S(1)}, bf16[1,8,16,256]{3,2,1,0:T(8,128)(2,1)S(1)}, u32[]{:S(2)}, u32[]{:S(2)}) collective-permute-start(bf16[1,8,16,256]{3,2,1,0:T(8,128)(2,1)S(1)} %get-tuple-element.40), channel_id=1, source_target_pairs={{0,4},{1,5},{2,6},{3,7},{4,0},{5,1},{6,2},{7,3},{8,12},{9,13},{10,... | collective-permute-start | bytes 196616 | tf_op jit(solution)/shard_map/ppermute | solution.py:572
  52.5 2.1 %collective-permute-start.6 = (bf16[1,8,16,256]{3,2,1,0:T(8,128)(2,1)S(1)}, bf16[1,8,16,256]{3,2,1,0:T(8,128)(2,1)S(1)}, u32[]{:S(2)}, u32[]{:S(2)}) collective-permute-start(bf16[1,8,16,256]{3,2,1,0:T(8,128)(2,1)S(1)} %get-tuple-element.39), channel_id=1, source_target_pairs={{0,3},{1,2},{2,1},{3,0},{4,7},{5,6},{6,5},{7,4},{8,11},{9,10},{10,... | collective-permute-start | bytes 196616 | tf_op jit(solution)/shard_map/ppermute | solution.py:572
  54.6 2.1 %collective-permute-start.9 = (bf16[1,8,16,256]{3,2,1,0:T(8,128)(2,1)S(1)}, bf16[1,8,16,256]{3,2,1,0:T(8,128)(2,1)S(1)}, u32[]{:S(2)}, u32[]{:S(2)}) collective-permute-start(bf16[1,8,16,256]{3,2,1,0:T(8,128)(2,1)S(1)} %get-tuple-element.38), channel_id=1, source_target_pairs={{0,12},{1,13},{2,14},{3,15},{4,8},{5,9},{6,10},{7,11},{8,4},{9,5},... | collective-permute-start | bytes 196616 | tf_op jit(solution)/shard_map/ppermute | solution.py:572
  56.7 0.8 collective-permute-start.1
  57.6 0.6 collective-permute-start.4
  58.2 2.0 %collective-permute-start.7 = (bf16[2,8,16,256]{3,2,1,0:T(8,128)(2,1)S(1)}, bf16[2,8,16,256]{3,2,1,0:T(8,128)(2,1)S(1)}, u32[]{:S(2)}, u32[]{:S(2)}) collective-permute-start(bf16[2,8,16,256]{3,2,1,0:T(8,128)(2,1)S(1)} %pad_maximum_fusion.10), channel_id=1, source_target_pairs={{0,12},{1,13},{2,14},{3,15},{4,8},{5,9},{6,10},{7,11},{8,4},{9,5},... | collective-permute-start | bytes 393224 | tf_op jit(solution)/shard_map/ppermute | solution.py:572
  60.2 0.1 collective-permute-done.9
  60.3 2.1 %collective-permute-start.10 = (bf16[2,8,16,256]{3,2,1,0:T(8,128)(2,1)S(1)}, bf16[2,8,16,256]{3,2,1,0:T(8,128)(2,1)S(1)}, u32[]{:S(2)}, u32[]{:S(2)}) collective-permute-start(bf16[2,8,16,256]{3,2,1,0:T(8,128)(2,1)S(1)} %pad_maximum_fusion.11), channel_id=1, source_target_pairs={{0,3},{1,2},{2,1},{3,0},{4,7},{5,6},{6,5},{7,4},{8,11},{9,10},{10,... | collective-permute-start | bytes 393224 | tf_op jit(solution)/shard_map/ppermute | solution.py:572
  62.4 1.3 %collective-permute-start.2 = (bf16[4,8,16,256]{3,2,1,0:T(8,128)(2,1)S(1)}, bf16[4,8,16,256]{3,2,1,0:T(8,128)(2,1)S(1)}, u32[]{:S(2)}, u32[]{:S(2)}) collective-permute-start(bf16[4,8,16,256]{3,2,1,0:T(8,128)(2,1)S(1)} %pad_maximum_fusion.4), channel_id=1, source_target_pairs={{0,3},{1,2},{2,1},{3,0},{4,7},{5,6},{6,5},{7,4},{8,11},{9,10},{10,... | collective-permute-start | bytes 786440 | tf_op jit(solution)/shard_map/ppermute | solution.py:572
  63.8 2.4 %collective-permute-start.5 = (bf16[4,8,16,256]{3,2,1,0:T(8,128)(2,1)S(1)}, bf16[4,8,16,256]{3,2,1,0:T(8,128)(2,1)S(1)}, u32[]{:S(2)}, u32[]{:S(2)}) collective-permute-start(bf16[4,8,16,256]{3,2,1,0:T(8,128)(2,1)S(1)} %pad_maximum_fusion.5), channel_id=1, source_target_pairs={{0,12},{1,13},{2,14},{3,15},{4,8},{5,9},{6,10},{7,11},{8,4},{9,5},... | collective-permute-start | bytes 786440 | tf_op jit(solution)/shard_map/ppermute | solution.py:572
  66.2 1.3 %collective-permute-start.8 = (bf16[4,8,16,256]{3,2,1,0:T(8,128)(2,1)S(1)}, bf16[4,8,16,256]{3,2,1,0:T(8,128)(2,1)S(1)}, u32[]{:S(2)}, u32[]{:S(2)}) collective-permute-start(bf16[4,8,16,256]{3,2,1,0:T(8,128)(2,1)S(1)} %pad_maximum_fusion.6), channel_id=1, source_target_pairs={{0,1},{1,0},{2,3},{3,2},{4,5},{5,4},{6,7},{7,6},{8,9},{9,8},{10,11... | collective-permute-start | bytes 786440 | tf_op jit(solution)/shard_map/ppermute | solution.py:572
  67.5 0.2 collective-permute-done.10
  67.7 0.6 collective-permute-start.11
  68.4 2.1 %collective-permute-done.2 = bf16[4,8,16,256]{3,2,1,0:T(8,128)(2,1)S(1)} collective-permute-done((bf16[4,8,16,256]{3,2,1,0:T(8,128)(2,1)S(1)}, bf16[4,8,16,256]{3,2,1,0:T(8,128)(2,1)S(1)}, u32[]{:S(2)}, u32[]{:S(2)}) %collective-permute-start.2) | collective-permute-done | bytes 262176 | tf_op jit(solution)/shard_map/ppermute | solution.py:572
  70.6 1.8 %collective-permute-start.12 = (bf16[8,8,16,256]{3,2,1,0:T(8,128)(2,1)S(1)}, bf16[8,8,16,256]{3,2,1,0:T(8,128)(2,1)S(1)}, u32[]{:S(2)}, u32[]{:S(2)}) collective-permute-start(bf16[8,8,16,256]{3,2,1,0:T(8,128)(2,1)S(1)} %pad_maximum_fusion.refs_0_), channel_id=1, source_target_pairs={{0,12},{1,13},{2,14},{3,15},{4,8},{5,9},{6,10},{7,11},{8,4},{9,5},... | collective-permute-start | bytes 1572872 | tf_op jit(solution)/shard_map/ppermute | solution.py:572
  72.4 0.1 pad_maximum_fusion.1.refs_1_
  72.5 1.9 %collective-permute-start.13 = (bf16[8,8,16,256]{3,2,1,0:T(8,128)(2,1)S(1)}, bf16[8,8,16,256]{3,2,1,0:T(8,128)(2,1)S(1)}, u32[]{:S(2)}, u32[]{:S(2)}) collective-permute-start(bf16[8,8,16,256]{3,2,1,0:T(8,128)(2,1)S(1)} %pad_maximum_fusion.1.refs_1_), channel_id=1, source_target_pairs={{0,3},{1,2},{2,1},{3,0},{4,7},{5,6},{6,5},{7,4},{8,11},{9,10},{10,... | collective-permute-start | bytes 1572872 | tf_op jit(solution)/shard_map/ppermute | solution.py:572
  74.3 0.1 pad_maximum_fusion.2.refs_2_
  74.4 0.1 collective-permute-start.14
  74.5 0.2 collective-permute-done.11
  74.7 3.0 %collective-permute-start.15 = (bf16[8,8,16,256]{3,2,1,0:T(8,128)(2,1)S(1)}, bf16[8,8,16,256]{3,2,1,0:T(8,128)(2,1)S(1)}, u32[]{:S(2)}, u32[]{:S(2)}) collective-permute-start(bf16[8,8,16,256]{3,2,1,0:T(8,128)(2,1)S(1)} %pad_maximum_fusion.3.refs_3_), channel_id=1, source_target_pairs={{0,1},{1,0},{2,3},{3,2},{4,5},{5,4},{6,7},{7,6},{8,9},{9,8},{10,11... | collective-permute-start | bytes 1572872 | tf_op jit(solution)/shard_map/ppermute | solution.py:572
  77.7 3.7 %near_scores.1 = (f32[20,256,256]{2,1,0:T(8,128)S(1)}, f32[8,8,256]{2,1,0:T(8,128)S(1)}, s32[49]{0:T(128)S(1)}) custom-call(s32[9]{0:T(128)S(1)} %get-tuple-element.26.start_ref, bf16[8,384,1024]{2,1,0:T(8,128)(2,1)S(1)} %copy-done.1, bf16[8,8,16,256]{3,2,1,0:T(8,128)(2,1)S(1)} %pad_maximum_fusion.refs_0_, ...), custom_call_target="tpu_custom_call" | custom-call | flops 1342177280 | bytes 5242880 | tf_op jit(solution)/shard_map/near_scores/pallas_call | solution.py:456
  81.4 1.3 %collective-permute-done.12.refs_4_ = bf16[8,8,16,256]{3,2,1,0:T(8,128)(2,1)S(1)} collective-permute-done((bf16[8,8,16,256]{3,2,1,0:T(8,128)(2,1)S(1)}, bf16[8,8,16,256]{3,2,1,0:T(8,128)(2,1)S(1)}, u32[]{:S(2)}, u32[]{:S(2)}) %collective-permute-start.12) | collective-permute-done | bytes 524320 | tf_op jit(solution)/shard_map/ppermute | solution.py:572
  82.7 1.1 collective-permute-done.13.refs_5_
  83.8 1.6 %collective-permute-done.14.refs_6_ = bf16[8,8,16,256]{3,2,1,0:T(8,128)(2,1)S(1)} collective-permute-done((bf16[8,8,16,256]{3,2,1,0:T(8,128)(2,1)S(1)}, bf16[8,8,16,256]{3,2,1,0:T(8,128)(2,1)S(1)}, u32[]{:S(2)}, u32[]{:S(2)}) %collective-permute-start.14) | collective-permute-done | bytes 524320 | tf_op jit(solution)/shard_map/ppermute | solution.py:572
  85.4 12.1 %cross.1 = bf16[384,1024]{1,0:T(8,128)(2,1)} custom-call(s32[49]{0:T(128)S(1)} %get-tuple-element.29.work_hbm, bf16[8,384,1024]{2,1,0:T(8,128)(2,1)S(1)} %copy-done.1, f32[20,256,256]{2,1,0:T(8,128)S(1)} %get-tuple-element.30.score_ref, f32[8,8,256]{2,1,0:T(8,128)S(1)} %get-tuple-element.31.square_ref, f32[384,1]{1,0:T(8,128)S(1)} %copy-done.11, ...), custom_call_target="tpu_custom_call" | custom-call | flops 3221225472 | bytes 4194304 | tf_op jit(solution)/shard_map/cross/pallas_call | solution.py:549
  97.5 4.8 %all-to-all-start.2 = ((bf16[16,24,1024]{2,1,0:T(8,128)(2,1)}), bf16[16,24,1024]{2,1,0:T(8,128)(2,1)S(1)}, u32[]{:S(2)}, u32[]{:S(2)}) async-start(bf16[16,24,1024]{2,1,0:T(8,128)(2,1)} %bitcast.11), calls=%async_computation.2 | async-start | bytes 1572864 | tf_op jit(solution)/shard_map/all_to_all | solution.py:654
  102.3 0.8 dynamic-slice_convert_fusion
  103.1 10.8 %all-to-all-done.2 = bf16[16,24,1024]{2,1,0:T(8,128)(2,1)S(1)} async-done(((bf16[16,24,1024]{2,1,0:T(8,128)(2,1)}), bf16[16,24,1024]{2,1,0:T(8,128)(2,1)S(1)}, u32[]{:S(2)}, u32[]{:S(2)}) %all-to-all-start.2) | async-done | bytes 786464 | tf_op jit(solution)/shard_map/all_to_all | solution.py:654
  113.9 0.1 convert_reduce_fusion
  114.0 0.6 add_convert_fusion
  (52 shorter events, 0.4 us)
Async XLA Ops:
  10.2 7.4 %copy-start.19 = (s32[384]{0:T(512)S(1)}, s32[384]{0:T(512)}, u32[]{:S(2)}) copy-start(s32[384]{0:T(512)} %param.27) | copy-start | bytes 4612
  10.2 7.5 %copy-start.2 = (bf16[1024,1024]{1,0:T(8,128)(2,1)S(1)}, bf16[1024,1024]{1,0:T(8,128)(2,1)}, u32[]{:S(2)}) copy-start(bf16[1024,1024]{1,0:T(8,128)(2,1)} %wq_ref.1) | copy-start | bytes 6291460
  10.3 7.5 %copy-start.14 = (f32[1024]{0:T(1024)S(1)}, f32[1024]{0:T(1024)}, u32[]{:S(2)}) copy-start(f32[1024]{0:T(1024)} %param.28) | copy-start | bytes 12292
  10.3 7.5 %copy-start.15 = (f32[1024]{0:T(1024)S(1)}, f32[1024]{0:T(1024)}, u32[]{:S(2)}) copy-start(f32[1024]{0:T(1024)} %param.29) | copy-start | bytes 12292
  10.3 7.4 %copy-start.16 = (s32[4]{0:T(128)S(1)}, s32[4]{0:T(128)}, u32[]{:S(2)}) copy-start(s32[4]{0:T(128)} %protein_hbm.1) | copy-start | bytes 52
  10.3 7.4 %copy-start.17 = (s32[32]{0:T(128)S(1)}, s32[32]{0:T(128)}, u32[]{:S(2)}) copy-start(s32[32]{0:T(128)} %length_hbm.1) | copy-start | bytes 388
  10.3 7.4 %copy-start.18 = (s32[32]{0:T(128)S(1)}, s32[32]{0:T(128)}, u32[]{:S(2)}) copy-start(s32[32]{0:T(128)} %group_ref.1) | copy-start | bytes 388
  10.3 25.0 %all-to-all-start = ((bf16[16,64,512]{2,1,0:T(8,128)(2,1)}), bf16[16,64,512]{2,1,0:T(8,128)(2,1)S(1)}, u32[]{:S(2)}, u32[]{:S(2)}) async-start(bf16[16,64,512]{2,1,0:T(8,128)(2,1)} %bitcast.18), calls=%async_computation | async-start | bytes 2097152 | tf_op jit(solution)/shard_map/all_to_all | solution.py:625
  17.8 1.6 %copy-start.3 = (bf16[1024,1024]{1,0:T(8,128)(2,1)S(1)}, bf16[1024,1024]{1,0:T(8,128)(2,1)}, u32[]{:S(2)}) copy-start(bf16[1024,1024]{1,0:T(8,128)(2,1)} %wk_ref.1) | copy-start | bytes 6291460
  19.3 1.6 %copy-start.4 = (bf16[1024,1024]{1,0:T(8,128)(2,1)S(1)}, bf16[1024,1024]{1,0:T(8,128)(2,1)}, u32[]{:S(2)}) copy-start(bf16[1024,1024]{1,0:T(8,128)(2,1)} %wv_ref.1) | copy-start | bytes 6291460
  20.9 1.2 %copy-start.8 = (bf16[512,1024]{1,0:T(8,128)(2,1)S(1)}, bf16[512,1024]{1,0:T(8,128)(2,1)}, u32[]{:S(2)}) copy-start(bf16[512,1024]{1,0:T(8,128)(2,1)} %residue_hbm.3) | copy-start | bytes 3145732
  22.2 1.1 copy-start.9
  28.8 2.6 %copy-start = (bf16[8,384,1024]{2,1,0:T(8,128)(2,1)}, bf16[8,384,1024]{2,1,0:T(8,128)(2,1)S(1)}, u32[]{:S(2)}) copy-start(bf16[8,384,1024]{2,1,0:T(8,128)(2,1)S(1)} %get-tuple-element.27.query_ref) | copy-start | bytes 18874372
  31.5 1.4 %copy-start.6 = (bf16[1024,1024]{1,0:T(8,128)(2,1)}, bf16[1024,1024]{1,0:T(8,128)(2,1)S(1)}, u32[]{:S(2)}) copy-start(bf16[1024,1024]{1,0:T(8,128)(2,1)S(1)} %get-tuple-element.35.wv_ref) | copy-start | bytes 6291460
  32.9 0.7 copy-start.10
  33.6 0.7 copy-start.12
  35.3 0.9 copy-start.13
  50.2 6.5 %collective-permute-start = (bf16[1,8,16,256]{3,2,1,0:T(8,128)(2,1)S(1)}, bf16[1,8,16,256]{3,2,1,0:T(8,128)(2,1)S(1)}, u32[]{:S(2)}, u32[]{:S(2)}) collective-permute-start(bf16[1,8,16,256]{3,2,1,0:T(8,128)(2,1)S(1)} %get-tuple-element.41), channel_id=1, source_target_pairs={{0,1},{1,0},{2,3},{3,2},{4,5},{5,4},{6,7},{7,6},{8,9},{9,8},{10,11... | collective-permute-start | bytes 196616 | tf_op jit(solution)/shard_map/ppermute | solution.py:572
  51.1 6.5 %collective-permute-start.3 = (bf16[1,8,16,256]{3,2,1,0:T(8,128)(2,1)S(1)}, bf16[1,8,16,256]{3,2,1,0:T(8,128)(2,1)S(1)}, u32[]{:S(2)}, u32[]{:S(2)}) collective-permute-start(bf16[1,8,16,256]{3,2,1,0:T(8,128)(2,1)S(1)} %get-tuple-element.40), channel_id=1, source_target_pairs={{0,4},{1,5},{2,6},{3,7},{4,0},{5,1},{6,2},{7,3},{8,12},{9,13},{10,... | collective-permute-start | bytes 196616 | tf_op jit(solution)/shard_map/ppermute | solution.py:572
  52.5 5.7 %collective-permute-start.6 = (bf16[1,8,16,256]{3,2,1,0:T(8,128)(2,1)S(1)}, bf16[1,8,16,256]{3,2,1,0:T(8,128)(2,1)S(1)}, u32[]{:S(2)}, u32[]{:S(2)}) collective-permute-start(bf16[1,8,16,256]{3,2,1,0:T(8,128)(2,1)S(1)} %get-tuple-element.39), channel_id=1, source_target_pairs={{0,3},{1,2},{2,1},{3,0},{4,7},{5,6},{6,5},{7,4},{8,11},{9,10},{10,... | collective-permute-start | bytes 196616 | tf_op jit(solution)/shard_map/ppermute | solution.py:572
  54.6 5.7 %collective-permute-start.9 = (bf16[1,8,16,256]{3,2,1,0:T(8,128)(2,1)S(1)}, bf16[1,8,16,256]{3,2,1,0:T(8,128)(2,1)S(1)}, u32[]{:S(2)}, u32[]{:S(2)}) collective-permute-start(bf16[1,8,16,256]{3,2,1,0:T(8,128)(2,1)S(1)} %get-tuple-element.38), channel_id=1, source_target_pairs={{0,12},{1,13},{2,14},{3,15},{4,8},{5,9},{6,10},{7,11},{8,4},{9,5},... | collective-permute-start | bytes 196616 | tf_op jit(solution)/shard_map/ppermute | solution.py:572
  56.7 5.7 %collective-permute-start.1 = (bf16[2,8,16,256]{3,2,1,0:T(8,128)(2,1)S(1)}, bf16[2,8,16,256]{3,2,1,0:T(8,128)(2,1)S(1)}, u32[]{:S(2)}, u32[]{:S(2)}) collective-permute-start(bf16[2,8,16,256]{3,2,1,0:T(8,128)(2,1)S(1)} %pad_maximum_fusion.8), channel_id=1, source_target_pairs={{0,4},{1,5},{2,6},{3,7},{4,0},{5,1},{6,2},{7,3},{8,12},{9,13},{10,... | collective-permute-start | bytes 393224 | tf_op jit(solution)/shard_map/ppermute | solution.py:572
  57.6 6.2 %collective-permute-start.4 = (bf16[2,8,16,256]{3,2,1,0:T(8,128)(2,1)S(1)}, bf16[2,8,16,256]{3,2,1,0:T(8,128)(2,1)S(1)}, u32[]{:S(2)}, u32[]{:S(2)}) collective-permute-start(bf16[2,8,16,256]{3,2,1,0:T(8,128)(2,1)S(1)} %pad_maximum_fusion.9), channel_id=1, source_target_pairs={{0,1},{1,0},{2,3},{3,2},{4,5},{5,4},{6,7},{7,6},{8,9},{9,8},{10,11... | collective-permute-start | bytes 393224 | tf_op jit(solution)/shard_map/ppermute | solution.py:572
  58.2 7.9 %collective-permute-start.7 = (bf16[2,8,16,256]{3,2,1,0:T(8,128)(2,1)S(1)}, bf16[2,8,16,256]{3,2,1,0:T(8,128)(2,1)S(1)}, u32[]{:S(2)}, u32[]{:S(2)}) collective-permute-start(bf16[2,8,16,256]{3,2,1,0:T(8,128)(2,1)S(1)} %pad_maximum_fusion.10), channel_id=1, source_target_pairs={{0,12},{1,13},{2,14},{3,15},{4,8},{5,9},{6,10},{7,11},{8,4},{9,5},... | collective-permute-start | bytes 393224 | tf_op jit(solution)/shard_map/ppermute | solution.py:572
  60.3 7.4 %collective-permute-start.10 = (bf16[2,8,16,256]{3,2,1,0:T(8,128)(2,1)S(1)}, bf16[2,8,16,256]{3,2,1,0:T(8,128)(2,1)S(1)}, u32[]{:S(2)}, u32[]{:S(2)}) collective-permute-start(bf16[2,8,16,256]{3,2,1,0:T(8,128)(2,1)S(1)} %pad_maximum_fusion.11), channel_id=1, source_target_pairs={{0,3},{1,2},{2,1},{3,0},{4,7},{5,6},{6,5},{7,4},{8,11},{9,10},{10,... | collective-permute-start | bytes 393224 | tf_op jit(solution)/shard_map/ppermute | solution.py:572
  62.4 15.3 %copy-start.1 = (bf16[8,384,1024]{2,1,0:T(8,128)(2,1)S(1)}, bf16[8,384,1024]{2,1,0:T(8,128)(2,1)}, u32[]{:S(2)}) copy-start(bf16[8,384,1024]{2,1,0:T(8,128)(2,1)} %copy-done) | copy-start | bytes 18874372
  62.4 8.1 %collective-permute-start.2 = (bf16[4,8,16,256]{3,2,1,0:T(8,128)(2,1)S(1)}, bf16[4,8,16,256]{3,2,1,0:T(8,128)(2,1)S(1)}, u32[]{:S(2)}, u32[]{:S(2)}) collective-permute-start(bf16[4,8,16,256]{3,2,1,0:T(8,128)(2,1)S(1)} %pad_maximum_fusion.4), channel_id=1, source_target_pairs={{0,3},{1,2},{2,1},{3,0},{4,7},{5,6},{6,5},{7,4},{8,11},{9,10},{10,... | collective-permute-start | bytes 786440 | tf_op jit(solution)/shard_map/ppermute | solution.py:572
  63.8 8.6 %collective-permute-start.5 = (bf16[4,8,16,256]{3,2,1,0:T(8,128)(2,1)S(1)}, bf16[4,8,16,256]{3,2,1,0:T(8,128)(2,1)S(1)}, u32[]{:S(2)}, u32[]{:S(2)}) collective-permute-start(bf16[4,8,16,256]{3,2,1,0:T(8,128)(2,1)S(1)} %pad_maximum_fusion.5), channel_id=1, source_target_pairs={{0,12},{1,13},{2,14},{3,15},{4,8},{5,9},{6,10},{7,11},{8,4},{9,5},... | collective-permute-start | bytes 786440 | tf_op jit(solution)/shard_map/ppermute | solution.py:572
  66.2 8.2 %collective-permute-start.8 = (bf16[4,8,16,256]{3,2,1,0:T(8,128)(2,1)S(1)}, bf16[4,8,16,256]{3,2,1,0:T(8,128)(2,1)S(1)}, u32[]{:S(2)}, u32[]{:S(2)}) collective-permute-start(bf16[4,8,16,256]{3,2,1,0:T(8,128)(2,1)S(1)} %pad_maximum_fusion.6), channel_id=1, source_target_pairs={{0,1},{1,0},{2,3},{3,2},{4,5},{5,4},{6,7},{7,6},{8,9},{9,8},{10,11... | collective-permute-start | bytes 786440 | tf_op jit(solution)/shard_map/ppermute | solution.py:572
  67.7 6.9 %collective-permute-start.11 = (bf16[4,8,16,256]{3,2,1,0:T(8,128)(2,1)S(1)}, bf16[4,8,16,256]{3,2,1,0:T(8,128)(2,1)S(1)}, u32[]{:S(2)}, u32[]{:S(2)}) collective-permute-start(bf16[4,8,16,256]{3,2,1,0:T(8,128)(2,1)S(1)} %pad_maximum_fusion.7), channel_id=1, source_target_pairs={{0,4},{1,5},{2,6},{3,7},{4,0},{5,1},{6,2},{7,3},{8,12},{9,13},{10,... | collective-permute-start | bytes 786440 | tf_op jit(solution)/shard_map/ppermute | solution.py:572
  70.6 12.2 %collective-permute-start.12 = (bf16[8,8,16,256]{3,2,1,0:T(8,128)(2,1)S(1)}, bf16[8,8,16,256]{3,2,1,0:T(8,128)(2,1)S(1)}, u32[]{:S(2)}, u32[]{:S(2)}) collective-permute-start(bf16[8,8,16,256]{3,2,1,0:T(8,128)(2,1)S(1)} %pad_maximum_fusion.refs_0_), channel_id=1, source_target_pairs={{0,12},{1,13},{2,14},{3,15},{4,8},{5,9},{6,10},{7,11},{8,4},{9,5},... | collective-permute-start | bytes 1572872 | tf_op jit(solution)/shard_map/ppermute | solution.py:572
  72.5 11.3 %collective-permute-start.13 = (bf16[8,8,16,256]{3,2,1,0:T(8,128)(2,1)S(1)}, bf16[8,8,16,256]{3,2,1,0:T(8,128)(2,1)S(1)}, u32[]{:S(2)}, u32[]{:S(2)}) collective-permute-start(bf16[8,8,16,256]{3,2,1,0:T(8,128)(2,1)S(1)} %pad_maximum_fusion.1.refs_1_), channel_id=1, source_target_pairs={{0,3},{1,2},{2,1},{3,0},{4,7},{5,6},{6,5},{7,4},{8,11},{9,10},{10,... | collective-permute-start | bytes 1572872 | tf_op jit(solution)/shard_map/ppermute | solution.py:572
  74.4 11.0 %collective-permute-start.14 = (bf16[8,8,16,256]{3,2,1,0:T(8,128)(2,1)S(1)}, bf16[8,8,16,256]{3,2,1,0:T(8,128)(2,1)S(1)}, u32[]{:S(2)}, u32[]{:S(2)}) collective-permute-start(bf16[8,8,16,256]{3,2,1,0:T(8,128)(2,1)S(1)} %pad_maximum_fusion.2.refs_2_), channel_id=1, source_target_pairs={{0,4},{1,5},{2,6},{3,7},{4,0},{5,1},{6,2},{7,3},{8,12},{9,13},{10,... | collective-permute-start | bytes 1572872 | tf_op jit(solution)/shard_map/ppermute | solution.py:572
  74.7 10.7 %collective-permute-start.15 = (bf16[8,8,16,256]{3,2,1,0:T(8,128)(2,1)S(1)}, bf16[8,8,16,256]{3,2,1,0:T(8,128)(2,1)S(1)}, u32[]{:S(2)}, u32[]{:S(2)}) collective-permute-start(bf16[8,8,16,256]{3,2,1,0:T(8,128)(2,1)S(1)} %pad_maximum_fusion.3.refs_3_), channel_id=1, source_target_pairs={{0,1},{1,0},{2,3},{3,2},{4,5},{5,4},{6,7},{7,6},{8,9},{9,8},{10,11... | collective-permute-start | bytes 1572872 | tf_op jit(solution)/shard_map/ppermute | solution.py:572
  77.7 7.7 %copy-start.5 = (bf16[1024,1024]{1,0:T(8,128)(2,1)S(1)}, bf16[1024,1024]{1,0:T(8,128)(2,1)}, u32[]{:S(2)}) copy-start(bf16[1024,1024]{1,0:T(8,128)(2,1)} %wo_ref.1) | copy-start | bytes 6291460
  77.7 7.7 %copy-start.7 = (bf16[1024,1024]{1,0:T(8,128)(2,1)S(1)}, bf16[1024,1024]{1,0:T(8,128)(2,1)}, u32[]{:S(2)}) copy-start(bf16[1024,1024]{1,0:T(8,128)(2,1)} %copy-done.6) | copy-start | bytes 6291460
  77.7 7.7 %copy-start.11 = (f32[384,1]{1,0:T(8,128)S(1)}, f32[384,1]{1,0:T(8,128)}, u32[]{:S(2)}) copy-start(f32[384,1]{1,0:T(8,128)} %copy-done.10) | copy-start | bytes 4612
  97.5 16.4 %all-to-all-start.2 = ((bf16[16,24,1024]{2,1,0:T(8,128)(2,1)}), bf16[16,24,1024]{2,1,0:T(8,128)(2,1)S(1)}, u32[]{:S(2)}, u32[]{:S(2)}) async-start(bf16[16,24,1024]{2,1,0:T(8,128)(2,1)} %bitcast.11), calls=%async_computation.2 | async-start | bytes 1572864 | tf_op jit(solution)/shard_map/all_to_all | solution.py:654
